TPU v7x, 32 devices: a whole 2x2x4 slice. The times are simulated.
32 devices in a mesh: ctx: 8 (over z, y), head: 4 (over x, core).
Axes of the slice: x: 2, y: 2, z: 4, core: 2. Of those that a mesh axis runs over, the one named last changes fastest.
Arguments:
- x_in: bfloat16 [1024, 8192], P(('ctx', 'head')), may hold values from -6 to 6
- b_in: bfloat16 [1024, 1024], P(('ctx', 'head')), may hold values from -6 to 6
- c_in: bfloat16 [1024, 1024], P(('ctx', 'head')), may hold values from -6 to 6
- dt_in: bfloat16 [1024, 128], P(('ctx', 'head')), may hold values from -5 to 8
- z_in: bfloat16 [1024, 8192], P(('ctx', 'head')), may hold values from -6 to 6
- conv_x: float32 [4, 8192], replicated, may hold values from -3 to 3
- input_state_taps: float32 [4, 1024], replicated, may hold values from -3 to 3
- conv_c: float32 [4, 1024], replicated, may hold values from -3 to 3
- dt_bias: float32 [128], replicated, may hold values from -0.5 to 0.5
- a_log: float32 [128], replicated, may hold values from -20 to -2
- norm_gain: float32 [8192], replicated, may hold values from 0.1 to 1.9
Outputs:
- y_out: bfloat16 [1024, 8192], P(('ctx', 'head'))
All inputs are finite; a program needn't handle non-finite values.
Results may differ from a plain program's by a relative error of at most 0.0052.
Values may be sent and summed in bfloat16 or wider, within the bound.
No kernel may reach another device: no remote copies, remote signals or barrier semaphores. Data moves between devices by JAX's collectives and lax.ppermute only.
A program may use at most 192 MiB of HBM per device.

v0:
```python
import jax
import jax.numpy as jnp
from jax import lax
from jax.sharding import PartitionSpec as P

HEAD_DIM = 64
STATE = 128
GROUPS = 8
BLOCK = 128


eps_norm = 1e-05


def passed_along(block, axis, distance):
    devices = range(lax.axis_size(axis))
    route = [(i - distance, i) for i in devices if i - distance in devices]
    return lax.ppermute(block, axis, route)


def prefix(shard, axis, combine, identity):
    size, here = (lax.axis_size(axis), lax.axis_index(axis))
    everything = jax.tree.map(lambda part: lax.all_gather(part, axis), shard)
    start = jax.tree.map(
        lambda part, zero: jnp.broadcast_to(jnp.asarray(zero, part.dtype), part.shape),
        shard,
        identity,
    )

    def lap(k, before):
        reached = k < here
        new = combine(before, jax.tree.map(lambda part: part[k], everything))
        return jax.tree.map(lambda a, b: jnp.where(reached, a, b), new, before)

    return lax.fori_loop(0, size, lap, start)


def conv_rows(window, weights):
    count = window.shape[0] - weights.shape[0] + 1
    total = jnp.zeros((count, window.shape[1]), jnp.float32)
    for position_shift in range(weights.shape[0]):
        total = total + weights[position_shift] * window[
            position_shift : position_shift + count
        ].astype(jnp.float32)
    return jax.nn.silu(total).astype(jnp.bfloat16)


def gate_norm(values, gate, gain, groups):
    gated = values.astype(jnp.float32) * jax.nn.silu(gate.astype(jnp.float32))
    shaped = gated.reshape(gated.shape[0], groups, -1)
    scale = lax.rsqrt(jnp.mean(shaped * shaped, axis=-1, keepdims=True) + eps_norm)
    return ((shaped * scale).reshape(gated.shape) * gain).astype(jnp.bfloat16)


def chain_step(earlier, later):
    return (earlier[0] * later[0], later[0][:, None, None] * earlier[1] + later[1])


def shards(
    x_in, b_in, c_in, dt_in, z_in, conv_x, input_state_taps, conv_c, dt_bias, a_log, norm_gain
):
    high = lax.Precision.HIGHEST
    parts = lax.axis_size("head")
    which = lax.axis_index("head")
    lead = conv_x.shape[0] - 1
    width_x = x_in.shape[1] // parts
    width_s = b_in.shape[1] // parts
    heads_here = dt_in.shape[1] // parts
    groups_here = GROUPS // parts
    per = heads_here // groups_here
    x_src, b_src, c_src = (x_in, b_in, c_in)
    x_loc, b_loc, c_loc, dt_loc = (
        lax.all_to_all(x_src, "head", split_axis=1, concat_axis=0, tiled=True),
        lax.all_to_all(b_src, "head", split_axis=1, concat_axis=0, tiled=True),
        lax.all_to_all(c_src, "head", split_axis=1, concat_axis=0, tiled=True),
        lax.all_to_all(dt_in, "head", split_axis=1, concat_axis=0, tiled=True),
    )
    prior = passed_along((x_loc[-lead:], b_loc[-lead:], c_loc[-lead:]), "ctx", 1)
    x_loc = conv_rows(
        jnp.concatenate([prior[0], x_loc], 0),
        lax.dynamic_slice_in_dim(conv_x, which * width_x, width_x, 1),
    )
    b_loc = conv_rows(
        jnp.concatenate([prior[1], b_loc], 0),
        lax.dynamic_slice_in_dim(input_state_taps, which * width_s, width_s, 1),
    )
    c_loc = conv_rows(
        jnp.concatenate([prior[2], c_loc], 0),
        lax.dynamic_slice_in_dim(conv_c, which * width_s, width_s, 1),
    )
    rows = x_loc.shape[0]
    block_list = rows // BLOCK
    local_bias_slice = lax.dynamic_slice_in_dim(dt_bias, which * heads_here, heads_here, 0)
    alog_here = lax.dynamic_slice_in_dim(a_log, which * heads_here, heads_here, 0)
    steps_dt = jax.nn.softplus(dt_loc.astype(jnp.float32) + local_bias_slice)
    cum = jnp.cumsum(
        (steps_dt * -jnp.exp(alog_here)).reshape(block_list, BLOCK, heads_here), axis=1
    )
    dt_blocks = steps_dt.reshape(block_list, BLOCK, heads_here)
    x_blocks = x_loc.reshape(block_list, BLOCK, heads_here, HEAD_DIM)
    b_blocks = b_loc.reshape(block_list, BLOCK, groups_here, STATE)
    c_blocks = c_loc.reshape(block_list, BLOCK, groups_here, STATE)
    scores = jnp.einsum("ktgn,ksgn->kgts", c_blocks, b_blocks, preferred_element_type=jnp.float32)
    causal = lax.broadcasted_iota(jnp.int32, (BLOCK, BLOCK), 0) >= lax.broadcasted_iota(
        jnp.int32, (BLOCK, BLOCK), 1
    )
    cum_heads = jnp.swapaxes(cum, 1, 2).reshape(block_list, groups_here, per, BLOCK)
    dt_heads = jnp.swapaxes(dt_blocks, 1, 2).reshape(block_list, groups_here, per, BLOCK)
    gap = jnp.where(causal, cum_heads[..., :, None] - cum_heads[..., None, :], 0.0)
    mix = jnp.where(causal, scores[:, :, None] * jnp.exp(gap) * dt_heads[..., None, :], 0.0).astype(
        jnp.bfloat16
    )
    mix = mix.reshape(block_list, heads_here, BLOCK, BLOCK)
    intra = jnp.einsum("khts,kshp->kthp", mix, x_blocks, preferred_element_type=jnp.float32)
    tail = jnp.exp(cum[:, -1:, :] - cum) * dt_blocks
    weighted = (x_blocks.astype(jnp.float32) * tail[..., None]).reshape(
        block_list, BLOCK, groups_here, per, HEAD_DIM
    )
    fresh = jnp.einsum("ktgqp,ktgn->kgqpn", weighted, b_blocks.astype(jnp.float32), precision=high)
    fresh = fresh.reshape(block_list, heads_here, HEAD_DIM, STATE)
    fade = jnp.exp(cum[:, -1, :])
    total = (fade[0], fresh[0])
    identity = (
        jnp.ones((heads_here,), jnp.float32),
        jnp.zeros((heads_here, HEAD_DIM, STATE), jnp.float32),
    )
    entering = prefix(total, "ctx", chain_step, identity)[1]
    starts = [entering]
    start_states = jnp.stack(starts).reshape(block_list, groups_here, per, HEAD_DIM, STATE)
    carried = jnp.einsum(
        "ktgn,kgqpn->ktgqp", c_blocks.astype(jnp.float32), start_states, precision=high
    )
    carried = carried.reshape(block_list, BLOCK, heads_here, HEAD_DIM) * jnp.exp(cum)[..., None]
    y_loc = (intra + carried).reshape(rows, width_x).astype(jnp.bfloat16)
    z_loc = lax.all_to_all(z_in, "head", split_axis=1, concat_axis=0, tiled=True)
    local_gain_slice = lax.dynamic_slice_in_dim(norm_gain, which * width_x, width_x, 0)
    leaving = gate_norm(lax.optimization_barrier(y_loc), z_loc, local_gain_slice, groups_here)
    returned = lax.all_to_all(leaving, "head", split_axis=0, concat_axis=1, tiled=True)
    return returned


def solution(mesh):
    placed = (
        P(("ctx", "head"), None),
        P(("ctx", "head"), None),
        P(("ctx", "head"), None),
        P(("ctx", "head"), None),
        P(("ctx", "head"), None),
        P(),
        P(),
        P(),
        P(),
        P(),
        P(),
    )
    return jax.shard_map(
        shards, mesh=mesh, in_specs=placed, out_specs=P(("ctx", "head"), None), check_vma=False
    )
```

profile of v0, /device:TPU:0, one launch (start us, length us, event | category | flops | bytes accessed | tf_op | source)
XLA Modules:
  0.0 210.7 jit_solution(3405749517287534782)
XLA Ops:
  6.5 0.8 copy.133
  7.3 0.7 reshape.343
  8.0 4.2 %all-to-all-start.3 = ((bf16[4,2,512]{2,1,0:T(2,128)(2,1)}), bf16[4,2,512]{2,1,0:T(2,128)(2,1)S(1)}, u32[]{:S(2)}, u32[]{:S(2)}) async-start(bf16[4,2,512]{2,1,0:T(2,128)(2,1)} %reshape.343), calls=%async_computation.3 | async-start | bytes 16384 | tf_op jit(solution)/shard_map/all_to_all | solution.py:76
  12.3 1.0 constant_dynamic-slice_fusion
  13.3 0.9 constant_dynamic-slice_fusion.1
  14.2 0.7 exponential_negate_fusion
  14.9 1.5 copy.170
  16.4 0.7 dynamic_slice.35
  17.2 1.9 copy.169
  19.1 3.3 %all-to-all-start.2 = ((bf16[32,4,256]{2,0,1:T(8,128)(2,1)}), bf16[32,4,256]{2,0,1:T(8,128)(2,1)S(1)}, u32[]{:S(2)}, u32[]{:S(2)}) async-start(bf16[32,4,256]{2,0,1:T(8,128)(2,1)} %bitcast.131), calls=%async_computation.2 | async-start | bytes 131072 | tf_op jit(solution)/shard_map/all_to_all | solution.py:74
  22.4 0.1 reshape.344
  22.6 0.1 reshape.329
  22.7 0.1 fusion.21
  22.8 0.1 reshape.331
  22.9 0.1 copy.135
  23.0 0.2 reduce_window_sum.13
  23.2 3.3 %all-to-all-done.2 = bf16[32,4,256]{2,0,1:T(8,128)(2,1)S(1)} async-done(((bf16[32,4,256]{2,0,1:T(8,128)(2,1)}), bf16[32,4,256]{2,0,1:T(8,128)(2,1)S(1)}, u32[]{:S(2)}, u32[]{:S(2)}) %all-to-all-start.2) | async-done | bytes 65568 | tf_op jit(solution)/shard_map/all_to_all | solution.py:74
  26.5 3.5 %all-to-all-start = ((bf16[32,4,2048]{2,0,1:T(8,128)(2,1)}), bf16[32,4,2048]{2,0,1:T(8,128)(2,1)S(1)}, u32[]{:S(2)}, u32[]{:S(2)}) async-start(bf16[32,4,2048]{2,0,1:T(8,128)(2,1)} %bitcast.130), calls=%async_computation | async-start | bytes 1048576 | tf_op jit(solution)/shard_map/all_to_all | solution.py:73
  30.1 0.1 sub.39
  30.2 3.9 %collective-permute-start.2 = (bf16[3,256]{1,0:T(4,128)(2,1)S(1)}, bf16[3,256]{1,0:T(4,128)(2,1)S(1)}, u32[]{:S(2)}, u32[]{:S(2)}) collective-permute-start(bf16[3,256]{1,0:T(4,128)(2,1)S(1)} %slice.111), channel_id=1, source_target_pairs={{0,4},{4,8},{8,12},{12,16},{16,20},{20,24},{24,28},{1,5},{5,9},{9,... | collective-permute-start | bytes 4616 | tf_op jit(solution)/shard_map/ppermute | solution.py:18
  34.0 0.1 fusion.20
  34.1 4.7 %all-to-all-done = bf16[32,4,2048]{2,0,1:T(8,128)(2,1)S(1)} async-done(((bf16[32,4,2048]{2,0,1:T(8,128)(2,1)}), bf16[32,4,2048]{2,0,1:T(8,128)(2,1)S(1)}, u32[]{:S(2)}, u32[]{:S(2)}) %all-to-all-start) | async-done | bytes 524320 | tf_op jit(solution)/shard_map/all_to_all | solution.py:73
  38.8 3.9 %collective-permute-start = (bf16[3,2048]{1,0:T(4,128)(2,1)S(1)}, bf16[3,2048]{1,0:T(4,128)(2,1)S(1)}, u32[]{:S(2)}, u32[]{:S(2)}) collective-permute-start(bf16[3,2048]{1,0:T(4,128)(2,1)S(1)} %slice.101), channel_id=1, source_target_pairs={{0,4},{4,8},{8,12},{12,16},{16,20},{20,24},{24,28},{1,5},{5,9},{9,... | collective-permute-start | bytes 36872 | tf_op jit(solution)/shard_map/ppermute | solution.py:18
  42.7 0.1 multiply_convert_fusion.2
  42.8 0.1 copy.130
  43.0 1.2 collective-permute-done
  44.1 0.7 multiply_convert_fusion.1
  44.9 0.2 copy.138
  45.1 1.7 fusion.10
  46.8 0.6 copy.171
  47.4 3.3 %all-to-all-start.1 = ((bf16[32,4,256]{2,0,1:T(8,128)(2,1)}), bf16[32,4,256]{2,0,1:T(8,128)(2,1)S(1)}, u32[]{:S(2)}, u32[]{:S(2)}) async-start(bf16[32,4,256]{2,0,1:T(8,128)(2,1)} %bitcast.132), calls=%async_computation.1 | async-start | bytes 131072 | tf_op jit(solution)/shard_map/all_to_all | solution.py:75
  50.8 0.8 copy.168
  51.6 3.2 %all-to-all-done.1 = bf16[32,4,256]{2,0,1:T(8,128)(2,1)S(1)} async-done(((bf16[32,4,256]{2,0,1:T(8,128)(2,1)}), bf16[32,4,256]{2,0,1:T(8,128)(2,1)S(1)}, u32[]{:S(2)}, u32[]{:S(2)}) %all-to-all-start.1) | async-done | bytes 65568 | tf_op jit(solution)/shard_map/all_to_all | solution.py:75
  54.8 3.5 %all-to-all-start.4 = ((bf16[32,4,2048]{2,0,1:T(8,128)(2,1)}), bf16[32,4,2048]{2,0,1:T(8,128)(2,1)S(1)}, u32[]{:S(2)}, u32[]{:S(2)}) async-start(bf16[32,4,2048]{2,0,1:T(8,128)(2,1)} %bitcast.129), calls=%async_computation.4 | async-start | bytes 1048576 | tf_op jit(solution)/shard_map/all_to_all | solution.py:135
  58.3 4.2 %collective-permute-start.1 = (bf16[3,256]{1,0:T(4,128)(2,1)S(1)}, bf16[3,256]{1,0:T(4,128)(2,1)S(1)}, u32[]{:S(2)}, u32[]{:S(2)}) collective-permute-start(bf16[3,256]{1,0:T(4,128)(2,1)S(1)} %slice.106), channel_id=1, source_target_pairs={{0,4},{4,8},{8,12},{12,16},{16,20},{20,24},{24,28},{1,5},{5,9},{9,... | collective-permute-start | bytes 4616 | tf_op jit(solution)/shard_map/ppermute | solution.py:18
  62.7 19.0 %all-gather = f32[8,1,32]{2,1,0:T(1,128)S(1)} all-gather(f32[1,1,32]{2,1,0:T(1,128)S(1)} %get-tuple-element.133), channel_id=2, replica_groups=mesh['ctx'=8,'head'=4] {'ctx'}, dimensions={0}, use_global_device_ids=true | all-gather | bytes 1152 | tf_op jit(solution)/shard_map/all_gather | solution.py:23
  81.7 0.1 multiply_convert_fusion.3
  81.8 0.1 copy.128
  81.9 0.2 fusion.22
  82.1 0.7 fusion.3
  82.9 1.0 copy.126
  83.9 89.1 %all-gather.3.cloned.1.call-done = f32[8,32,64,128]{3,2,1,0:T(8,128)} async-done(((f32[1,32,64,128]{3,2,1,0:T(8,128)}), f32[8,32,64,128]{3,2,1,0:T(8,128)}) %all-gather.3.cloned.1.call-update) | async-done | bytes 8388624 | tf_op jit(solution)/shard_map/all_gather | solution.py:23
  173.0 12.0 %while.14 = (s32[]{:T(128)}, f32[32,64,128]{2,1,0:T(8,128)S(1)}, s32[]{:T(128)}, f32[8,32]{1,0:T(8,128)S(1)}, f32[8,32,64,128]{3,2,1,0:T(8,128)}, /*index=5*/s32[]{:T(128)}, s32[]{:T(128)}) while((s32[]{:T(128)}, f32[32,64,128]{2,1,0:T(8,128)S(1)}, s32[]{:T(128)}, f32[8,32]{1,0:T(8,128)S(1)}, f32[8,32,64,128]{3,2,1,0:T(8,128)}, ...), condition=%wide.region_2.3_spmd.clone, body=%wide.region_1.2_spmd.clone.sunk | while | flops 1048580 | bytes 3146217 | solution.py:35
  173.0 1.5 fusion.32
  174.5 1.5 fusion.32
  176.0 1.5 fusion.32
  177.5 1.5 fusion.32
  179.0 1.5 fusion.32
  180.5 1.5 fusion.32
  182.0 1.5 fusion.32
  183.5 1.5 fusion.32
  185.0 0.6 fusion.23
  185.6 0.1 bitcast_multiply_fusion.1
  185.7 0.3 copy-done
  186.0 1.6 fusion.5
  187.6 1.2 copy.144
  188.9 0.3 fusion.15
  189.2 0.9 mul.336
  190.1 0.3 reduce_sum.9
  190.5 0.3 mul.337
  190.9 0.3 copy.162
  191.2 0.4 multiply_convert_fusion
  191.6 11.4 %all_to_all.102 = bf16[4,32,2048]{2,1,0:T(8,128)(2,1)S(1)} all-to-all(bf16[4,32,2048]{2,1,0:T(8,128)(2,1)S(1)} %bitcast.144), channel_id=1, replica_groups=mesh['ctx'=8,'head'=4] {'head'}, dimensions={0} | all-to-all | bytes 1048576 | tf_op jit(solution)/shard_map/all_to_all | solution.py:138
  203.0 0.8 copy.161
  (35 shorter events, 0.6 us)
Async XLA Ops:
  8.0 11.1 %all-to-all-start.3 = ((bf16[4,2,512]{2,1,0:T(2,128)(2,1)}), bf16[4,2,512]{2,1,0:T(2,128)(2,1)S(1)}, u32[]{:S(2)}, u32[]{:S(2)}) async-start(bf16[4,2,512]{2,1,0:T(2,128)(2,1)} %reshape.343), calls=%async_computation.3 | async-start | bytes 16384 | tf_op jit(solution)/shard_map/all_to_all | solution.py:76
  19.1 7.4 %all-to-all-start.2 = ((bf16[32,4,256]{2,0,1:T(8,128)(2,1)}), bf16[32,4,256]{2,0,1:T(8,128)(2,1)S(1)}, u32[]{:S(2)}, u32[]{:S(2)}) async-start(bf16[32,4,256]{2,0,1:T(8,128)(2,1)} %bitcast.131), calls=%async_computation.2 | async-start | bytes 131072 | tf_op jit(solution)/shard_map/all_to_all | solution.py:74
  26.5 12.3 %all-to-all-start = ((bf16[32,4,2048]{2,0,1:T(8,128)(2,1)}), bf16[32,4,2048]{2,0,1:T(8,128)(2,1)S(1)}, u32[]{:S(2)}, u32[]{:S(2)}) async-start(bf16[32,4,2048]{2,0,1:T(8,128)(2,1)} %bitcast.130), calls=%async_computation | async-start | bytes 1048576 | tf_op jit(solution)/shard_map/all_to_all | solution.py:73
  30.0 143.0 %all-gather.3.cloned.1.call-start = ((), (), s32[]{:S(2)}) async-start(), calls=%async_computation.6 | async-start | bytes 9437184 | tf_op jit(solution)/shard_map/all_gather | solution.py:23
  30.2 12.5 %collective-permute-start.2 = (bf16[3,256]{1,0:T(4,128)(2,1)S(1)}, bf16[3,256]{1,0:T(4,128)(2,1)S(1)}, u32[]{:S(2)}, u32[]{:S(2)}) collective-permute-start(bf16[3,256]{1,0:T(4,128)(2,1)S(1)} %slice.111), channel_id=1, source_target_pairs={{0,4},{4,8},{8,12},{12,16},{16,20},{20,24},{24,28},{1,5},{5,9},{9,... | collective-permute-start | bytes 4616 | tf_op jit(solution)/shard_map/ppermute | solution.py:18
  38.8 5.3 %collective-permute-start = (bf16[3,2048]{1,0:T(4,128)(2,1)S(1)}, bf16[3,2048]{1,0:T(4,128)(2,1)S(1)}, u32[]{:S(2)}, u32[]{:S(2)}) collective-permute-start(bf16[3,2048]{1,0:T(4,128)(2,1)S(1)} %slice.101), channel_id=1, source_target_pairs={{0,4},{4,8},{8,12},{12,16},{16,20},{20,24},{24,28},{1,5},{5,9},{9,... | collective-permute-start | bytes 36872 | tf_op jit(solution)/shard_map/ppermute | solution.py:18
  44.8 1.9 copy-start.2
  45.1 5.7 %copy-start.1 = (bf16[32,8192]{1,0:T(8,128)(2,1)S(1)}, bf16[32,8192]{1,0:T(8,128)(2,1)}, u32[]{:S(2)}) copy-start(bf16[32,8192]{1,0:T(8,128)(2,1)} %param.17) | copy-start | bytes 1572868
  47.4 7.4 %all-to-all-start.1 = ((bf16[32,4,256]{2,0,1:T(8,128)(2,1)}), bf16[32,4,256]{2,0,1:T(8,128)(2,1)S(1)}, u32[]{:S(2)}, u32[]{:S(2)}) async-start(bf16[32,4,256]{2,0,1:T(8,128)(2,1)} %bitcast.132), calls=%async_computation.1 | async-start | bytes 131072 | tf_op jit(solution)/shard_map/all_to_all | solution.py:75
  54.8 134.1 %all-to-all-start.4 = ((bf16[32,4,2048]{2,0,1:T(8,128)(2,1)}), bf16[32,4,2048]{2,0,1:T(8,128)(2,1)S(1)}, u32[]{:S(2)}, u32[]{:S(2)}) async-start(bf16[32,4,2048]{2,0,1:T(8,128)(2,1)} %bitcast.129), calls=%async_computation.4 | async-start | bytes 1048576 | tf_op jit(solution)/shard_map/all_to_all | solution.py:135
  58.3 23.4 %collective-permute-start.1 = (bf16[3,256]{1,0:T(4,128)(2,1)S(1)}, bf16[3,256]{1,0:T(4,128)(2,1)S(1)}, u32[]{:S(2)}, u32[]{:S(2)}) collective-permute-start(bf16[3,256]{1,0:T(4,128)(2,1)S(1)} %slice.106), channel_id=1, source_target_pairs={{0,4},{4,8},{8,12},{12,16},{16,20},{20,24},{24,28},{1,5},{5,9},{9,... | collective-permute-start | bytes 4616 | tf_op jit(solution)/shard_map/ppermute | solution.py:18
  185.0 1.0 copy-start
  190.1 1.1 dynamic-slice-start
Sparse Core Ops, SparseCore 0:
  46.9 126.0 all-gather.2
where the time goes:
time: 212 us; the launch traced here: 211 us
  waiting for transfers between devices  102 us (48%)
  blocking collectives  30.4 us (14%)
  starting transfers between devices  29.7 us (14%)
  other arithmetic  15.7 us (7%)
  local copies, waits for them, and re-layouts  15.3 us (7%)
  between operations  13.7 us (6%)
  matrix products  4.09 us (2%)
    all_gather x1, waiting for transfers between devices, prefix(): everything = jax.tree.map(lambda part: lax.all_gather(part, axis), shard)  89.1 us
    all_gather x1, blocking collectives, prefix(): everything = jax.tree.map(lambda part: lax.all_gather(part, axis), shard)  19 us
    ppermute x3, starting transfers between devices, passed_along(): return lax.ppermute(block, axis, route)  11.9 us
    select_n x8, other arithmetic, lap(): return jax.tree.map(lambda a, b: jnp.where(reached, a, b), new, before)  11.7 us
    all_to_all x1, blocking collectives, shards(): lax.all_to_all(leaving, 'head', split_axis=0, concat_axis=1, tiled=True)  11.4 us
    all_to_all x1, waiting for transfers between devices, shards(): lax.all_to_all(x_src, 'head', split_axis=1, concat_axis=0, tiled=True)  4.69 us
  transfers between devices with their start and end apart: 9, of which 5 were waited for; matrix products, arithmetic and copies ran while one was open for 13% of the time, Pallas kernels for 0%

commit v1 on v0

v1 whole, which is shorter than its diff:
```python
import functools
import jax
import jax.numpy as jnp
from jax import lax
from jax.experimental import pallas as pl
from jax.experimental.pallas import tpu as pltpu
from jax.sharding import Mesh
from jax.sharding import PartitionSpec as P

HEAD_DIM = 64
STATE = 128
GROUPS = 8
BLOCK = 128
OWN = 8
WIDE = OWN * HEAD_DIM
CONV = WIDE + 2 * STATE
LANES = 128

eps_norm = 1e-05
F32 = jnp.float32
BF16 = jnp.bfloat16


def dot(a, b):
    return jnp.dot(a, b, preferred_element_type=F32)


def parts_of(values, count):
    out = []
    for k in range(count):
        piece = values.astype(BF16)
        out.append(piece)
        if k + 1 < count:
            values = values - piece.astype(F32)
    return out


def silu(v):
    return v * jax.nn.sigmoid(v)


def expander(mine):
    row = lax.broadcasted_iota(jnp.int32, (LANES, WIDE), 0)
    col = lax.broadcasted_iota(jnp.int32, (LANES, WIDE), 1)
    return (row - mine * OWN == col // HEAD_DIM).astype(F32).astype(BF16)


def expand(values, spread):
    return sum(dot(piece, spread) for piece in parts_of(values, 2))


def pack_body(x_ref, b_ref, c_ref, dt_ref, out_ref):
    count = out_ref.shape[0]
    share = count // (b_ref.shape[1] // STATE)
    for k in range(count):
        g = k // share
        out_ref[k, :, :WIDE] = x_ref[:, k * WIDE : (k + 1) * WIDE]
        out_ref[k, :, WIDE : WIDE + STATE] = b_ref[:, g * STATE : (g + 1) * STATE]
        out_ref[k, :, WIDE + STATE : CONV] = c_ref[:, g * STATE : (g + 1) * STATE]
        out_ref[k, :, CONV:] = dt_ref[...]


def conv_block(win, taps, out_ref):
    tap_x, tap_b, tap_c = taps
    lead = tap_x.shape[0] - 1
    for lo in range(0, CONV, LANES):
        if lo < WIDE:
            tap, at = tap_x, lo
        else:
            tap, at = (tap_b, 0) if lo == WIDE else (tap_c, 0)
        total = jnp.zeros((BLOCK, LANES), F32)
        for k in range(lead + 1):
            first = 8 - lead + k
            total = total + tap[k : k + 1, at : at + LANES] * win[first : first + BLOCK, lo : lo + LANES]
        out_ref[:, lo : lo + LANES] = silu(total).astype(BF16)


def fresh_state(xbc, cum, dt, spread):
    last = cum[BLOCK - 1 :, :]
    tail = expand(jnp.exp(last - cum) * dt, spread)
    weighted = xbc[:, :WIDE].astype(F32) * tail
    turned = xbc[:, WIDE : WIDE + STATE].T
    return sum(dot(turned, piece) for piece in parts_of(weighted, 2))


def fade_of(cum, spread):
    last = jnp.broadcast_to(jnp.exp(cum[BLOCK - 1 :, :]), (8, LANES))
    return expand(last, spread)[:1]


def intra_block(xbc, cum, dt, mine, rows, put):
    b = xbc[:, WIDE : WIDE + STATE]
    c = xbc[:, WIDE + STATE : CONV]
    scores = lax.dot_general(c, b, (((1,), (1,)), ((), ())), preferred_element_type=F32)
    t_at = lax.broadcasted_iota(jnp.int32, (BLOCK, BLOCK), 0)
    s_at = lax.broadcasted_iota(jnp.int32, (BLOCK, BLOCK), 1)
    scores = jnp.where(t_at >= s_at, scores, 0.0)
    rows[0] = cum.T
    rows[1] = dt.T
    first = pl.multiple_of(mine * OWN, OWN)
    cum_rows = rows[0, pl.ds(first, OWN), :]
    dt_rows = rows[1, pl.ds(first, OWN), :]
    cum_cols = pltpu.roll(cum, lax.rem(LANES - mine * OWN, LANES), 1)
    left = lax.broadcasted_iota(jnp.int32, (BLOCK, LANES), 1) < HEAD_DIM
    zero = jnp.zeros((BLOCK, LANES), BF16)
    for q in range(WIDE // LANES):
        x = xbc[:, q * LANES : (q + 1) * LANES]
        total = None
        for half in range(2):
            h = 2 * q + half
            gap = jnp.minimum(cum_cols[:, h : h + 1] - cum_rows[h : h + 1, :], 0.0)
            mix = (scores * jnp.exp(gap) * dt_rows[h : h + 1, :]).astype(BF16)
            term = dot(mix, jnp.where(left if half == 0 else ~left, x, zero))
            total = term if total is None else total + term
        put(q, total)


def states_body(
    mine_ref, r_ref, halo_ref, tap_x, tap_b, tap_c, bias_ref, log_ref,
    xbc_ref, dt_ref, cum_ref, s_ref, send_ref, fade_ref, win, state, total_fade,
):
    j = pl.program_id(0)
    spread = expander(mine_ref[0])

    @pl.when(j == 0)
    def _():
        win[0:8] = halo_ref[...]
        state[...] = jnp.zeros_like(state)
        total_fade[...] = jnp.ones_like(total_fade)

    @pl.when(j > 0)
    def _():
        win[0:8] = win[BLOCK : BLOCK + 8]

    win[8 : 8 + BLOCK] = r_ref[:, :CONV].astype(F32)
    conv_block(win, (tap_x, tap_b, tap_c), xbc_ref)
    raw = r_ref[:, CONV:].astype(F32) + bias_ref[...]
    dt = jnp.maximum(raw, 0.0) + jnp.log1p(jnp.exp(-jnp.abs(raw)))
    t_at = lax.broadcasted_iota(jnp.int32, (BLOCK, BLOCK), 0)
    s_at = lax.broadcasted_iota(jnp.int32, (BLOCK, BLOCK), 1)
    lower = (t_at >= s_at).astype(F32).astype(BF16)
    cum = sum(dot(lower, piece) for piece in parts_of(dt * -jnp.exp(log_ref[...]), 3))
    dt_ref[...] = dt
    cum_ref[...] = cum
    fresh = fresh_state(xbc_ref, cum, dt, spread)
    fade = fade_of(cum, spread)
    s_ref[0] = fresh
    state[...] = fade * state[...] + fresh
    total_fade[...] = total_fade[...] * fade

    @pl.when(j == pl.num_programs(0) - 1)
    def _():
        send_ref[:STATE] = state[...].astype(BF16)
        send_ref[STATE : STATE + 16] = r_ref[BLOCK - 16 :, :WIDE]
        send_ref[STATE + 16 :, : 2 * STATE] = r_ref[BLOCK - 16 :, WIDE:CONV]
        send_ref[STATE + 16 :, 2 * STATE :] = jnp.zeros((16, WIDE - 2 * STATE), BF16)
        fade_ref[...] = jnp.broadcast_to(total_fade[...], (8, WIDE))


def intra_body(mine_ref, xbc_ref, dt_ref, cum_ref, y_ref, rows):
    def put(q, values):
        y_ref[:, q * LANES : (q + 1) * LANES] = values

    intra_block(xbc_ref, cum_ref[...], dt_ref[...], mine_ref[0], rows, put)


def carry_body(
    mine_ref, r_ref, got_ref, tap_x, tap_b, tap_c, xbc_ref, dt_ref, cum_ref, s_ref, part_ref,
    y_ref, win, first, rows, state, intra, fresh,
):
    j = pl.program_id(0)
    mine = mine_ref[0]
    spread = expander(mine)
    cum = cum_ref[...]
    dt = dt_ref[...]

    @pl.when(j == 0)
    def _():
        state[...] = got_ref[:STATE].astype(F32)
        win[0:8, :WIDE] = got_ref[STATE : STATE + 16].astype(F32)[8:]
        win[0:8, WIDE:] = got_ref[STATE + 16 :, : 2 * STATE].astype(F32)[8:]
        win[8 : 8 + BLOCK] = r_ref[:, :CONV].astype(F32)
        conv_block(win, (tap_x, tap_b, tap_c), first)

        def put(q, values):
            intra[:, q * LANES : (q + 1) * LANES] = values

        intra_block(first, cum, dt, mine, rows, put)
        fresh[...] = fresh_state(first, cum, dt, spread)

    @pl.when(j > 0)
    def _():
        first[:, WIDE + STATE :] = xbc_ref[:, WIDE + STATE :]
        intra[...] = part_ref[...]
        fresh[...] = s_ref[0]

    entering = state[...]
    c = first[:, WIDE + STATE :]
    carried = sum(dot(c, piece) for piece in parts_of(entering, 2))
    y_ref[...] = (intra[...] + carried * expand(jnp.exp(cum), spread)).astype(BF16)
    state[...] = fade_of(cum, spread) * entering + fresh[...]


def norm_body(y_ref, z_ref, gain_ref, out_ref):
    count = y_ref.shape[0]
    share = GROUPS * y_ref.shape[0] * WIDE // (GROUPS * out_ref.shape[1])
    per = 1024 // WIDE
    for g in range(count // per):
        gated = []
        square = 0.0
        for k in range(per):
            at = (g * per + k) * WIDE
            z = z_ref[:, at : at + WIDE].astype(F32)
            v = y_ref[g * per + k].astype(F32) * silu(z)
            gated.append(v)
            square = square + jnp.sum(v * v, axis=1, keepdims=True)
        scale = lax.rsqrt(square / (per * WIDE) + eps_norm)
        for k in range(per):
            at = (g * per + k) * WIDE
            out_ref[:, at : at + WIDE] = (gated[k] * scale * gain_ref[:, at : at + WIDE]).astype(BF16)


def shift(block, axis, distance):
    size = lax.axis_size(axis)
    return lax.ppermute(block, axis, [(i, i + distance) for i in range(size - distance)])


def shards(x_in, b_in, c_in, dt_in, z_in, conv_x, input_state_taps, conv_c, dt_bias, a_log, norm_gain):
    outer, inner, head = (lax.axis_size(a) for a in ("outer", "inner", "head"))
    dests = inner * head
    rows = x_in.shape[0]
    tokens = rows * dests
    blocks = tokens // BLOCK
    lead = conv_x.shape[0] - 1
    mine = (lax.axis_index("inner") * head + lax.axis_index("head")).astype(jnp.int32).reshape(1)
    share = dests * STATE // b_in.shape[1]
    params = functools.partial(pltpu.CompilerParams, vmem_limit_bytes=32 * 2**20)

    step = 4
    sent = pl.pallas_call(
        pack_body,
        grid=(dests // step,),
        in_specs=[
            pl.BlockSpec((rows, step * WIDE), lambda i: (0, i)),
            pl.BlockSpec((rows, step * STATE // share), lambda i: (0, i)),
            pl.BlockSpec((rows, step * STATE // share), lambda i: (0, i)),
            pl.BlockSpec((rows, LANES), lambda i: (0, 0)),
        ],
        out_specs=pl.BlockSpec((step, rows, CONV + LANES), lambda i: (i, 0, 0)),
        out_shape=jax.ShapeDtypeStruct((dests, rows, CONV + LANES), BF16),
        compiler_params=params(),
        name="pack",
    )(x_in, b_in, c_in, dt_in)
    got = lax.all_to_all(sent, ("inner", "head"), 0, 0, tiled=True).reshape(tokens, CONV + LANES)

    if outer > 2:
        halo = shift(got[-8:, :CONV], "outer", 1).astype(F32)
    else:
        halo = jnp.zeros((8, CONV), F32)
    tap_specs = [
        pl.BlockSpec((lead + 1, WIDE), lambda i, m: (0, m[0])),
        pl.BlockSpec((lead + 1, STATE), lambda i, m: (0, m[0] // share)),
        pl.BlockSpec((lead + 1, STATE), lambda i, m: (0, m[0] // share)),
    ]
    taps = (conv_x, input_state_taps, conv_c)

    def per_block(width, ahead=0):
        return pl.BlockSpec((BLOCK, width), lambda i, m: (i + ahead, 0))

    def whole(*shape):
        return pl.BlockSpec(shape, lambda i, m: (0,) * len(shape))

    extra = STATE + 32
    xbc, dt, cum, fresh, total, fade = pl.pallas_call(
        states_body,
        grid_spec=pltpu.PrefetchScalarGridSpec(
            num_scalar_prefetch=1,
            grid=(blocks,),
            in_specs=[per_block(CONV + LANES), whole(8, CONV), *tap_specs, whole(1, LANES), whole(1, LANES)],
            out_specs=[
                per_block(CONV), per_block(LANES), per_block(LANES),
                pl.BlockSpec((1, STATE, WIDE), lambda i, m: (i, 0, 0)),
                whole(extra, WIDE), whole(8, WIDE),
            ],
            scratch_shapes=[
                pltpu.VMEM((BLOCK + 8, CONV), F32),
                pltpu.VMEM((STATE, WIDE), F32),
                pltpu.VMEM((1, WIDE), F32),
            ],
        ),
        out_shape=[
            jax.ShapeDtypeStruct((tokens, CONV), BF16),
            jax.ShapeDtypeStruct((tokens, LANES), F32),
            jax.ShapeDtypeStruct((tokens, LANES), F32),
            jax.ShapeDtypeStruct((blocks, STATE, WIDE), F32),
            jax.ShapeDtypeStruct((extra, WIDE), BF16),
            jax.ShapeDtypeStruct((8, WIDE), F32),
        ],
        compiler_params=params(),
        name="states",
    )(mine, got, halo, *taps, dt_bias.reshape(1, -1), a_log.reshape(1, -1))

    before = shift(total, "outer", 1)
    reach = 1
    if outer > 2:
        entering, held = before[:STATE].astype(F32), shift(fade, "outer", 1)
        while reach < outer - 1:
            entering = entering + held[:1] * shift(entering, "outer", reach)
            held = held * shift(held, "outer", reach)
            reach *= 2
        before = jnp.concatenate([entering.astype(BF16), before[STATE:]], 0)

    part = pl.pallas_call(
        intra_body,
        grid_spec=pltpu.PrefetchScalarGridSpec(
            num_scalar_prefetch=1,
            grid=(blocks - 1,),
            in_specs=[per_block(CONV, 1), per_block(LANES, 1), per_block(LANES, 1)],
            out_specs=per_block(WIDE),
            scratch_shapes=[pltpu.VMEM((2, LANES, BLOCK), F32)],
        ),
        out_shape=jax.ShapeDtypeStruct((tokens - BLOCK, WIDE), F32),
        compiler_params=params(),
        cost_estimate=pl.CostEstimate(
            flops=2 * blocks * OWN * BLOCK * BLOCK * 160,
            bytes_accessed=tokens * (CONV * 2 + LANES * 8 + WIDE * 4),
            transcendentals=blocks * OWN * BLOCK * BLOCK,
        ),
        name="intra",
    )(mine, xbc, dt, cum)

    y = pl.pallas_call(
        carry_body,
        grid_spec=pltpu.PrefetchScalarGridSpec(
            num_scalar_prefetch=1,
            grid=(blocks,),
            in_specs=[
                whole(BLOCK, CONV + LANES), whole(extra, WIDE), *tap_specs,
                per_block(CONV), per_block(LANES), per_block(LANES),
                pl.BlockSpec((1, STATE, WIDE), lambda i, m: (i, 0, 0)),
                pl.BlockSpec((BLOCK, WIDE), lambda i, m: (jnp.maximum(i - 1, 0), 0)),
            ],
            out_specs=per_block(WIDE),
            scratch_shapes=[
                pltpu.VMEM((BLOCK + 8, CONV), F32),
                pltpu.VMEM((BLOCK, CONV), BF16),
                pltpu.VMEM((2, LANES, BLOCK), F32),
                pltpu.VMEM((STATE, WIDE), F32),
                pltpu.VMEM((BLOCK, WIDE), F32),
                pltpu.VMEM((STATE, WIDE), F32),
            ],
        ),
        out_shape=jax.ShapeDtypeStruct((tokens, WIDE), BF16),
        compiler_params=params(),
        name="carry",
    )(mine, got, before, *taps, xbc, dt, cum, fresh, part)

    home = lax.all_to_all(y.reshape(dests, rows, WIDE), ("inner", "head"), 0, 0, tiled=True)
    return pl.pallas_call(
        norm_body,
        grid=(dests // step,),
        in_specs=[
            pl.BlockSpec((step, rows, WIDE), lambda i: (i, 0, 0)),
            pl.BlockSpec((rows, step * WIDE), lambda i: (0, i)),
            pl.BlockSpec((1, step * WIDE), lambda i: (0, i)),
        ],
        out_specs=pl.BlockSpec((rows, step * WIDE), lambda i: (0, i)),
        out_shape=jax.ShapeDtypeStruct((rows, dests * WIDE), BF16),
        compiler_params=params(),
        name="norm",
    )(home, z_in, norm_gain.reshape(1, -1))


def solution(mesh):
    ctx, head = mesh.devices.shape
    inner = max(1, GROUPS * 16 // (OWN * head))
    cut = Mesh(mesh.devices.reshape(ctx // inner, inner, head), ("outer", "inner", "head"))
    rows = P(("outer", "inner", "head"), None)
    return jax.shard_map(
        shards,
        mesh=cut,
        in_specs=(rows,) * 5 + (P(),) * 6,
        out_specs=rows,
        check_vma=False,
    )
```

time: 212 us -> 61 us (0.29)
  waiting for transfers between devices: 102 us -> 16.4 us
  starting transfers between devices: 29.7 us -> 10.9 us
  other arithmetic: 15.7 us -> 0 us
  between operations: 13.7 us -> 0.11 us
  blocking collectives: 30.4 us -> 17.1 us
  Pallas kernels: 0 us -> 12.6 us
  local copies, waits for them, and re-layouts: 15.3 us -> 3.45 us
  matrix products: 4.09 us -> 0 us
    all_gather x1 -> x0, waiting for transfers between devices: 89.1 us -> none  [prefix(): everything = jax.tree.map(lambda part: lax.all_gather(part, axis), shard)]
    all_gather x1 -> x0, blocking collectives: 19 us -> none  [prefix(): everything = jax.tree.map(lambda part: lax.all_gather(part, axis), shard)]
    pallas_call x0 -> x5, Pallas kernels: none -> 12.6 us  [the longest x1 4.88 us: shards(): pl.pallas_call(states_body, grid_spec=pltpu.PrefetchScalarGridSpec(num_sc...]
    select_n x8 -> x0, other arithmetic: 11.7 us -> none  [lap(): return jax.tree.map(lambda a, b: jnp.where(reached, a, b), new, before)]
    all_to_all x5 -> x1, starting transfers between devices: 17.7 us -> 6.42 us  [shards(): lax.all_to_all(sent, ('inner', 'head'), 0, 0, tiled=True)]
    ppermute x3 -> x1, starting transfers between devices: 11.9 us -> 4.49 us  [shift(): lax.ppermute(block, axis, [(i, i + distance) for i in range(size - distan...]
    all_to_all x1, blocking collectives: 11.4 us -> 17.1 us  [shards(): lax.all_to_all(y.reshape(dests, rows, WIDE), ('inner', 'head'), 0, 0, til...]
    all_to_all x5 -> x0, local copies, waits for them, and re-layouts: 5.66 us -> none  [the longest x1 1.88 us: shards(): lax.all_to_all(x_src, 'head', split_axis=1, concat_axis=0, tiled=True)]
  transfers between devices with their start and end apart: 9 -> 2, of which waited for: 5 -> 2; matrix products, arithmetic and copies ran while one was open for 13% -> 0% of each run, Pallas kernels for 0% -> 3%
where the time goes in v1:
time: 61 us; the launch traced here: 60.6 us
  blocking collectives  17.1 us (28%)
  waiting for transfers between devices  16.4 us (27%)
  Pallas kernels  12.6 us (21%)
  starting transfers between devices  10.9 us (18%)
  local copies, waits for them, and re-layouts  3.45 us (6%)
    all_to_all x1, blocking collectives, shards(): lax.all_to_all(y.reshape(dests, rows, WIDE), ('inner', 'head'), 0, 0, til...  17.1 us
    all_to_all x1, waiting for transfers between devices, shards(): lax.all_to_all(sent, ('inner', 'head'), 0, 0, tiled=True)  14.7 us
    all_to_all x1, starting transfers between devices, shards(): lax.all_to_all(sent, ('inner', 'head'), 0, 0, tiled=True)  6.42 us
    pallas_call x1, Pallas kernels, shards(): pl.pallas_call(states_body, grid_spec=pltpu.PrefetchScalarGridSpec(num_sc...  4.88 us
    ppermute x1, starting transfers between devices, shift(): lax.ppermute(block, axis, [(i, i + distance) for i in range(size - distan...  4.49 us
    unnamed x22, local copies, waits for them, and re-layouts  3.45 us
    pallas_call x1, Pallas kernels, shards(): pl.pallas_call(carry_body, grid_spec=pltpu.PrefetchScalarGridSpec(num_sca...  2.68 us
    pallas_call x1, Pallas kernels, shards(): pl.pallas_call(norm_body, grid=(dests // step,), in_specs=[pl.BlockSpec((...  1.89 us
  transfers between devices with their start and end apart: 2, of which 2 were waited for; matrix products, arithmetic and copies ran while one was open for 0% of the time, Pallas kernels for 3%

profile of v1, /device:TPU:0, one launch (start us, length us, event | category | flops | bytes accessed | tf_op | source)
XLA Modules:
  0.0 60.6 jit_solution(3964722714786494998)
XLA Ops:
  0.0 0.0 copy-start
  0.0 1.0 %copy-done = bf16[32,8192]{1,0:T(8,128)(2,1)S(1)} copy-done((bf16[32,8192]{1,0:T(8,128)(2,1)S(1)}, bf16[32,8192]{1,0:T(8,128)(2,1)}, u32[]{:S(2)}) %copy-start) | copy-done | bytes 524312
  1.0 0.0 copy-start.5
  1.0 0.8 %copy-done.5 = bf16[32,1024]{1,0:T(8,128)(2,1)S(1)} copy-done((bf16[32,1024]{1,0:T(8,128)(2,1)S(1)}, bf16[32,1024]{1,0:T(8,128)(2,1)}, u32[]{:S(2)}) %copy-start.5) | copy-done | bytes 65560
  1.9 0.0 copy-start.6
  1.9 0.8 %copy-done.6 = bf16[32,1024]{1,0:T(8,128)(2,1)S(1)} copy-done((bf16[32,1024]{1,0:T(8,128)(2,1)S(1)}, bf16[32,1024]{1,0:T(8,128)(2,1)}, u32[]{:S(2)}) %copy-start.6) | copy-done | bytes 65560
  2.7 0.0 copy-start.8
  2.7 0.7 %copy-done.8 = bf16[32,128]{1,0:T(8,128)(2,1)S(1)} copy-done((bf16[32,128]{1,0:T(8,128)(2,1)S(1)}, bf16[32,128]{1,0:T(8,128)(2,1)}, u32[]{:S(2)}) %copy-start.8) | copy-done | bytes 8216
  3.4 1.6 %pack.1 = bf16[16,32,896]{2,1,0:T(8,128)(2,1)} custom-call(bf16[32,8192]{1,0:T(8,128)(2,1)S(1)} %copy-done, bf16[32,1024]{1,0:T(8,128)(2,1)S(1)} %copy-done.5, bf16[32,1024]{1,0:T(8,128)(2,1)S(1)} %copy-done.6, bf16[32,128]{1,0:T(8,128)(2,1)S(1)} %copy-done.8), custom_call_target="tpu_custom_call" | custom-call | tf_op jit(solution)/shard_map/pack/pallas_call | solution.py:240
  5.0 0.0 copy-start.2
  5.0 0.0 copy-start.9
  5.0 0.0 copy-start.10
  5.0 6.4 %all-to-all-start = ((bf16[16,32,896]{2,1,0:T(8,128)(2,1)}), bf16[16,32,896]{2,1,0:T(8,128)(2,1)S(1)}, u32[]{:S(2)}, u32[]{:S(2)}) async-start(bf16[16,32,896]{2,1,0:T(8,128)(2,1)} %pack.1), calls=%async_computation | async-start | bytes 1835008 | tf_op jit(solution)/shard_map/all_to_all | solution.py:254
  11.4 0.0 copy-start.3
  11.4 0.0 copy-start.4
  11.5 14.7 %all-to-all-done = bf16[16,32,896]{2,1,0:T(8,128)(2,1)S(1)} async-done(((bf16[16,32,896]{2,1,0:T(8,128)(2,1)}), bf16[16,32,896]{2,1,0:T(8,128)(2,1)S(1)}, u32[]{:S(2)}, u32[]{:S(2)}) %all-to-all-start) | async-done | bytes 917536 | tf_op jit(solution)/shard_map/all_to_all | solution.py:254
  26.2 0.0 copy-done.2
  26.2 0.0 copy-done.9
  26.2 0.0 copy-done.10
  26.2 0.0 copy-done.3
  26.2 0.0 copy-done.4
  26.2 4.9 %states.1 = (bf16[512,768]{1,0:T(8,128)(2,1)S(1)}, f32[512,128]{1,0:T(8,128)S(1)}, f32[512,128]{1,0:T(8,128)S(1)}, f32[4,128,512]{2,1,0:T(8,128)S(1)}, bf16[160,512]{1,0:T(8,128)(2,1)S(1)}, /*index=5*/f32[8,512]{1,0:T(8,128)}) custom-call(s32[1]{0:T(128)} %bitcast.mine_ref, bf16[512,896]{1,0:T(8,128)(2,1)S(1)} %bitcast.6, ...), custom_call_target="tpu_custom_call" | custom-call | tf_op jit(solution)/shard_map/states/pallas_call | solution.py:274
  31.1 4.5 %collective-permute-start = (bf16[160,512]{1,0:T(8,128)(2,1)S(1)}, bf16[160,512]{1,0:T(8,128)(2,1)S(1)}, u32[]{:S(2)}, u32[]{:S(2)}) collective-permute-start(bf16[160,512]{1,0:T(8,128)(2,1)S(1)} %get-tuple-element.10), channel_id=1, source_target_pairs={{0,16},{1,17},{2,18},{3,19},{4,20},{5,21},{6,22},{7,23},{8,24},{9,... | collective-permute-start | bytes 491528 | tf_op jit(solution)/shard_map/ppermute | solution.py:225
  35.6 1.6 %intra.1.part_ref = f32[384,512]{1,0:T(8,128)S(1)} custom-call(s32[1]{0:T(128)} %bitcast.mine_ref, bf16[512,768]{1,0:T(8,128)(2,1)S(1)} %get-tuple-element.11.xbc_ref, f32[512,128]{1,0:T(8,128)S(1)} %get-tuple-element.12.dt_ref, f32[512,128]{1,0:T(8,128)S(1)} %get-tuple-element.13.cum_ref), custom_call_target="tpu_custom_call" | custom-call | flops 167772160 | bytes 2359296 | tf_op jit(solution)/shard_map/intra/pallas_call | solution.py:313
  37.2 1.7 %collective-permute-done.got_ref = bf16[160,512]{1,0:T(8,128)(2,1)S(1)} collective-permute-done((bf16[160,512]{1,0:T(8,128)(2,1)S(1)}, bf16[160,512]{1,0:T(8,128)(2,1)S(1)}, u32[]{:S(2)}, u32[]{:S(2)}) %collective-permute-start) | collective-permute-done | bytes 163872 | tf_op jit(solution)/shard_map/ppermute | solution.py:225
  38.9 2.7 %carry.1 = bf16[512,512]{1,0:T(8,128)(2,1)S(1)} custom-call(s32[1]{0:T(128)} %bitcast.mine_ref, bf16[512,896]{1,0:T(8,128)(2,1)S(1)} %bitcast.7, bf16[160,512]{1,0:T(8,128)(2,1)S(1)} %collective-permute-done.got_ref, f32[4,8192]{1,0:T(4,128)S(1)} %copy-done.2, f32[4,1024]{1,0:T(4,128)S(1)} %copy-done.3, f32[4,1024]{1,0:T(4,128)S(1)} %copy-done.4, ...), custom_call_target="tpu_custom_call" | custom-call | tf_op jit(solution)/shard_map/carry/pallas_call | solution.py:332
  41.6 0.0 copy-start.1
  41.6 0.0 copy-start.7
  41.6 17.1 %all_to_all.10.y_ref = bf16[16,32,512]{2,1,0:T(8,128)(2,1)S(1)} all-to-all(bf16[16,32,512]{2,1,0:T(8,128)(2,1)S(1)} %bitcast.8), channel_id=1, replica_groups=mesh['outer'=2,'inner'=4,'head'=4] {'inner','head'}, dimensions={0} | all-to-all | bytes 1048576 | tf_op jit(solution)/shard_map/all_to_all | solution.py:358
  58.7 0.0 copy-done.1
  58.7 0.0 copy-done.7
  58.7 1.9 %norm.1 = bf16[32,8192]{1,0:T(8,128)(2,1)} custom-call(bf16[16,32,512]{2,1,0:T(8,128)(2,1)S(1)} %all_to_all.10.y_ref, bf16[32,8192]{1,0:T(8,128)(2,1)S(1)} %copy-done.1, f32[1,8192]{1,0:T(1,128)S(1)} %bitcast.9), custom_call_target="tpu_custom_call" | custom-call | tf_op jit(solution)/shard_map/norm/pallas_call | solution.py:359
  (1 shorter events, 0.0 us)
Async XLA Ops:
  0.0 1.0 %copy-start = (bf16[32,8192]{1,0:T(8,128)(2,1)S(1)}, bf16[32,8192]{1,0:T(8,128)(2,1)}, u32[]{:S(2)}) copy-start(bf16[32,8192]{1,0:T(8,128)(2,1)} %x_ref.1) | copy-start | bytes 1572868
  1.0 0.8 %copy-start.5 = (bf16[32,1024]{1,0:T(8,128)(2,1)S(1)}, bf16[32,1024]{1,0:T(8,128)(2,1)}, u32[]{:S(2)}) copy-start(bf16[32,1024]{1,0:T(8,128)(2,1)} %b_ref.1) | copy-start | bytes 196612
  1.9 0.8 %copy-start.6 = (bf16[32,1024]{1,0:T(8,128)(2,1)S(1)}, bf16[32,1024]{1,0:T(8,128)(2,1)}, u32[]{:S(2)}) copy-start(bf16[32,1024]{1,0:T(8,128)(2,1)} %c_ref.1) | copy-start | bytes 196612
  2.7 0.7 %copy-start.8 = (bf16[32,128]{1,0:T(8,128)(2,1)S(1)}, bf16[32,128]{1,0:T(8,128)(2,1)}, u32[]{:S(2)}) copy-start(bf16[32,128]{1,0:T(8,128)(2,1)} %dt_ref.1) | copy-start | bytes 24580
  5.0 21.2 %copy-start.2 = (f32[4,8192]{1,0:T(4,128)S(1)}, f32[4,8192]{1,0:T(4,128)}, u32[]{:S(2)}) copy-start(f32[4,8192]{1,0:T(4,128)} %tap_x.3) | copy-start | bytes 393220
  5.0 21.2 %copy-start.9 = (f32[128]{0:T(128)S(1)}, f32[128]{0:T(128)}, u32[]{:S(2)}) copy-start(f32[128]{0:T(128)} %param.19) | copy-start | bytes 1540
  5.0 21.2 %copy-start.10 = (f32[128]{0:T(128)S(1)}, f32[128]{0:T(128)}, u32[]{:S(2)}) copy-start(f32[128]{0:T(128)} %param.20) | copy-start | bytes 1540
  5.0 21.2 %all-to-all-start = ((bf16[16,32,896]{2,1,0:T(8,128)(2,1)}), bf16[16,32,896]{2,1,0:T(8,128)(2,1)S(1)}, u32[]{:S(2)}, u32[]{:S(2)}) async-start(bf16[16,32,896]{2,1,0:T(8,128)(2,1)} %pack.1), calls=%async_computation | async-start | bytes 1835008 | tf_op jit(solution)/shard_map/all_to_all | solution.py:254
  11.4 14.8 %copy-start.3 = (f32[4,1024]{1,0:T(4,128)S(1)}, f32[4,1024]{1,0:T(4,128)}, u32[]{:S(2)}) copy-start(f32[4,1024]{1,0:T(4,128)} %tap_b.3) | copy-start | bytes 49156
  11.4 14.8 %copy-start.4 = (f32[4,1024]{1,0:T(4,128)S(1)}, f32[4,1024]{1,0:T(4,128)}, u32[]{:S(2)}) copy-start(f32[4,1024]{1,0:T(4,128)} %tap_c.3) | copy-start | bytes 49156
  31.1 7.8 %collective-permute-start = (bf16[160,512]{1,0:T(8,128)(2,1)S(1)}, bf16[160,512]{1,0:T(8,128)(2,1)S(1)}, u32[]{:S(2)}, u32[]{:S(2)}) collective-permute-start(bf16[160,512]{1,0:T(8,128)(2,1)S(1)} %get-tuple-element.10), channel_id=1, source_target_pairs={{0,16},{1,17},{2,18},{3,19},{4,20},{5,21},{6,22},{7,23},{8,24},{9,... | collective-permute-start | bytes 491528 | tf_op jit(solution)/shard_map/ppermute | solution.py:225
  41.6 17.1 %copy-start.1 = (bf16[32,8192]{1,0:T(8,128)(2,1)S(1)}, bf16[32,8192]{1,0:T(8,128)(2,1)}, u32[]{:S(2)}) copy-start(bf16[32,8192]{1,0:T(8,128)(2,1)} %z_ref.1) | copy-start | bytes 1572868
  41.6 17.1 %copy-start.7 = (f32[8192]{0:T(1024)S(1)}, f32[8192]{0:T(1024)}, u32[]{:S(2)}) copy-start(f32[8192]{0:T(1024)} %param.21) | copy-start | bytes 98308

commit v2 on v0

v2 whole, which is shorter than its diff:
```python
import jax
import jax.numpy as jnp
from jax import lax
from jax.experimental import pallas as pl
from jax.experimental.pallas import tpu as pltpu
from jax.sharding import Mesh
from jax.sharding import PartitionSpec as P

HEAD_DIM = 64
STATE = 128
GROUPS = 8
BLOCK = 128
OWN = 8
WIDE = OWN * HEAD_DIM
LANES = 128
TILES = WIDE // LANES
TOP = 8

eps_norm = 1e-05
F32 = jnp.float32
BF16 = jnp.bfloat16
IN_VMEM = pl.BlockSpec(memory_space=pltpu.VMEM)
IN_SMEM = pl.BlockSpec(memory_space=pltpu.SMEM)


def dot(a, b):
    return jnp.dot(a, b, preferred_element_type=F32)


def dot_t(a, b):
    return lax.dot_general(a, b, (((0,), (0,)), ((), ())), preferred_element_type=F32)


def iota(shape, axis):
    return lax.broadcasted_iota(jnp.int32, shape, axis)


def parts_of(values, count):
    out = []
    for k in range(count):
        piece = values.astype(BF16).astype(F32)
        out.append(piece)
        if k + 1 < count:
            values = values - piece
    return out


def stacked(values, count):
    return jnp.concatenate(parts_of(values, count), 0).astype(BF16)


def one_hot(rows, width):
    shape = (rows, OWN * width)
    return (iota(shape, 0) % OWN == iota(shape, 1) // width).astype(F32).astype(BF16)


def expand(values):
    return dot_t(stacked(values, 2), one_hot(2 * OWN, HEAD_DIM))


def silu(v):
    return v * jax.nn.sigmoid(v)


def conv(window, tap):
    total = tap[0:1] * window(0)
    for k in range(1, tap.shape[0]):
        total = total + tap[k : k + 1] * window(k)
    return silu(total)


def tap_tiles(mine, share, tap_x, tap_b, tap_c):
    at_x = pl.multiple_of(mine * WIDE, WIDE)
    at_s = pl.multiple_of(mine // share * STATE, STATE)
    return [tap_x[:, pl.ds(at_x + q * LANES, LANES)] for q in range(TILES)] + [
        tap_b[:, pl.ds(at_s, STATE)],
        tap_c[:, pl.ds(at_s, STATE)],
    ]


def pack_body(mine_ref, x_hbm, b_hbm, c_hbm, dt_hbm, out_hbm, x_v, b_v, c_v, dt_v, turn, out_v, sem_in, sem_out):
    count, total, _ = out_v.shape
    rows = x_v.shape[0]
    share = count * STATE // b_v.shape[1]
    cuts = 4
    step = count // cuts
    wide = step * WIDE
    small = [
        pltpu.make_async_copy(src, dst, sem_in.at[k])
        for k, (src, dst) in enumerate(((dt_hbm, dt_v), (b_hbm, b_v), (c_hbm, c_v)))
    ]
    large = [
        pltpu.make_async_copy(x_hbm.at[:, pl.ds(i * wide, wide)], x_v.at[:, pl.ds(i * wide, wide)], sem_in.at[3 + i])
        for i in range(cuts)
    ]
    for copy in small + large:
        copy.start()
    small[0].wait()
    turn[...] = jnp.zeros_like(turn)
    at = pl.multiple_of(lax.rem(mine_ref[0], BLOCK // rows) * rows, rows)
    turn[pl.ds(at, rows), :] = dt_v[...].astype(F32)
    heads = turn[...].T
    for k in range(count):
        out_v[k, (TILES + 2) * rows :, :] = heads[k * OWN : (k + 1) * OWN].astype(BF16)
    small[1].wait()
    small[2].wait()
    for k in range(count):
        g = k // share
        out_v[k, TILES * rows : (TILES + 1) * rows, :] = b_v[:, g * STATE : (g + 1) * STATE]
        out_v[k, (TILES + 1) * rows : (TILES + 2) * rows, :] = c_v[:, g * STATE : (g + 1) * STATE]
    out = []
    for i in range(cuts):
        large[i].wait()
        for k in range(i * step, (i + 1) * step):
            for q in range(TILES):
                lo = k * WIDE + q * LANES
                out_v[k, q * rows : (q + 1) * rows, :] = x_v[:, lo : lo + LANES]
        copy = pltpu.make_async_copy(out_v.at[pl.ds(i * step, step)], out_hbm.at[pl.ds(i * step, step)], sem_out.at[i])
        copy.start()
        out.append(copy)
    for copy in out:
        copy.wait()


def gate_body(z_ref, out_ref):
    for lo in range(0, z_ref.shape[1], WIDE):
        out_ref[:, lo : lo + WIDE] = silu(z_ref[:, lo : lo + WIDE].astype(F32))


def states_body(
    share, mine_ref, got_ref, halo_ref, tap_x, tap_b, tap_c, bias_ref, log_ref,
    xb_ref, dt_ref, cum_ref, s_ref, send_ref, fade_ref, win,
):
    mine = mine_ref[0]
    sources, total, _ = got_ref.shape
    rows = (total - OWN) // (TILES + 2)
    blocks = sources * rows // BLOCK
    per = BLOCK // rows

    own = iota((OWN, LANES), 0) + mine * OWN == iota((OWN, LANES), 1)
    bias = jnp.sum(jnp.where(own, bias_ref[...], 0.0), axis=1, keepdims=True)
    rate = -jnp.exp(jnp.sum(jnp.where(own, log_ref[...], 0.0), axis=1, keepdims=True))
    upto = (iota((BLOCK, BLOCK), 0) <= iota((BLOCK, BLOCK), 1)).astype(F32).astype(BF16)
    for j in range(blocks):
        raw = got_ref[j * per, (TILES + 2) * rows :, :].astype(F32)
        for s in range(1, per):
            raw = raw + got_ref[j * per + s, (TILES + 2) * rows :, :].astype(F32)
        raw = raw + bias
        dt = jnp.maximum(raw, 0.0) + jnp.log1p(jnp.exp(-jnp.abs(raw)))
        sums = dot(stacked(dt * rate, 4), upto)
        cum = sums[:OWN] + sums[OWN : 2 * OWN] + sums[2 * OWN : 3 * OWN]
        dt_ref[j] = dt
        cum_ref[j] = cum

    taps = tap_tiles(mine, share, tap_x, tap_b, tap_c)
    first = TOP - taps[0].shape[0] + 1
    for q in range(TILES + 1):
        win[q, :TOP] = halo_ref[:, q * LANES : (q + 1) * LANES]
        for s in range(sources):
            at = TOP + s * rows
            win[q, at : at + rows] = got_ref[s, q * rows : (q + 1) * rows, :].astype(F32)
    state = None
    for j in range(blocks):
        at = j * BLOCK
        for q in range(TILES + 1):
            done = conv(lambda k: win[q, at + first + k : at + first + k + BLOCK], taps[q])
            xb_ref[at : at + BLOCK, q * LANES : (q + 1) * LANES] = done.astype(BF16)
        cum = cum_ref[j]
        last = cum[:, BLOCK - 1 :]
        tail = expand(jnp.exp(last - cum) * dt_ref[j])
        fade = expand(jnp.broadcast_to(jnp.exp(last), (OWN, LANES)))[:1]
        b = xb_ref[at : at + BLOCK, WIDE:]
        weighted = xb_ref[at : at + BLOCK, :WIDE].astype(F32) * tail
        twice = jnp.concatenate([b, b], 0)
        if j == 0:
            top = iota((BLOCK, WIDE), 0) < TOP
            head = dot_t(twice, stacked(jnp.where(top, weighted, 0.0), 2))
            weighted = jnp.where(top, 0.0, weighted)
        fresh = dot_t(twice, stacked(weighted, 2))
        s_ref[j] = fresh
        state = fresh + head if j == 0 else fade * state + fresh
        whole = fade if j == 0 else whole * fade
    send_ref[:STATE] = state.astype(BF16)
    ends = [got_ref[sources - 1, q * rows : (q + 1) * rows, :].astype(F32)[rows - TOP :] for q in range(TILES + 2)]
    ends += [jnp.zeros_like(ends[0])] * (TILES - 2)
    send_ref[STATE:] = jnp.concatenate(
        [jnp.concatenate(ends[:TILES], 1), jnp.concatenate(ends[TILES:], 1)], 0
    ).astype(BF16)
    fade_ref[...] = jnp.broadcast_to(whole, (8, WIDE))


def intra_body(
    share, mine_ref, got_ref, halo_ref, tap_x, tap_b, tap_c, xb_ref, dt_ref, cum_ref,
    c_ref, part_ref, win, turn,
):
    sources, total, _ = got_ref.shape
    rows = (total - OWN) // (TILES + 2)
    blocks = sources * rows // BLOCK
    tap = tap_tiles(mine_ref[0], share, tap_x, tap_b, tap_c)[-1]
    first = TOP - tap.shape[0] + 1
    q = TILES + 1
    win[:TOP] = halo_ref[:, q * LANES : (q + 1) * LANES]
    for s in range(sources):
        at = TOP + s * rows
        win[at : at + rows] = got_ref[s, q * rows : (q + 1) * rows, :].astype(F32)
    turn[...] = jnp.zeros_like(turn)
    for j in range(blocks):
        turn[j * OWN : (j + 1) * OWN] = cum_ref[j]
    cols = turn[...].T
    t_at = iota((BLOCK, BLOCK), 0)
    s_at = iota((BLOCK, BLOCK), 1)
    left = iota((BLOCK, LANES), 1) < HEAD_DIM
    zero = jnp.zeros((BLOCK, LANES), BF16)
    for j in range(blocks):
        at = j * BLOCK
        c = conv(lambda k: win[at + first + k : at + first + k + BLOCK], tap).astype(BF16)
        c_ref[at : at + BLOCK] = c
        b = xb_ref[at : at + BLOCK, WIDE:]
        scores = lax.dot_general(c, b, (((1,), (1,)), ((), ())), preferred_element_type=F32)
        keep = t_at >= s_at
        if j == 0:
            keep = keep & (s_at >= TOP)
        scores = jnp.where(keep, scores, 0.0)
        cum = cum_ref[j]
        dt = dt_ref[j]
        for q in range(TILES):
            x = xb_ref[at : at + BLOCK, q * LANES : (q + 1) * LANES]
            mixes = []
            for h in (2 * q, 2 * q + 1):
                col = j * OWN + h
                gap = jnp.minimum(cols[:, col : col + 1] - cum[h : h + 1], 0.0)
                mixes.append((scores * jnp.exp(gap) * dt[h : h + 1]).astype(BF16))
            both = jnp.concatenate([jnp.where(left, x, zero), jnp.where(left, zero, x)], 0)
            part_ref[at : at + BLOCK, q * LANES : (q + 1) * LANES] = dot(jnp.concatenate(mixes, 1), both)


def carry_body(
    share, mine_ref, got_ref, before_ref, tap_x, tap_b, tap_c, dt_ref, cum_ref, s_ref, c_ref, part_ref,
    y_ref, win, c_first,
):
    sources, total, _ = got_ref.shape
    rows = (total - OWN) // (TILES + 2)
    blocks = sources * rows // BLOCK
    taps = tap_tiles(mine_ref[0], share, tap_x, tap_b, tap_c)
    first = TOP - taps[0].shape[0] + 1

    halo = before_ref[STATE:].astype(F32)
    tops = []
    for q in range(TILES + 2):
        if q < TILES:
            win[q, :TOP] = halo[:TOP, q * LANES : (q + 1) * LANES]
        else:
            win[q, :TOP] = halo[TOP:, (q - TILES) * LANES : (q - TILES + 1) * LANES]
        win[q, TOP:] = got_ref[0, q * rows : (q + 1) * rows, :].astype(F32)[:TOP]
        done = conv(lambda k: win[q, first + k : first + k + TOP], taps[q])
        tops.append(done.astype(BF16).astype(F32))
    x_top = jnp.concatenate(tops[:TILES], 1)
    b_top = tops[TILES]
    c_first[...] = c_ref[:BLOCK].astype(F32)
    c_first[:TOP] = tops[TILES + 1]
    c = c_first[...].astype(BF16)
    wide = OWN * TOP
    scores = lax.dot_general(
        c, jnp.concatenate([b_top] * OWN, 0).astype(BF16), (((1,), (1,)), ((), ())), preferred_element_type=F32
    )
    cum = cum_ref[0]
    dt = dt_ref[0]
    spread = one_hot(4 * OWN, TOP)
    cum_t = dot_t(stacked(cum, 4), spread)
    same = iota((TOP, wide), 0) == iota((TOP, wide), 1) % TOP
    cum_s = jnp.sum(jnp.where(same, cum_t[:TOP], 0.0), axis=0, keepdims=True)
    dt_s = jnp.sum(jnp.where(same, dot_t(stacked(dt, 4), spread)[:TOP], 0.0), axis=0, keepdims=True)
    mix = scores * jnp.exp(jnp.minimum(cum_t - cum_s, 0.0)) * dt_s
    mix = jnp.where(iota((BLOCK, wide), 0) >= iota((BLOCK, wide), 1) % TOP, mix, 0.0).astype(BF16)
    shape = (wide, WIDE)
    own = iota(shape, 0) // TOP == iota(shape, 1) // HEAD_DIM
    added = dot(mix, jnp.where(own, jnp.concatenate([x_top] * OWN, 0), 0.0).astype(BF16))
    tail = expand(jnp.exp(cum[:, BLOCK - 1 :] - cum) * dt)[:TOP]
    b_twice = jnp.concatenate([b_top, b_top], 0).astype(BF16)
    head = dot_t(b_twice, stacked(x_top * tail, 2))

    state = before_ref[:STATE].astype(F32)
    for j in range(blocks):
        at = j * BLOCK
        grown = expand(jnp.exp(cum_ref[j]))
        if j > 0:
            c = c_ref[at : at + BLOCK]
        carried = dot(jnp.concatenate([c, c], 1), stacked(state, 2))
        part = part_ref[at : at + BLOCK]
        if j == 0:
            part = part + added
        y_ref[at : at + BLOCK] = (part + carried * grown).astype(BF16)
        if j + 1 < blocks:
            state = grown[BLOCK - 1 :] * state + s_ref[j]
            if j == 0:
                state = state + head


def norm_body(y_ref, gate_ref, gain_ref, out_ref):
    count = y_ref.shape[0]
    per = count // GROUPS
    for g in range(GROUPS):
        gated = []
        square = 0.0
        for k in range(g * per, (g + 1) * per):
            v = y_ref[k].astype(F32) * gate_ref[:, k * WIDE : (k + 1) * WIDE]
            gated.append(v)
            square = square + jnp.sum(v * v, axis=1, keepdims=True)
        scale = lax.rsqrt(square / (per * WIDE) + eps_norm)
        for k in range(g * per, (g + 1) * per):
            at = k * WIDE
            gain = gain_ref[:, at : at + WIDE]
            out_ref[:, at : at + WIDE] = (gated[k - g * per] * scale * gain).astype(BF16)


def shift(block, axis, distance):
    size = lax.axis_size(axis)
    return lax.ppermute(block, axis, [(i, i + distance) for i in range(size - distance)])


def kernel(body, name, ins, outs, scratch=(), cost=None, out_specs=None):
    return pl.pallas_call(
        body,
        in_specs=ins,
        out_specs=out_specs or [IN_VMEM] * len(outs),
        out_shape=outs,
        scratch_shapes=list(scratch),
        compiler_params=pltpu.CompilerParams(vmem_limit_bytes=40 * 2**20),
        cost_estimate=cost,
        name=name,
    )


def shards(x_in, b_in, c_in, dt_in, z_in, conv_x, input_state_taps, conv_c, dt_bias, a_log, norm_gain):
    outer, inner, head = (lax.axis_size(a) for a in ("outer", "inner", "head"))
    dests = inner * head
    rows = x_in.shape[0]
    tokens = rows * dests
    blocks = tokens // BLOCK
    mine = (lax.axis_index("inner") * head + lax.axis_index("head")).astype(jnp.int32).reshape(1)
    share = dests * STATE // b_in.shape[1]

    def of(dtype, *shape):
        return jax.ShapeDtypeStruct(shape, dtype)

    def bind(body):
        def bound(*refs):
            return body(share, *refs)

        return bound

    total = (TILES + 2) * rows + OWN
    hbm = pl.BlockSpec(memory_space=pltpu.HBM)
    [sent] = kernel(
        pack_body, "pack", [IN_SMEM] + [hbm] * 4, [of(BF16, dests, total, LANES)],
        [
            pltpu.VMEM(x_in.shape, BF16), pltpu.VMEM(b_in.shape, BF16), pltpu.VMEM(c_in.shape, BF16),
            pltpu.VMEM(dt_in.shape, BF16), pltpu.VMEM((BLOCK, LANES), F32), pltpu.VMEM((dests, total, LANES), BF16),
            pltpu.SemaphoreType.DMA((7,)), pltpu.SemaphoreType.DMA((4,)),
        ],
        out_specs=[hbm],
    )(mine, x_in, b_in, c_in, dt_in)
    got = lax.all_to_all(sent, ("inner", "head"), 0, 0, tiled=True)
    [gate] = kernel(
        gate_body, "gate", [IN_VMEM], [of(F32, *z_in.shape)],
        cost=pl.CostEstimate(flops=5 * z_in.size, bytes_accessed=6 * z_in.size, transcendentals=z_in.size),
    )(z_in)

    if outer > 2:
        ends = got[-1, : (TILES + 2) * rows].reshape(TILES + 2, rows, LANES)[:, -TOP:]
        halo = shift(ends, "outer", 1).transpose(1, 0, 2).reshape(TOP, -1).astype(F32)
    else:
        halo = jnp.zeros((TOP, (TILES + 2) * LANES), F32)
    taps = (conv_x, input_state_taps, conv_c)

    extra = STATE + 2 * TOP
    xb, dt, cum, fresh, send, fade = kernel(
        bind(states_body), "states", [IN_SMEM] + [IN_VMEM] * 7,
        [
            of(BF16, tokens, WIDE + STATE), of(F32, blocks, OWN, BLOCK), of(F32, blocks, OWN, BLOCK),
            of(F32, blocks, STATE, WIDE), of(BF16, extra, WIDE), of(F32, 8, WIDE),
        ],
        [pltpu.VMEM((TILES + 1, TOP + tokens, LANES), F32)],
    )(mine, got, halo, *taps, dt_bias.reshape(1, -1), a_log.reshape(1, -1))

    before = shift(send, "outer", 1)
    if outer > 2:
        entering, held, reach = before[:STATE].astype(F32), shift(fade, "outer", 1), 1
        while reach < outer - 1:
            entering = entering + held[:1] * shift(entering, "outer", reach)
            held = held * shift(held, "outer", reach)
            reach *= 2
        before = jnp.concatenate([entering.astype(BF16), before[STATE:]], 0)

    c, part = kernel(
        bind(intra_body), "intra", [IN_SMEM] + [IN_VMEM] * 8,
        [of(BF16, tokens, STATE), of(F32, tokens, WIDE)],
        [pltpu.VMEM((TOP + tokens, LANES), F32), pltpu.VMEM((BLOCK, LANES), F32)],
        pl.CostEstimate(
            flops=2 * blocks * OWN * BLOCK * BLOCK * 160,
            bytes_accessed=tokens * WIDE * 8,
            transcendentals=blocks * OWN * BLOCK * BLOCK,
        ),
    )(mine, got, halo, *taps, xb, dt, cum)

    [y] = kernel(
        bind(carry_body), "carry", [IN_SMEM] + [IN_VMEM] * 10, [of(BF16, tokens, WIDE)],
        [pltpu.VMEM((TILES + 2, 2 * TOP, LANES), F32), pltpu.VMEM((BLOCK, STATE), F32)],
    )(mine, got, before, *taps, dt, cum, fresh, c, part)

    home = lax.all_to_all(y.reshape(dests, rows, WIDE), ("inner", "head"), 0, 0, tiled=True)
    [out] = kernel(
        norm_body, "norm", [IN_VMEM] * 3, [of(BF16, rows, dests * WIDE)],
    )(home, gate, norm_gain.reshape(1, -1))
    return out


def solution(mesh):
    ctx, head = mesh.devices.shape
    inner = max(1, GROUPS * 16 // (OWN * head))
    cut = Mesh(mesh.devices.reshape(ctx // inner, inner, head), ("outer", "inner", "head"))
    rows = P(("outer", "inner", "head"), None)
    return jax.shard_map(
        shards,
        mesh=cut,
        in_specs=(rows,) * 5 + (P(),) * 6,
        out_specs=rows,
        check_vma=False,
    )
```

time: 212 us -> 55.2 us (0.26)
  waiting for transfers between devices: 102 us -> 11.8 us
  starting transfers between devices: 29.7 us -> 10.4 us
  other arithmetic: 15.7 us -> 0 us
  between operations: 13.7 us -> 0.1 us
  local copies, waits for them, and re-layouts: 15.3 us -> 4.13 us
  blocking collectives: 30.4 us -> 19.9 us
  Pallas kernels: 0 us -> 8.35 us
  matrix products: 4.09 us -> 0 us
    all_gather x1 -> x0, waiting for transfers between devices: 89.1 us -> none  [prefix(): everything = jax.tree.map(lambda part: lax.all_gather(part, axis), shard)]
    all_gather x1 -> x0, blocking collectives: 19 us -> none  [prefix(): everything = jax.tree.map(lambda part: lax.all_gather(part, axis), shard)]
    all_to_all x5 -> x1, starting transfers between devices: 17.7 us -> 5.89 us  [shards(): lax.all_to_all(y.reshape(dests, rows, WIDE), ('inner', 'head'), 0, 0, til...]
    select_n x8 -> x0, other arithmetic: 11.7 us -> none  [lap(): return jax.tree.map(lambda a, b: jnp.where(reached, a, b), new, before)]
    all_to_all x1, blocking collectives: 11.4 us -> 19.9 us  [shards(): got = lax.all_to_all(sent, ('inner', 'head'), 0, 0, tiled=True)]
    pallas_call x0 -> x6, Pallas kernels: none -> 8.35 us  [the longest x1 2.3 us: shards(): kernel(bind(states_body), 'states', [IN_SMEM] + [IN_VMEM] * 7, [of(BF16,...]
    ppermute x3 -> x1, starting transfers between devices: 11.9 us -> 4.47 us  [shift(): lax.ppermute(block, axis, [(i, i + distance) for i in range(size - distan...]
    all_to_all x5 -> x0, local copies, waits for them, and re-layouts: 5.66 us -> none  [the longest x1 1.88 us: shards(): lax.all_to_all(x_src, 'head', split_axis=1, concat_axis=0, tiled=True)]
  transfers between devices with their start and end apart: 9 -> 2, of which waited for: 5 -> 2; matrix products, arithmetic and copies ran while one was open for 13% -> 0% of each run, Pallas kernels for 0% -> 2%
where the time goes in v2:
time: 55.2 us; the launch traced here: 54.7 us
  blocking collectives  19.9 us (36%)
  waiting for transfers between devices  11.8 us (21%)
  starting transfers between devices  10.4 us (19%)
  Pallas kernels  8.35 us (15%)
  local copies, waits for them, and re-layouts  4.13 us (7%)
    all_to_all x1, blocking collectives, shards(): got = lax.all_to_all(sent, ('inner', 'head'), 0, 0, tiled=True)  19.9 us
    all_to_all x1, waiting for transfers between devices, shards(): lax.all_to_all(y.reshape(dests, rows, WIDE), ('inner', 'head'), 0, 0, til...  10.4 us
    all_to_all x1, starting transfers between devices, shards(): lax.all_to_all(y.reshape(dests, rows, WIDE), ('inner', 'head'), 0, 0, til...  5.89 us
    ppermute x1, starting transfers between devices, shift(): lax.ppermute(block, axis, [(i, i + distance) for i in range(size - distan...  4.47 us
    unnamed x22, local copies, waits for them, and re-layouts  4.13 us
    pallas_call x1, Pallas kernels, shards(): kernel(bind(states_body), 'states', [IN_SMEM] + [IN_VMEM] * 7, [of(BF16,...  2.3 us
    pallas_call x1, Pallas kernels, shards(): kernel(bind(carry_body), 'carry', [IN_SMEM] + [IN_VMEM] * 10, [of(BF16, t...  1.96 us
    pallas_call x1, Pallas kernels, shards(): kernel(pack_body, 'pack', [IN_SMEM] + [hbm] * 4, [of(BF16, dests, total,...  1.72 us
  transfers between devices with their start and end apart: 2, of which 2 were waited for; matrix products, arithmetic and copies ran while one was open for 0% of the time, Pallas kernels for 2%

profile of v2, /device:TPU:0, one launch (start us, length us, event | category | flops | bytes accessed | tf_op | source)
XLA Modules:
  0.0 54.7 jit_solution(11952687836272476678)
XLA Ops:
  0.0 0.0 copy-start.8
  0.0 0.7 %copy-done.8 = bf16[32,128]{1,0:T(8,128)(2,1)S(1)} copy-done((bf16[32,128]{1,0:T(8,128)(2,1)S(1)}, bf16[32,128]{1,0:T(8,128)(2,1)}, u32[]{:S(2)}) %copy-start.8) | copy-done | bytes 8216
  0.7 0.0 copy-start.2
  0.7 1.0 %copy-done.2 = bf16[32,8192]{1,0:T(8,128)(2,1)S(1)} copy-done((bf16[32,8192]{1,0:T(8,128)(2,1)S(1)}, bf16[32,8192]{1,0:T(8,128)(2,1)}, u32[]{:S(2)}) %copy-start.2) | copy-done | bytes 524312
  1.7 0.0 copy-start.5
  1.7 0.8 %copy-done.5 = bf16[32,1024]{1,0:T(8,128)(2,1)S(1)} copy-done((bf16[32,1024]{1,0:T(8,128)(2,1)S(1)}, bf16[32,1024]{1,0:T(8,128)(2,1)}, u32[]{:S(2)}) %copy-start.5) | copy-done | bytes 65560
  2.6 0.0 copy-start.6
  2.6 0.8 %copy-done.6 = bf16[32,1024]{1,0:T(8,128)(2,1)S(1)} copy-done((bf16[32,1024]{1,0:T(8,128)(2,1)S(1)}, bf16[32,1024]{1,0:T(8,128)(2,1)}, u32[]{:S(2)}) %copy-start.6) | copy-done | bytes 65560
  3.4 1.7 %pack.1 = bf16[16,200,128]{2,1,0:T(8,128)(2,1)S(1)} custom-call(s32[1]{0:T(128)} %bitcast.mine_ref.refs_0_, bf16[32,8192]{1,0:T(8,128)(2,1)S(1)} %copy-done.2, bf16[32,1024]{1,0:T(8,128)(2,1)S(1)} %copy-done.5, bf16[32,1024]{1,0:T(8,128)(2,1)S(1)} %copy-done.6, bf16[32,128]{1,0:T(8,128)(2,1)S(1)} %copy-done.8), custom_call_target="tpu_custom_call" | custom-call | tf_op jit(solution)/shard_map/pack/pallas_call | solution.py:354
  5.1 0.0 copy-start
  5.2 0.0 copy-start.4
  5.2 19.9 %all_to_all.10.refs_1_ = bf16[16,200,128]{2,1,0:T(8,128)(2,1)S(1)} all-to-all(bf16[16,200,128]{2,1,0:T(8,128)(2,1)S(1)} %pack.1), channel_id=1, replica_groups=mesh['outer'=2,'inner'=4,'head'=4] {'inner','head'}, dimensions={0} | all-to-all | bytes 1638400 | tf_op jit(solution)/shard_map/all_to_all | solution.py:363
  25.1 0.0 copy-start.3
  25.1 0.0 copy-start.9
  25.1 0.0 copy-start.10
  25.1 0.0 copy-done
  25.1 0.0 copy-done.4
  25.1 0.7 %copy-done.3 = f32[4,1024]{1,0:T(4,128)S(1)} copy-done((f32[4,1024]{1,0:T(4,128)S(1)}, f32[4,1024]{1,0:T(4,128)}, u32[]{:S(2)}) %copy-start.3) | copy-done | bytes 16408
  25.8 0.0 copy-done.9
  25.8 0.0 copy-done.10
  25.8 2.3 %states.1 = (bf16[512,640]{1,0:T(8,128)(2,1)S(1)}, f32[4,8,128]{2,1,0:T(8,128)S(1)}, f32[4,8,128]{2,1,0:T(8,128)S(1)}, f32[4,128,512]{2,1,0:T(8,128)S(1)}, bf16[...) custom-call(s32[1]{0:T(128)} %bitcast.mine_ref.refs_0_, bf16[16,200,128]{2,1,0:T(8,128)(2,1)S(1)} %all_to_all.10.refs_1_, ...), custom_call_target="tpu_custom_call" | custom-call | tf_op jit(solution)/shard_map/states/pallas_call | solution.py:377
  28.1 4.5 %collective-permute-start = (bf16[144,512]{1,0:T(8,128)(2,1)S(1)}, bf16[144,512]{1,0:T(8,128)(2,1)S(1)}, u32[]{:S(2)}, u32[]{:S(2)}) collective-permute-start(bf16[144,512]{1,0:T(8,128)(2,1)S(1)} %get-tuple-element.12), channel_id=1, source_target_pairs={{0,16},{1,17},{2,18},{3,19},{4,20},{5,21},{6,22},{7,23},{8,24},{9,... | collective-permute-start | bytes 442376 | tf_op jit(solution)/shard_map/ppermute | solution.py:318
  32.6 1.2 %intra.1 = (bf16[512,128]{1,0:T(8,128)(2,1)S(1)}, f32[512,512]{1,0:T(8,128)S(1)}) custom-call(s32[1]{0:T(128)} %bitcast.mine_ref.refs_0_, bf16[16,200,128]{2,1,0:T(8,128)(2,1)S(1)} %all_to_all.10.refs_1_, f32[8,768]{1,0:T(8,128)S(1)} %broadcast_in_dim.3.refs_2_, f32[4,8192]{1,0:T(4,128)S(1)} %copy-done, f32[4,1024]{1,0:T(4,128)S(1)} %copy-done.3, ...), custom_call_target="tpu_custom_call" | custom-call | flops 167772160 | bytes 2097152 | tf_op jit(solution)/shard_map/intra/pallas_call | solution.py:395
  33.8 1.4 %collective-permute-done.refs_2_ = bf16[144,512]{1,0:T(8,128)(2,1)S(1)} collective-permute-done((bf16[144,512]{1,0:T(8,128)(2,1)S(1)}, bf16[144,512]{1,0:T(8,128)(2,1)S(1)}, u32[]{:S(2)}, u32[]{:S(2)}) %collective-permute-start) | collective-permute-done | bytes 147488 | tf_op jit(solution)/shard_map/ppermute | solution.py:318
  35.2 2.0 %carry.1 = bf16[512,512]{1,0:T(8,128)(2,1)} custom-call(s32[1]{0:T(128)} %bitcast.mine_ref.refs_0_, bf16[16,200,128]{2,1,0:T(8,128)(2,1)S(1)} %all_to_all.10.refs_1_, bf16[144,512]{1,0:T(8,128)(2,1)S(1)} %collective-permute-done.refs_2_, f32[4,8192]{1,0:T(4,128)S(1)} %copy-done, f32[4,1024]{1,0:T(4,128)S(1)} %copy-done.3, f32[4,1024]{1,0:T(4,128)S(1)} %copy-done.4, ...), custom_call_target="tpu_custom_call" | custom-call | tf_op jit(solution)/shard_map/carry/pallas_call | solution.py:406
  37.2 0.0 copy-start.1
  37.2 5.9 %all-to-all-start.1 = ((bf16[16,32,512]{2,1,0:T(8,128)(2,1)}), bf16[16,32,512]{2,1,0:T(8,128)(2,1)S(1)}, u32[]{:S(2)}, u32[]{:S(2)}) async-start(bf16[16,32,512]{2,1,0:T(8,128)(2,1)} %bitcast.3), calls=%async_computation.1 | async-start | bytes 1048576 | tf_op jit(solution)/shard_map/all_to_all | solution.py:411
  43.1 0.0 copy-done.1
  43.1 0.0 copy-start.7
  43.1 0.1 gate.1.gate_ref
  43.3 10.4 %all-to-all-done.1.y_ref = bf16[16,32,512]{2,1,0:T(8,128)(2,1)S(1)} async-done(((bf16[16,32,512]{2,1,0:T(8,128)(2,1)}), bf16[16,32,512]{2,1,0:T(8,128)(2,1)S(1)}, u32[]{:S(2)}, u32[]{:S(2)}) %all-to-all-start.1) | async-done | bytes 524320 | tf_op jit(solution)/shard_map/all_to_all | solution.py:411
  53.7 0.0 copy-done.7
  53.7 1.0 %norm.1 = bf16[32,8192]{1,0:T(8,128)(2,1)} custom-call(bf16[16,32,512]{2,1,0:T(8,128)(2,1)S(1)} %all-to-all-done.1.y_ref, f32[32,8192]{1,0:T(8,128)S(1)} %gate.1.gate_ref, f32[1,8192]{1,0:T(1,128)S(1)} %bitcast.5), custom_call_target="tpu_custom_call" | custom-call | tf_op jit(solution)/shard_map/norm/pallas_call | solution.py:412
  (1 shorter events, 0.0 us)
Async XLA Ops:
  0.0 0.7 %copy-start.8 = (bf16[32,128]{1,0:T(8,128)(2,1)S(1)}, bf16[32,128]{1,0:T(8,128)(2,1)}, u32[]{:S(2)}) copy-start(bf16[32,128]{1,0:T(8,128)(2,1)} %dt_hbm.1) | copy-start | bytes 24580
  0.7 1.0 %copy-start.2 = (bf16[32,8192]{1,0:T(8,128)(2,1)S(1)}, bf16[32,8192]{1,0:T(8,128)(2,1)}, u32[]{:S(2)}) copy-start(bf16[32,8192]{1,0:T(8,128)(2,1)} %x_hbm.1) | copy-start | bytes 1572868
  1.7 0.8 %copy-start.5 = (bf16[32,1024]{1,0:T(8,128)(2,1)S(1)}, bf16[32,1024]{1,0:T(8,128)(2,1)}, u32[]{:S(2)}) copy-start(bf16[32,1024]{1,0:T(8,128)(2,1)} %b_hbm.1) | copy-start | bytes 196612
  2.6 0.8 %copy-start.6 = (bf16[32,1024]{1,0:T(8,128)(2,1)S(1)}, bf16[32,1024]{1,0:T(8,128)(2,1)}, u32[]{:S(2)}) copy-start(bf16[32,1024]{1,0:T(8,128)(2,1)} %c_hbm.1) | copy-start | bytes 196612
  5.1 20.0 %copy-start = (f32[4,8192]{1,0:T(4,128)S(1)}, f32[4,8192]{1,0:T(4,128)}, u32[]{:S(2)}) copy-start(f32[4,8192]{1,0:T(4,128)} %refs_3_.5) | copy-start | bytes 393220
  5.2 20.0 %copy-start.4 = (f32[4,1024]{1,0:T(4,128)S(1)}, f32[4,1024]{1,0:T(4,128)}, u32[]{:S(2)}) copy-start(f32[4,1024]{1,0:T(4,128)} %refs_5_.5) | copy-start | bytes 49156
  25.1 0.7 %copy-start.3 = (f32[4,1024]{1,0:T(4,128)S(1)}, f32[4,1024]{1,0:T(4,128)}, u32[]{:S(2)}) copy-start(f32[4,1024]{1,0:T(4,128)} %refs_4_.5) | copy-start | bytes 49156
  25.1 0.7 %copy-start.9 = (f32[128]{0:T(128)S(1)}, f32[128]{0:T(128)}, u32[]{:S(2)}) copy-start(f32[128]{0:T(128)} %param.19) | copy-start | bytes 1540
  25.1 0.7 %copy-start.10 = (f32[128]{0:T(128)S(1)}, f32[128]{0:T(128)}, u32[]{:S(2)}) copy-start(f32[128]{0:T(128)} %param.20) | copy-start | bytes 1540
  28.1 7.1 %collective-permute-start = (bf16[144,512]{1,0:T(8,128)(2,1)S(1)}, bf16[144,512]{1,0:T(8,128)(2,1)S(1)}, u32[]{:S(2)}, u32[]{:S(2)}) collective-permute-start(bf16[144,512]{1,0:T(8,128)(2,1)S(1)} %get-tuple-element.12), channel_id=1, source_target_pairs={{0,16},{1,17},{2,18},{3,19},{4,20},{5,21},{6,22},{7,23},{8,24},{9,... | collective-permute-start | bytes 442376 | tf_op jit(solution)/shard_map/ppermute | solution.py:318
  37.2 5.9 %copy-start.1 = (bf16[32,8192]{1,0:T(8,128)(2,1)S(1)}, bf16[32,8192]{1,0:T(8,128)(2,1)}, u32[]{:S(2)}) copy-start(bf16[32,8192]{1,0:T(8,128)(2,1)} %z_ref.1) | copy-start | bytes 1572868
  37.2 16.4 %all-to-all-start.1 = ((bf16[16,32,512]{2,1,0:T(8,128)(2,1)}), bf16[16,32,512]{2,1,0:T(8,128)(2,1)S(1)}, u32[]{:S(2)}, u32[]{:S(2)}) async-start(bf16[16,32,512]{2,1,0:T(8,128)(2,1)} %bitcast.3), calls=%async_computation.1 | async-start | bytes 1048576 | tf_op jit(solution)/shard_map/all_to_all | solution.py:411
  43.1 10.5 %copy-start.7 = (f32[8192]{0:T(1024)S(1)}, f32[8192]{0:T(1024)}, u32[]{:S(2)}) copy-start(f32[8192]{0:T(1024)} %param.21) | copy-start | bytes 98308

commit v3 on v2

--- a/solution.py
+++ b/solution.py
@@ -69,17 +69,20 @@
     return silu(total)
 
 
-def tap_tiles(mine, share, tap_x, tap_b, tap_c):
-    at_x = pl.multiple_of(mine * WIDE, WIDE)
-    at_s = pl.multiple_of(mine // share * STATE, STATE)
-    return [tap_x[:, pl.ds(at_x + q * LANES, LANES)] for q in range(TILES)] + [
-        tap_b[:, pl.ds(at_s, STATE)],
-        tap_c[:, pl.ds(at_s, STATE)],
-    ]
-
-
-def pack_body(mine_ref, x_hbm, b_hbm, c_hbm, dt_hbm, out_hbm, x_v, b_v, c_v, dt_v, turn, out_v, sem_in, sem_out):
-    count, total, _ = out_v.shape
+def tiles_of(own_ref):
+    return [own_ref[:lead_of(own_ref), q * LANES : (q + 1) * LANES] for q in range(TILES + 2)]
+
+
+def lead_of(own_ref):
+    return own_ref.shape[0] - 2 * OWN
+
+
+def pack_body(
+    mine_ref, x_hbm, b_hbm, c_hbm, dt_hbm, tap_x, tap_b, tap_c, bias_hbm, log_hbm,
+    out_v, own_ref, x_v, b_v, c_v, dt_v, turn, x_tap, s_taps, heads_v, sem_in, sem_own,
+):
+    mine = mine_ref[0]
+    count = out_v.shape[0]
     rows = x_v.shape[0]
     share = count * STATE // b_v.shape[1]
     cuts = 4
@@ -93,11 +96,23 @@
         pltpu.make_async_copy(x_hbm.at[:, pl.ds(i * wide, wide)], x_v.at[:, pl.ds(i * wide, wide)], sem_in.at[3 + i])
         for i in range(cuts)
     ]
-    for copy in small + large:
+    at_x = pl.multiple_of(mine * WIDE, WIDE)
+    at_s = pl.multiple_of(mine // share * STATE, STATE)
+    own = [
+        pltpu.make_async_copy(src, dst, sem_own.at[k])
+        for k, (src, dst) in enumerate((
+            (tap_x.at[:, pl.ds(at_x, WIDE)], x_tap),
+            (tap_b.at[:, pl.ds(at_s, STATE)], s_taps.at[0]),
+            (tap_c.at[:, pl.ds(at_s, STATE)], s_taps.at[1]),
+            (bias_hbm, heads_v.at[0]),
+            (log_hbm, heads_v.at[1]),
+        ))
+    ]
+    for copy in small + large + own:
         copy.start()
     small[0].wait()
     turn[...] = jnp.zeros_like(turn)
-    at = pl.multiple_of(lax.rem(mine_ref[0], BLOCK // rows) * rows, rows)
+    at = pl.multiple_of(lax.rem(mine, BLOCK // rows) * rows, rows)
     turn[pl.ds(at, rows), :] = dt_v[...].astype(F32)
     heads = turn[...].T
     for k in range(count):
@@ -108,18 +123,23 @@
         g = k // share
         out_v[k, TILES * rows : (TILES + 1) * rows, :] = b_v[:, g * STATE : (g + 1) * STATE]
         out_v[k, (TILES + 1) * rows : (TILES + 2) * rows, :] = c_v[:, g * STATE : (g + 1) * STATE]
-    out = []
     for i in range(cuts):
         large[i].wait()
         for k in range(i * step, (i + 1) * step):
             for q in range(TILES):
                 lo = k * WIDE + q * LANES
                 out_v[k, q * rows : (q + 1) * rows, :] = x_v[:, lo : lo + LANES]
-        copy = pltpu.make_async_copy(out_v.at[pl.ds(i * step, step)], out_hbm.at[pl.ds(i * step, step)], sem_out.at[i])
-        copy.start()
-        out.append(copy)
-    for copy in out:
+    for copy in own:
         copy.wait()
+    taps = x_tap.shape[0]
+    own_ref[:taps, :WIDE] = x_tap[...]
+    own_ref[:taps, WIDE : WIDE + STATE] = s_taps[0]
+    own_ref[:taps, WIDE + STATE :] = s_taps[1]
+    mask = iota((OWN, LANES), 0) + mine * OWN == iota((OWN, LANES), 1)
+    for k in range(2):
+        column = jnp.sum(jnp.where(mask, heads_v[k], 0.0), axis=1, keepdims=True)
+        at = taps + k * OWN
+        own_ref[at : at + OWN, :LANES] = jnp.broadcast_to(column, (OWN, LANES))
 
 
 def gate_body(z_ref, out_ref):
@@ -128,18 +148,16 @@
 
 
 def states_body(
-    share, mine_ref, got_ref, halo_ref, tap_x, tap_b, tap_c, bias_ref, log_ref,
-    xb_ref, dt_ref, cum_ref, s_ref, send_ref, fade_ref, win,
+    got_ref, halo_ref, own_ref, xb_ref, dt_ref, cum_ref, s_ref, send_ref, fade_ref, win,
 ):
-    mine = mine_ref[0]
     sources, total, _ = got_ref.shape
     rows = (total - OWN) // (TILES + 2)
     blocks = sources * rows // BLOCK
     per = BLOCK // rows
 
-    own = iota((OWN, LANES), 0) + mine * OWN == iota((OWN, LANES), 1)
-    bias = jnp.sum(jnp.where(own, bias_ref[...], 0.0), axis=1, keepdims=True)
-    rate = -jnp.exp(jnp.sum(jnp.where(own, log_ref[...], 0.0), axis=1, keepdims=True))
+    lead = lead_of(own_ref)
+    bias = own_ref[lead : lead + OWN, :LANES]
+    rate = -jnp.exp(own_ref[lead + OWN :, :LANES])
     upto = (iota((BLOCK, BLOCK), 0) <= iota((BLOCK, BLOCK), 1)).astype(F32).astype(BF16)
     for j in range(blocks):
         raw = got_ref[j * per, (TILES + 2) * rows :, :].astype(F32)
@@ -152,8 +170,8 @@
         dt_ref[j] = dt
         cum_ref[j] = cum
 
-    taps = tap_tiles(mine, share, tap_x, tap_b, tap_c)
-    first = TOP - taps[0].shape[0] + 1
+    taps = tiles_of(own_ref)
+    first = TOP - lead + 1
     for q in range(TILES + 1):
         win[q, :TOP] = halo_ref[:, q * LANES : (q + 1) * LANES]
         for s in range(sources):
@@ -183,20 +201,21 @@
     send_ref[:STATE] = state.astype(BF16)
     ends = [got_ref[sources - 1, q * rows : (q + 1) * rows, :].astype(F32)[rows - TOP :] for q in range(TILES + 2)]
     ends += [jnp.zeros_like(ends[0])] * (TILES - 2)
-    send_ref[STATE:] = jnp.concatenate(
-        [jnp.concatenate(ends[:TILES], 1), jnp.concatenate(ends[TILES:], 1)], 0
-    ).astype(BF16)
+    half = TOP // 2
+    upper = pltpu.roll(jnp.concatenate(ends[:TILES], 1), half, 0)
+    keep = iota((TOP, WIDE), 0) < half
+    send_ref[STATE:] = jnp.where(keep, upper, jnp.concatenate(ends[TILES:], 1)).astype(BF16)
     fade_ref[...] = jnp.broadcast_to(whole, (8, WIDE))
 
 
 def intra_body(
-    share, mine_ref, got_ref, halo_ref, tap_x, tap_b, tap_c, xb_ref, dt_ref, cum_ref,
-    c_ref, part_ref, win, turn,
+    got_ref, halo_ref, own_ref, xb_ref, dt_ref, cum_ref, s_ref,
+    c_ref, part_ref, grown_ref, factor_ref, tail_ref, win, turn,
 ):
     sources, total, _ = got_ref.shape
     rows = (total - OWN) // (TILES + 2)
     blocks = sources * rows // BLOCK
-    tap = tap_tiles(mine_ref[0], share, tap_x, tap_b, tap_c)[-1]
+    tap = tiles_of(own_ref)[-1]
     first = TOP - tap.shape[0] + 1
     q = TILES + 1
     win[:TOP] = halo_ref[:, q * LANES : (q + 1) * LANES]
@@ -211,6 +230,7 @@
     s_at = iota((BLOCK, BLOCK), 1)
     left = iota((BLOCK, LANES), 1) < HEAD_DIM
     zero = jnp.zeros((BLOCK, LANES), BF16)
+    past = jnp.zeros((OWN, 1), F32)
     for j in range(blocks):
         at = j * BLOCK
         c = conv(lambda k: win[at + first + k : at + first + k + BLOCK], tap).astype(BF16)
@@ -223,39 +243,66 @@
         scores = jnp.where(keep, scores, 0.0)
         cum = cum_ref[j]
         dt = dt_ref[j]
+        grown = expand(jnp.exp(cum))
+        if j < 2:
+            grown_ref[at : at + BLOCK] = grown
+        else:
+            past = past + cum_ref[j - 1][:, BLOCK - 1 :]
+            grown_ref[at : at + BLOCK] = expand(jnp.exp(cum + past))
+        if j > 0:
+            local = s_ref[0] if j == 1 else fade * local + s_ref[j - 1]
+            carried = dot(jnp.concatenate([c, c], 1), stacked(local, 2)) * grown
+        fade = grown[BLOCK - 1 :]
         for q in range(TILES):
-            x = xb_ref[at : at + BLOCK, q * LANES : (q + 1) * LANES]
+            lo = q * LANES
+            x = xb_ref[at : at + BLOCK, lo : lo + LANES]
             mixes = []
             for h in (2 * q, 2 * q + 1):
                 col = j * OWN + h
                 gap = jnp.minimum(cols[:, col : col + 1] - cum[h : h + 1], 0.0)
                 mixes.append((scores * jnp.exp(gap) * dt[h : h + 1]).astype(BF16))
             both = jnp.concatenate([jnp.where(left, x, zero), jnp.where(left, zero, x)], 0)
-            part_ref[at : at + BLOCK, q * LANES : (q + 1) * LANES] = dot(jnp.concatenate(mixes, 1), both)
-
-
-def carry_body(
-    share, mine_ref, got_ref, before_ref, tap_x, tap_b, tap_c, dt_ref, cum_ref, s_ref, c_ref, part_ref,
-    y_ref, win, c_first,
-):
+            part = dot(jnp.concatenate(mixes, 1), both)
+            part_ref[at : at + BLOCK, lo : lo + LANES] = part if j == 0 else part + carried[:, lo : lo + LANES]
+
+    cum = cum_ref[0]
+    dt = dt_ref[0]
+    wide = OWN * TOP
+    spread = one_hot(4 * OWN, TOP)
+    cum_t = dot_t(stacked(cum, 4), spread)
+    same = iota((TOP, wide), 0) == iota((TOP, wide), 1) % TOP
+    cum_s = jnp.sum(jnp.where(same, cum_t[:TOP], 0.0), axis=0, keepdims=True)
+    dt_s = jnp.sum(jnp.where(same, dot_t(stacked(dt, 4), spread)[:TOP], 0.0), axis=0, keepdims=True)
+    decay = jnp.exp(jnp.minimum(cum_t - cum_s, 0.0))
+    seen = iota((BLOCK, wide), 0) >= iota((BLOCK, wide), 1) % TOP
+    factor_ref[0] = jnp.where(seen, decay, 0.0)
+    factor_ref[1] = jnp.broadcast_to(dt_s, (BLOCK, wide))
+    tail_ref[...] = expand(jnp.exp(cum[:, BLOCK - 1 :] - cum) * dt)[:TOP]
+
+
+def carry_body(got_ref, before_ref, own_ref, c_ref, part_ref, grown_ref, factor_ref, tail_ref, y_ref, win, c_first):
     sources, total, _ = got_ref.shape
     rows = (total - OWN) // (TILES + 2)
     blocks = sources * rows // BLOCK
-    taps = tap_tiles(mine_ref[0], share, tap_x, tap_b, tap_c)
+    taps = tiles_of(own_ref)
     first = TOP - taps[0].shape[0] + 1
 
     halo = before_ref[STATE:].astype(F32)
+    upper = pltpu.roll(halo, TOP // 2, 0)
     tops = []
     for q in range(TILES + 2):
-        if q < TILES:
-            win[q, :TOP] = halo[:TOP, q * LANES : (q + 1) * LANES]
-        else:
-            win[q, :TOP] = halo[TOP:, (q - TILES) * LANES : (q - TILES + 1) * LANES]
+        lo = q * LANES
+        win[q, :TOP] = upper[:, lo : lo + LANES] if q < TILES else halo[:, lo - WIDE : lo - WIDE + LANES]
         win[q, TOP:] = got_ref[0, q * rows : (q + 1) * rows, :].astype(F32)[:TOP]
         done = conv(lambda k: win[q, first + k : first + k + TOP], taps[q])
         tops.append(done.astype(BF16).astype(F32))
     x_top = jnp.concatenate(tops[:TILES], 1)
     b_top = tops[TILES]
+    b_twice = jnp.concatenate([b_top, b_top], 0).astype(BF16)
+    head = dot_t(b_twice, stacked(x_top * tail_ref[...], 2))
+    state = before_ref[:STATE]
+    later = stacked(grown_ref[BLOCK - 1 : BLOCK] * state.astype(F32) + head, 2)
+
     c_first[...] = c_ref[:BLOCK].astype(F32)
     c_first[:TOP] = tops[TILES + 1]
     c = c_first[...].astype(BF16)
@@ -263,37 +310,16 @@
     scores = lax.dot_general(
         c, jnp.concatenate([b_top] * OWN, 0).astype(BF16), (((1,), (1,)), ((), ())), preferred_element_type=F32
     )
-    cum = cum_ref[0]
-    dt = dt_ref[0]
-    spread = one_hot(4 * OWN, TOP)
-    cum_t = dot_t(stacked(cum, 4), spread)
-    same = iota((TOP, wide), 0) == iota((TOP, wide), 1) % TOP
-    cum_s = jnp.sum(jnp.where(same, cum_t[:TOP], 0.0), axis=0, keepdims=True)
-    dt_s = jnp.sum(jnp.where(same, dot_t(stacked(dt, 4), spread)[:TOP], 0.0), axis=0, keepdims=True)
-    mix = scores * jnp.exp(jnp.minimum(cum_t - cum_s, 0.0)) * dt_s
-    mix = jnp.where(iota((BLOCK, wide), 0) >= iota((BLOCK, wide), 1) % TOP, mix, 0.0).astype(BF16)
+    mix = (scores * factor_ref[0] * factor_ref[1]).astype(BF16)
     shape = (wide, WIDE)
     own = iota(shape, 0) // TOP == iota(shape, 1) // HEAD_DIM
     added = dot(mix, jnp.where(own, jnp.concatenate([x_top] * OWN, 0), 0.0).astype(BF16))
-    tail = expand(jnp.exp(cum[:, BLOCK - 1 :] - cum) * dt)[:TOP]
-    b_twice = jnp.concatenate([b_top, b_top], 0).astype(BF16)
-    head = dot_t(b_twice, stacked(x_top * tail, 2))
-
-    state = before_ref[:STATE].astype(F32)
-    for j in range(blocks):
+    y_ref[:BLOCK] = (part_ref[:BLOCK] + added + dot(c, state) * grown_ref[:BLOCK]).astype(BF16)
+    for j in range(1, blocks):
         at = j * BLOCK
-        grown = expand(jnp.exp(cum_ref[j]))
-        if j > 0:
-            c = c_ref[at : at + BLOCK]
-        carried = dot(jnp.concatenate([c, c], 1), stacked(state, 2))
-        part = part_ref[at : at + BLOCK]
-        if j == 0:
-            part = part + added
-        y_ref[at : at + BLOCK] = (part + carried * grown).astype(BF16)
-        if j + 1 < blocks:
-            state = grown[BLOCK - 1 :] * state + s_ref[j]
-            if j == 0:
-                state = state + head
+        c = c_ref[at : at + BLOCK]
+        carried = dot(jnp.concatenate([c, c], 1), later)
+        y_ref[at : at + BLOCK] = (part_ref[at : at + BLOCK] + carried * grown_ref[at : at + BLOCK]).astype(BF16)
 
 
 def norm_body(y_ref, gate_ref, gain_ref, out_ref):
@@ -338,28 +364,24 @@
     tokens = rows * dests
     blocks = tokens // BLOCK
     mine = (lax.axis_index("inner") * head + lax.axis_index("head")).astype(jnp.int32).reshape(1)
-    share = dests * STATE // b_in.shape[1]
 
     def of(dtype, *shape):
         return jax.ShapeDtypeStruct(shape, dtype)
 
-    def bind(body):
-        def bound(*refs):
-            return body(share, *refs)
-
-        return bound
-
     total = (TILES + 2) * rows + OWN
+    lead = conv_x.shape[0]
     hbm = pl.BlockSpec(memory_space=pltpu.HBM)
-    [sent] = kernel(
-        pack_body, "pack", [IN_SMEM] + [hbm] * 4, [of(BF16, dests, total, LANES)],
+    operands = (x_in, b_in, c_in, dt_in, conv_x, input_state_taps, conv_c, dt_bias.reshape(1, -1), a_log.reshape(1, -1))
+    sent, own = kernel(
+        pack_body, "pack", [IN_SMEM] + [hbm] * len(operands),
+        [of(BF16, dests, total, LANES), of(F32, lead + 2 * OWN, WIDE + 2 * STATE)],
         [
             pltpu.VMEM(x_in.shape, BF16), pltpu.VMEM(b_in.shape, BF16), pltpu.VMEM(c_in.shape, BF16),
-            pltpu.VMEM(dt_in.shape, BF16), pltpu.VMEM((BLOCK, LANES), F32), pltpu.VMEM((dests, total, LANES), BF16),
-            pltpu.SemaphoreType.DMA((7,)), pltpu.SemaphoreType.DMA((4,)),
+            pltpu.VMEM(dt_in.shape, BF16), pltpu.VMEM((BLOCK, LANES), F32),
+            pltpu.VMEM((lead, WIDE), F32), pltpu.VMEM((2, lead, STATE), F32), pltpu.VMEM((2, 1, LANES), F32),
+            pltpu.SemaphoreType.DMA((7,)), pltpu.SemaphoreType.DMA((5,)),
         ],
-        out_specs=[hbm],
-    )(mine, x_in, b_in, c_in, dt_in)
+    )(mine, *(pltpu.with_memory_space_constraint(a, pltpu.HBM) for a in operands))
     got = lax.all_to_all(sent, ("inner", "head"), 0, 0, tiled=True)
     [gate] = kernel(
         gate_body, "gate", [IN_VMEM], [of(F32, *z_in.shape)],
@@ -371,17 +393,16 @@
         halo = shift(ends, "outer", 1).transpose(1, 0, 2).reshape(TOP, -1).astype(F32)
     else:
         halo = jnp.zeros((TOP, (TILES + 2) * LANES), F32)
-    taps = (conv_x, input_state_taps, conv_c)
-
-    extra = STATE + 2 * TOP
+
+    extra = STATE + TOP
     xb, dt, cum, fresh, send, fade = kernel(
-        bind(states_body), "states", [IN_SMEM] + [IN_VMEM] * 7,
+        states_body, "states", [IN_VMEM] * 3,
         [
             of(BF16, tokens, WIDE + STATE), of(F32, blocks, OWN, BLOCK), of(F32, blocks, OWN, BLOCK),
             of(F32, blocks, STATE, WIDE), of(BF16, extra, WIDE), of(F32, 8, WIDE),
         ],
         [pltpu.VMEM((TILES + 1, TOP + tokens, LANES), F32)],
-    )(mine, got, halo, *taps, dt_bias.reshape(1, -1), a_log.reshape(1, -1))
+    )(got, halo, own)
 
     before = shift(send, "outer", 1)
     if outer > 2:
@@ -392,21 +413,25 @@
             reach *= 2
         before = jnp.concatenate([entering.astype(BF16), before[STATE:]], 0)
 
-    c, part = kernel(
-        bind(intra_body), "intra", [IN_SMEM] + [IN_VMEM] * 8,
-        [of(BF16, tokens, STATE), of(F32, tokens, WIDE)],
+    wide = OWN * TOP
+    c, part, grown, factor, tail = kernel(
+        intra_body, "intra", [IN_VMEM] * 7,
+        [
+            of(BF16, tokens, STATE), of(F32, tokens, WIDE), of(F32, tokens, WIDE),
+            of(F32, 2, BLOCK, wide), of(F32, TOP, WIDE),
+        ],
         [pltpu.VMEM((TOP + tokens, LANES), F32), pltpu.VMEM((BLOCK, LANES), F32)],
         pl.CostEstimate(
             flops=2 * blocks * OWN * BLOCK * BLOCK * 160,
-            bytes_accessed=tokens * WIDE * 8,
+            bytes_accessed=tokens * WIDE * 12,
             transcendentals=blocks * OWN * BLOCK * BLOCK,
         ),
-    )(mine, got, halo, *taps, xb, dt, cum)
+    )(got, halo, own, xb, dt, cum, fresh)
 
     [y] = kernel(
-        bind(carry_body), "carry", [IN_SMEM] + [IN_VMEM] * 10, [of(BF16, tokens, WIDE)],
+        carry_body, "carry", [IN_VMEM] * 8, [of(BF16, tokens, WIDE)],
         [pltpu.VMEM((TILES + 2, 2 * TOP, LANES), F32), pltpu.VMEM((BLOCK, STATE), F32)],
-    )(mine, got, before, *taps, dt, cum, fresh, c, part)
+    )(got, before, own, c, part, grown, factor, tail)
 
     home = lax.all_to_all(y.reshape(dests, rows, WIDE), ("inner", "head"), 0, 0, tiled=True)
     [out] = kernel(

time: 55.2 us -> 49.4 us (0.89)
  local copies, waits for them, and re-layouts: 4.13 us -> 0.01 us
  Pallas kernels: 8.35 us -> 7.57 us
    unnamed x22 -> x4, local copies, waits for them, and re-layouts: 4.13 us -> 0.01 us
    pallas_call x4, Pallas kernels: 7.17 us -> 6.39 us  [the longest x1 2.21 us: shards(): kernel(states_body, 'states', [IN_VMEM] * 3, [of(BF16, tokens, WIDE + STA...]
  transfers between devices with their start and end apart: 2 -> 2, of which waited for: 2 -> 2; matrix products, arithmetic and copies ran while one was open for 0% -> 0% of each run, Pallas kernels for 2% -> 3%
where the time goes in v3:
time: 49.4 us; the launch traced here: 49.1 us
  blocking collectives  19.8 us (40%)
  waiting for transfers between devices  11.5 us (23%)
  starting transfers between devices  10.1 us (20%)
  Pallas kernels  7.57 us (15%)
    all_to_all x1, blocking collectives, shards(): got = lax.all_to_all(sent, ('inner', 'head'), 0, 0, tiled=True)  19.8 us
    all_to_all x1, waiting for transfers between devices, shards(): lax.all_to_all(y.reshape(dests, rows, WIDE), ('inner', 'head'), 0, 0, til...  10.4 us
    all_to_all x1, starting transfers between devices, shards(): lax.all_to_all(y.reshape(dests, rows, WIDE), ('inner', 'head'), 0, 0, til...  5.62 us
    ppermute x1, starting transfers between devices, shift(): lax.ppermute(block, axis, [(i, i + distance) for i in range(size - distan...  4.48 us
    pallas_call x1, Pallas kernels, shards(): kernel(states_body, 'states', [IN_VMEM] * 3, [of(BF16, tokens, WIDE + STA...  2.21 us
    pallas_call x1, Pallas kernels, shards(): kernel(pack_body, 'pack', [IN_SMEM] + [hbm] * len(operands), [of(BF16, de...  1.45 us
    pallas_call x1, Pallas kernels, shards(): kernel(intra_body, 'intra', [IN_VMEM] * 7, [of(BF16, tokens, STATE), of(F...  1.4 us
    pallas_call x1, Pallas kernels, shards(): kernel(carry_body, 'carry', [IN_VMEM] * 8, [of(BF16, tokens, WIDE)], [plt...  1.33 us
  transfers between devices with their start and end apart: 2, of which 2 were waited for; matrix products, arithmetic and copies ran while one was open for 0% of the time, Pallas kernels for 3%

profile of v3, /device:TPU:0, one launch (start us, length us, event | category | flops | bytes accessed | tf_op | source)
XLA Modules:
  0.0 49.1 jit_solution(6101344024935233498)
XLA Ops:
  0.0 1.5 %pack.1 = (bf16[16,200,128]{2,1,0:T(8,128)(2,1)S(1)}, f32[20,768]{1,0:T(8,128)S(1)}) custom-call(s32[1]{0:T(128)} %bitcast.mine_ref, bf16[32,8192]{1,0:T(8,128)(2,1)} %x_hbm.1, bf16[32,1024]{1,0:T(8,128)(2,1)} %b_hbm.1, bf16[32,1024]{1,0:T(8,128)(2,1)} %c_hbm.1, bf16[32,128]{1,0:T(8,128)(2,1)} %dt_hbm.1, f32[4,8192]{1,0:T(4,128)} %tap_x.1, f32[4,1024]{1,0:T(4,128)} %tap_b.1, ...), custom_call_target="tpu_custom_call" | custom-call | tf_op jit(solution)/shard_map/pack/pallas_call | solution.py:375
  1.5 19.8 %all_to_all.10.got_ref = bf16[16,200,128]{2,1,0:T(8,128)(2,1)S(1)} all-to-all(bf16[16,200,128]{2,1,0:T(8,128)(2,1)S(1)} %get-tuple-element.17), channel_id=1, replica_groups=mesh['outer'=2,'inner'=4,'head'=4] {'inner','head'}, dimensions={0} | all-to-all | bytes 1638400 | tf_op jit(solution)/shard_map/all_to_all | solution.py:385
  21.3 2.2 %states.1 = (bf16[512,640]{1,0:T(8,128)(2,1)S(1)}, f32[4,8,128]{2,1,0:T(8,128)S(1)}, f32[4,8,128]{2,1,0:T(8,128)S(1)}, f32[4,128,512]{2,1,0:T(8,128)S(1)}, bf16[...) custom-call(bf16[16,200,128]{2,1,0:T(8,128)(2,1)S(1)} %all_to_all.10.got_ref, f32[8,768]{1,0:T(8,128)S(1)} %broadcast_in_dim.3.halo_ref, ...), custom_call_target="tpu_custom_call" | custom-call | tf_op jit(solution)/shard_map/states/pallas_call | solution.py:398
  23.5 4.5 %collective-permute-start = (bf16[136,512]{1,0:T(8,128)(2,1)S(1)}, bf16[136,512]{1,0:T(8,128)(2,1)S(1)}, u32[]{:S(2)}, u32[]{:S(2)}) collective-permute-start(bf16[136,512]{1,0:T(8,128)(2,1)S(1)} %get-tuple-element.19), channel_id=1, source_target_pairs={{0,16},{1,17},{2,18},{3,19},{4,20},{5,21},{6,22},{7,23},{8,24},{9,... | collective-permute-start | bytes 417800 | tf_op jit(solution)/shard_map/ppermute | solution.py:344
  28.0 1.4 %intra.1 = (bf16[512,128]{1,0:T(8,128)(2,1)S(1)}, f32[512,512]{1,0:T(8,128)S(1)}, f32[512,512]{1,0:T(8,128)S(1)}, f32[2,128,64]{2,1,0:T(8,128)S(1)}, f32[8,512]{1,0:T(8,128)S(1)}) custom-call(bf16[16,200,128]{2,1,0:T(8,128)(2,1)S(1)} %all_to_all.10.got_ref, f32[8,768]{1,0:T(8,128)S(1)} %broadcast_in_dim.3.halo_ref, f32[20,768]{1,0:T(8,128)S(1)} %get-tuple-element.18.own_ref, ...), custom_call_target="tpu_custom_call" | custom-call | flops 167772160 | bytes 3145728 | tf_op jit(solution)/shard_map/intra/pallas_call | solution.py:417
  29.4 1.2 %collective-permute-done.before_ref = bf16[136,512]{1,0:T(8,128)(2,1)S(1)} collective-permute-done((bf16[136,512]{1,0:T(8,128)(2,1)S(1)}, bf16[136,512]{1,0:T(8,128)(2,1)S(1)}, u32[]{:S(2)}, u32[]{:S(2)}) %collective-permute-start) | collective-permute-done | bytes 139296 | tf_op jit(solution)/shard_map/ppermute | solution.py:344
  30.5 1.3 %carry.1 = bf16[512,512]{1,0:T(8,128)(2,1)} custom-call(bf16[16,200,128]{2,1,0:T(8,128)(2,1)S(1)} %all_to_all.10.got_ref, bf16[136,512]{1,0:T(8,128)(2,1)S(1)} %collective-permute-done.before_ref, f32[20,768]{1,0:T(8,128)S(1)} %get-tuple-element.18.own_ref, bf16[512,128]{1,0:T(8,128)(2,1)S(1)} %get-tuple-element.24.c_ref, ...), custom_call_target="tpu_custom_call" | custom-call | tf_op jit(solution)/shard_map/carry/pallas_call | solution.py:431
  31.9 0.0 copy-start
  31.9 5.6 %all-to-all-start.1 = ((bf16[16,32,512]{2,1,0:T(8,128)(2,1)}), bf16[16,32,512]{2,1,0:T(8,128)(2,1)S(1)}, u32[]{:S(2)}, u32[]{:S(2)}) async-start(bf16[16,32,512]{2,1,0:T(8,128)(2,1)} %bitcast.3), calls=%async_computation.1 | async-start | bytes 1048576 | tf_op jit(solution)/shard_map/all_to_all | solution.py:436
  37.5 0.0 copy-done
  37.5 0.0 copy-start.1
  37.5 0.1 gate.1.gate_ref
  37.7 10.4 %all-to-all-done.1.y_ref = bf16[16,32,512]{2,1,0:T(8,128)(2,1)S(1)} async-done(((bf16[16,32,512]{2,1,0:T(8,128)(2,1)}), bf16[16,32,512]{2,1,0:T(8,128)(2,1)S(1)}, u32[]{:S(2)}, u32[]{:S(2)}) %all-to-all-start.1) | async-done | bytes 524320 | tf_op jit(solution)/shard_map/all_to_all | solution.py:436
  48.0 0.0 copy-done.1
  48.0 1.0 %norm.1 = bf16[32,8192]{1,0:T(8,128)(2,1)} custom-call(bf16[16,32,512]{2,1,0:T(8,128)(2,1)S(1)} %all-to-all-done.1.y_ref, f32[32,8192]{1,0:T(8,128)S(1)} %gate.1.gate_ref, f32[1,8192]{1,0:T(1,128)S(1)} %bitcast.5), custom_call_target="tpu_custom_call" | custom-call | tf_op jit(solution)/shard_map/norm/pallas_call | solution.py:437
  (1 shorter events, 0.0 us)
Async XLA Ops:
  23.5 7.1 %collective-permute-start = (bf16[136,512]{1,0:T(8,128)(2,1)S(1)}, bf16[136,512]{1,0:T(8,128)(2,1)S(1)}, u32[]{:S(2)}, u32[]{:S(2)}) collective-permute-start(bf16[136,512]{1,0:T(8,128)(2,1)S(1)} %get-tuple-element.19), channel_id=1, source_target_pairs={{0,16},{1,17},{2,18},{3,19},{4,20},{5,21},{6,22},{7,23},{8,24},{9,... | collective-permute-start | bytes 417800 | tf_op jit(solution)/shard_map/ppermute | solution.py:344
  31.9 5.6 %copy-start = (bf16[32,8192]{1,0:T(8,128)(2,1)S(1)}, bf16[32,8192]{1,0:T(8,128)(2,1)}, u32[]{:S(2)}) copy-start(bf16[32,8192]{1,0:T(8,128)(2,1)} %z_ref.1) | copy-start | bytes 1572868
  31.9 16.2 %all-to-all-start.1 = ((bf16[16,32,512]{2,1,0:T(8,128)(2,1)}), bf16[16,32,512]{2,1,0:T(8,128)(2,1)S(1)}, u32[]{:S(2)}, u32[]{:S(2)}) async-start(bf16[16,32,512]{2,1,0:T(8,128)(2,1)} %bitcast.3), calls=%async_computation.1 | async-start | bytes 1048576 | tf_op jit(solution)/shard_map/all_to_all | solution.py:436
  37.5 10.5 %copy-start.1 = (f32[8192]{0:T(1024)S(1)}, f32[8192]{0:T(1024)}, u32[]{:S(2)}) copy-start(f32[8192]{0:T(1024)} %param.21) | copy-start | bytes 98308

commit v4 on v3

--- a/solution.py
+++ b/solution.py
@@ -147,143 +147,142 @@
         out_ref[:, lo : lo + WIDE] = silu(z_ref[:, lo : lo + WIDE].astype(F32))
 
 
-def states_body(
-    got_ref, halo_ref, own_ref, xb_ref, dt_ref, cum_ref, s_ref, send_ref, fade_ref, win,
-):
+def sizes_of(got_ref):
     sources, total, _ = got_ref.shape
     rows = (total - OWN) // (TILES + 2)
-    blocks = sources * rows // BLOCK
+    return sources, rows, sources * rows // BLOCK
+
+
+def fill(win, got_ref, halo_ref, tiles):
+    sources, rows, _ = sizes_of(got_ref)
+    for q in range(tiles):
+        win[q, :TOP] = halo_ref[:, q * LANES : (q + 1) * LANES]
+        for s in range(sources):
+            at = TOP + s * rows
+            win[q, at : at + rows] = got_ref[s, q * rows : (q + 1) * rows, :].astype(F32)
+
+
+def conv_tile(win, taps, j, q):
+    first = j * BLOCK + TOP - taps[q].shape[0] + 1
+    return conv(lambda k: win[q, first + k : first + k + BLOCK], taps[q]).astype(BF16)
+
+
+def steps_of(got_ref, own_ref):
+    _, rows, blocks = sizes_of(got_ref)
     per = BLOCK // rows
-
     lead = lead_of(own_ref)
-    bias = own_ref[lead : lead + OWN, :LANES]
-    rate = -jnp.exp(own_ref[lead + OWN :, :LANES])
-    upto = (iota((BLOCK, BLOCK), 0) <= iota((BLOCK, BLOCK), 1)).astype(F32).astype(BF16)
+    raws = []
     for j in range(blocks):
         raw = got_ref[j * per, (TILES + 2) * rows :, :].astype(F32)
         for s in range(1, per):
             raw = raw + got_ref[j * per + s, (TILES + 2) * rows :, :].astype(F32)
-        raw = raw + bias
-        dt = jnp.maximum(raw, 0.0) + jnp.log1p(jnp.exp(-jnp.abs(raw)))
-        sums = dot(stacked(dt * rate, 4), upto)
-        cum = sums[:OWN] + sums[OWN : 2 * OWN] + sums[2 * OWN : 3 * OWN]
-        dt_ref[j] = dt
-        cum_ref[j] = cum
-
+        raws.append(raw + own_ref[lead : lead + OWN, :LANES])
+    raw = jnp.concatenate(raws, 0)
+    dt = jnp.maximum(raw, 0.0) + jnp.log1p(jnp.exp(-jnp.abs(raw)))
+    rate = jnp.concatenate([-jnp.exp(own_ref[lead + OWN :, :LANES])] * blocks, 0)
+    upto = (iota((BLOCK, BLOCK), 0) <= iota((BLOCK, BLOCK), 1)).astype(F32).astype(BF16)
+    sums = dot(stacked(dt * rate, 4), upto)
+    n = blocks * OWN
+    cum = sums[:n] + sums[n : 2 * n] + sums[2 * n : 3 * n] + sums[3 * n :]
+    return [[v[j * OWN : (j + 1) * OWN] for j in range(blocks)] for v in (dt, cum)]
+
+
+def total_body(sends_ref, got_ref, halo_ref, own_ref, send_ref, fade_ref, win):
+    @pl.when(sends_ref[0] != 0)
+    def _():
+        sources, rows, blocks = sizes_of(got_ref)
+        dts, cums = steps_of(got_ref, own_ref)
+        taps = tiles_of(own_ref)
+        fill(win, got_ref, halo_ref, TILES + 1)
+        state = jnp.zeros((STATE, WIDE), F32)
+        after = jnp.zeros((OWN, 1), F32)
+        for j in reversed(range(blocks)):
+            after = after + cums[j][:, BLOCK - 1 :]
+            tail = expand(jnp.exp(after - cums[j]) * dts[j])
+            x = jnp.concatenate([conv_tile(win, taps, j, q) for q in range(TILES)], 1)
+            b = conv_tile(win, taps, j, TILES)
+            state = state + dot_t(jnp.concatenate([b, b], 0), stacked(x.astype(F32) * tail, 2))
+        fade_ref[...] = expand(jnp.broadcast_to(jnp.exp(after), (OWN, LANES)))[:8]
+        send_ref[:STATE] = state.astype(BF16)
+        ends = [got_ref[sources - 1, q * rows : (q + 1) * rows, :].astype(F32)[rows - TOP :] for q in range(TILES + 2)]
+        ends += [jnp.zeros_like(ends[0])] * (TILES - 2)
+        half = TOP // 2
+        upper = pltpu.roll(jnp.concatenate(ends[:TILES], 1), half, 0)
+        keep = iota((TOP, WIDE), 0) < half
+        send_ref[STATE:] = jnp.where(keep, upper, jnp.concatenate(ends[TILES:], 1)).astype(BF16)
+
+
+def local_body(
+    got_ref, halo_ref, own_ref, order_ref, c_ref, part_ref, grown_ref, factor_ref, tail_ref, win, turn,
+):
+    _, _, blocks = sizes_of(got_ref)
+    dts, cums = steps_of(got_ref, own_ref)
     taps = tiles_of(own_ref)
-    first = TOP - lead + 1
-    for q in range(TILES + 1):
-        win[q, :TOP] = halo_ref[:, q * LANES : (q + 1) * LANES]
-        for s in range(sources):
-            at = TOP + s * rows
-            win[q, at : at + rows] = got_ref[s, q * rows : (q + 1) * rows, :].astype(F32)
-    state = None
-    for j in range(blocks):
-        at = j * BLOCK
-        for q in range(TILES + 1):
-            done = conv(lambda k: win[q, at + first + k : at + first + k + BLOCK], taps[q])
-            xb_ref[at : at + BLOCK, q * LANES : (q + 1) * LANES] = done.astype(BF16)
-        cum = cum_ref[j]
-        last = cum[:, BLOCK - 1 :]
-        tail = expand(jnp.exp(last - cum) * dt_ref[j])
-        fade = expand(jnp.broadcast_to(jnp.exp(last), (OWN, LANES)))[:1]
-        b = xb_ref[at : at + BLOCK, WIDE:]
-        weighted = xb_ref[at : at + BLOCK, :WIDE].astype(F32) * tail
-        twice = jnp.concatenate([b, b], 0)
-        if j == 0:
-            top = iota((BLOCK, WIDE), 0) < TOP
-            head = dot_t(twice, stacked(jnp.where(top, weighted, 0.0), 2))
-            weighted = jnp.where(top, 0.0, weighted)
-        fresh = dot_t(twice, stacked(weighted, 2))
-        s_ref[j] = fresh
-        state = fresh + head if j == 0 else fade * state + fresh
-        whole = fade if j == 0 else whole * fade
-    send_ref[:STATE] = state.astype(BF16)
-    ends = [got_ref[sources - 1, q * rows : (q + 1) * rows, :].astype(F32)[rows - TOP :] for q in range(TILES + 2)]
-    ends += [jnp.zeros_like(ends[0])] * (TILES - 2)
-    half = TOP // 2
-    upper = pltpu.roll(jnp.concatenate(ends[:TILES], 1), half, 0)
-    keep = iota((TOP, WIDE), 0) < half
-    send_ref[STATE:] = jnp.where(keep, upper, jnp.concatenate(ends[TILES:], 1)).astype(BF16)
-    fade_ref[...] = jnp.broadcast_to(whole, (8, WIDE))
-
-
-def intra_body(
-    got_ref, halo_ref, own_ref, xb_ref, dt_ref, cum_ref, s_ref,
-    c_ref, part_ref, grown_ref, factor_ref, tail_ref, win, turn,
-):
-    sources, total, _ = got_ref.shape
-    rows = (total - OWN) // (TILES + 2)
-    blocks = sources * rows // BLOCK
-    tap = tiles_of(own_ref)[-1]
-    first = TOP - tap.shape[0] + 1
-    q = TILES + 1
-    win[:TOP] = halo_ref[:, q * LANES : (q + 1) * LANES]
-    for s in range(sources):
-        at = TOP + s * rows
-        win[at : at + rows] = got_ref[s, q * rows : (q + 1) * rows, :].astype(F32)
+    fill(win, got_ref, halo_ref, TILES + 2)
     turn[...] = jnp.zeros_like(turn)
     for j in range(blocks):
-        turn[j * OWN : (j + 1) * OWN] = cum_ref[j]
+        turn[j * OWN : (j + 1) * OWN] = cums[j]
     cols = turn[...].T
     t_at = iota((BLOCK, BLOCK), 0)
     s_at = iota((BLOCK, BLOCK), 1)
     left = iota((BLOCK, LANES), 1) < HEAD_DIM
     zero = jnp.zeros((BLOCK, LANES), BF16)
     past = jnp.zeros((OWN, 1), F32)
+    local = None
     for j in range(blocks):
         at = j * BLOCK
-        c = conv(lambda k: win[at + first + k : at + first + k + BLOCK], tap).astype(BF16)
+        x = [conv_tile(win, taps, j, q) for q in range(TILES)]
+        b = conv_tile(win, taps, j, TILES)
+        c = conv_tile(win, taps, j, TILES + 1)
         c_ref[at : at + BLOCK] = c
-        b = xb_ref[at : at + BLOCK, WIDE:]
         scores = lax.dot_general(c, b, (((1,), (1,)), ((), ())), preferred_element_type=F32)
         keep = t_at >= s_at
         if j == 0:
             keep = keep & (s_at >= TOP)
         scores = jnp.where(keep, scores, 0.0)
-        cum = cum_ref[j]
-        dt = dt_ref[j]
+        cum, dt = cums[j], dts[j]
+        last = cum[:, BLOCK - 1 :]
         grown = expand(jnp.exp(cum))
         if j < 2:
             grown_ref[at : at + BLOCK] = grown
         else:
-            past = past + cum_ref[j - 1][:, BLOCK - 1 :]
+            past = past + cums[j - 1][:, BLOCK - 1 :]
             grown_ref[at : at + BLOCK] = expand(jnp.exp(cum + past))
         if j > 0:
-            local = s_ref[0] if j == 1 else fade * local + s_ref[j - 1]
             carried = dot(jnp.concatenate([c, c], 1), stacked(local, 2)) * grown
-        fade = grown[BLOCK - 1 :]
         for q in range(TILES):
             lo = q * LANES
-            x = xb_ref[at : at + BLOCK, lo : lo + LANES]
             mixes = []
             for h in (2 * q, 2 * q + 1):
                 col = j * OWN + h
                 gap = jnp.minimum(cols[:, col : col + 1] - cum[h : h + 1], 0.0)
                 mixes.append((scores * jnp.exp(gap) * dt[h : h + 1]).astype(BF16))
-            both = jnp.concatenate([jnp.where(left, x, zero), jnp.where(left, zero, x)], 0)
+            both = jnp.concatenate([jnp.where(left, x[q], zero), jnp.where(left, zero, x[q])], 0)
             part = dot(jnp.concatenate(mixes, 1), both)
             part_ref[at : at + BLOCK, lo : lo + LANES] = part if j == 0 else part + carried[:, lo : lo + LANES]
-
-    cum = cum_ref[0]
-    dt = dt_ref[0]
+        tail = expand(jnp.exp(last - cum) * dt)
+        if j == 0:
+            tail_ref[...] = tail[:TOP]
+            tail = jnp.where(iota((BLOCK, WIDE), 0) < TOP, 0.0, tail)
+        if j + 1 < blocks:
+            weighted = stacked(jnp.concatenate(x, 1).astype(F32) * tail, 2)
+            fresh = dot_t(jnp.concatenate([b, b], 0), weighted)
+            local = fresh if j == 0 else grown[BLOCK - 1 :] * local + fresh
+
     wide = OWN * TOP
     spread = one_hot(4 * OWN, TOP)
-    cum_t = dot_t(stacked(cum, 4), spread)
+    cum_t = dot_t(stacked(cums[0], 4), spread)
     same = iota((TOP, wide), 0) == iota((TOP, wide), 1) % TOP
     cum_s = jnp.sum(jnp.where(same, cum_t[:TOP], 0.0), axis=0, keepdims=True)
-    dt_s = jnp.sum(jnp.where(same, dot_t(stacked(dt, 4), spread)[:TOP], 0.0), axis=0, keepdims=True)
+    dt_s = jnp.sum(jnp.where(same, dot_t(stacked(dts[0], 4), spread)[:TOP], 0.0), axis=0, keepdims=True)
     decay = jnp.exp(jnp.minimum(cum_t - cum_s, 0.0))
     seen = iota((BLOCK, wide), 0) >= iota((BLOCK, wide), 1) % TOP
     factor_ref[0] = jnp.where(seen, decay, 0.0)
     factor_ref[1] = jnp.broadcast_to(dt_s, (BLOCK, wide))
-    tail_ref[...] = expand(jnp.exp(cum[:, BLOCK - 1 :] - cum) * dt)[:TOP]
 
 
 def carry_body(got_ref, before_ref, own_ref, c_ref, part_ref, grown_ref, factor_ref, tail_ref, y_ref, win, c_first):
-    sources, total, _ = got_ref.shape
-    rows = (total - OWN) // (TILES + 2)
-    blocks = sources * rows // BLOCK
+    _, rows, blocks = sizes_of(got_ref)
     taps = tiles_of(own_ref)
     first = TOP - taps[0].shape[0] + 1
 
@@ -322,9 +321,10 @@
         y_ref[at : at + BLOCK] = (part_ref[at : at + BLOCK] + carried * grown_ref[at : at + BLOCK]).astype(BF16)
 
 
-def norm_body(y_ref, gate_ref, gain_ref, out_ref):
+def norm_body(y_ref, gate_ref, gain_ref, out_hbm, out_v, sem):
     count = y_ref.shape[0]
     per = count // GROUPS
+    copies = []
     for g in range(GROUPS):
         gated = []
         square = 0.0
@@ -336,7 +336,12 @@
         for k in range(g * per, (g + 1) * per):
             at = k * WIDE
             gain = gain_ref[:, at : at + WIDE]
-            out_ref[:, at : at + WIDE] = (gated[k - g * per] * scale * gain).astype(BF16)
+            out_v[:, at : at + WIDE] = (gated[k - g * per] * scale * gain).astype(BF16)
+        part = pl.ds(g * per * WIDE, per * WIDE)
+        copies.append(pltpu.make_async_copy(out_v.at[:, part], out_hbm.at[:, part], sem.at[g]))
+        copies[-1].start()
+    for copy in copies:
+        copy.wait()
 
 
 def shift(block, axis, distance):
@@ -395,14 +400,12 @@
         halo = jnp.zeros((TOP, (TILES + 2) * LANES), F32)
 
     extra = STATE + TOP
-    xb, dt, cum, fresh, send, fade = kernel(
-        states_body, "states", [IN_VMEM] * 3,
-        [
-            of(BF16, tokens, WIDE + STATE), of(F32, blocks, OWN, BLOCK), of(F32, blocks, OWN, BLOCK),
-            of(F32, blocks, STATE, WIDE), of(BF16, extra, WIDE), of(F32, 8, WIDE),
-        ],
+    sends = (lax.axis_index("outer") < outer - 1).astype(jnp.int32).reshape(1)
+    send, fade = kernel(
+        total_body, "total", [IN_SMEM] + [IN_VMEM] * 3,
+        [of(BF16, extra, WIDE), of(F32, 8, WIDE)],
         [pltpu.VMEM((TILES + 1, TOP + tokens, LANES), F32)],
-    )(got, halo, own)
+    )(sends, got, halo, own)
 
     before = shift(send, "outer", 1)
     if outer > 2:
@@ -415,18 +418,18 @@
 
     wide = OWN * TOP
     c, part, grown, factor, tail = kernel(
-        intra_body, "intra", [IN_VMEM] * 7,
+        local_body, "local", [IN_VMEM] * 4,
         [
             of(BF16, tokens, STATE), of(F32, tokens, WIDE), of(F32, tokens, WIDE),
             of(F32, 2, BLOCK, wide), of(F32, TOP, WIDE),
         ],
-        [pltpu.VMEM((TOP + tokens, LANES), F32), pltpu.VMEM((BLOCK, LANES), F32)],
+        [pltpu.VMEM((TILES + 2, TOP + tokens, LANES), F32), pltpu.VMEM((BLOCK, LANES), F32)],
         pl.CostEstimate(
             flops=2 * blocks * OWN * BLOCK * BLOCK * 160,
             bytes_accessed=tokens * WIDE * 12,
             transcendentals=blocks * OWN * BLOCK * BLOCK,
         ),
-    )(got, halo, own, xb, dt, cum, fresh)
+    )(got, halo, own, fade)
 
     [y] = kernel(
         carry_body, "carry", [IN_VMEM] * 8, [of(BF16, tokens, WIDE)],
@@ -436,6 +439,7 @@
     home = lax.all_to_all(y.reshape(dests, rows, WIDE), ("inner", "head"), 0, 0, tiled=True)
     [out] = kernel(
         norm_body, "norm", [IN_VMEM] * 3, [of(BF16, rows, dests * WIDE)],
+        [pltpu.VMEM((rows, dests * WIDE), BF16), pltpu.SemaphoreType.DMA((GROUPS,))], out_specs=[hbm],
     )(home, gate, norm_gain.reshape(1, -1))
     return out
 

time: 49.4 us -> 48.7 us (0.986)
  blocking collectives: 19.8 us -> 0 us
  waiting for transfers between devices: 11.5 us -> 24.2 us
  starting transfers between devices: 10.1 us -> 15.2 us
  Pallas kernels: 7.57 us -> 8.81 us
    all_to_all x1 -> x0, blocking collectives: 19.8 us -> none  [shards(): got = lax.all_to_all(sent, ('inner', 'head'), 0, 0, tiled=True)]
    all_to_all x0 -> x1, waiting for transfers between devices: none -> 13.7 us  [shards(): got = lax.all_to_all(sent, ('inner', 'head'), 0, 0, tiled=True)]
    all_to_all x0 -> x1, starting transfers between devices: none -> 6.3 us  [shards(): got = lax.all_to_all(sent, ('inner', 'head'), 0, 0, tiled=True)]
    ppermute x1, starting transfers between devices: 4.48 us -> 3.02 us  [shift(): lax.ppermute(block, axis, [(i, i + distance) for i in range(size - distan...]
    ppermute x1, waiting for transfers between devices: 1.16 us -> 0.15 us  [shift(): lax.ppermute(block, axis, [(i, i + distance) for i in range(size - distan...]
    pallas_call x1, Pallas kernels: 1.45 us -> 2.27 us  [shards(): kernel(pack_body, 'pack', [IN_SMEM] + [hbm] * len(operands), [of(BF16, de...]
  transfers between devices with their start and end apart: 2 -> 3, of which waited for: 2 -> 3; matrix products, arithmetic and copies ran while one was open for 0% -> 0% of each run, Pallas kernels for 3% -> 6%
where the time goes in v4:
time: 48.7 us; the launch traced here: 48.4 us
  waiting for transfers between devices  24.2 us (50%)
  starting transfers between devices  15.2 us (31%)
  Pallas kernels  8.81 us (18%)
    all_to_all x1, waiting for transfers between devices, shards(): got = lax.all_to_all(sent, ('inner', 'head'), 0, 0, tiled=True)  13.7 us
    all_to_all x1, waiting for transfers between devices, shards(): lax.all_to_all(y.reshape(dests, rows, WIDE), ('inner', 'head'), 0, 0, til...  10.4 us
    all_to_all x1, starting transfers between devices, shards(): got = lax.all_to_all(sent, ('inner', 'head'), 0, 0, tiled=True)  6.3 us
    all_to_all x1, starting transfers between devices, shards(): lax.all_to_all(y.reshape(dests, rows, WIDE), ('inner', 'head'), 0, 0, til...  5.9 us
    ppermute x1, starting transfers between devices, shift(): lax.ppermute(block, axis, [(i, i + distance) for i in range(size - distan...  3.02 us
    pallas_call x1, Pallas kernels, shards(): kernel(local_body, 'local', [IN_VMEM] * 4, [of(BF16, tokens, STATE), of(F...  2.59 us
    pallas_call x1, Pallas kernels, shards(): kernel(pack_body, 'pack', [IN_SMEM] + [hbm] * len(operands), [of(BF16, de...  2.27 us
    pallas_call x1, Pallas kernels, shards(): kernel(total_body, 'total', [IN_SMEM] + [IN_VMEM] * 3, [of(BF16, extra, W...  1.46 us
  transfers between devices with their start and end apart: 3, of which 3 were waited for; matrix products, arithmetic and copies ran while one was open for 0% of the time, Pallas kernels for 6%

profile of v4, /device:TPU:0, one launch (start us, length us, event | category | flops | bytes accessed | tf_op | source)
XLA Modules:
  0.0 48.4 jit_solution(7275638869866427771)
XLA Ops:
  0.0 2.3 %pack.1 = (bf16[16,200,128]{2,1,0:T(8,128)(2,1)}, f32[20,768]{1,0:T(8,128)S(1)}) custom-call(s32[1]{0:T(128)} %bitcast.mine_ref, bf16[32,8192]{1,0:T(8,128)(2,1)} %x_hbm.1, bf16[32,1024]{1,0:T(8,128)(2,1)} %b_hbm.1, bf16[32,1024]{1,0:T(8,128)(2,1)} %c_hbm.1, bf16[32,128]{1,0:T(8,128)(2,1)} %dt_hbm.1, f32[4,8192]{1,0:T(4,128)} %tap_x.1, f32[4,1024]{1,0:T(4,128)} %tap_b.1, ...), custom_call_target="tpu_custom_call" | custom-call | tf_op jit(solution)/shard_map/pack/pallas_call | solution.py:380
  2.3 6.3 %all-to-all-start = ((bf16[16,200,128]{2,1,0:T(8,128)(2,1)}), bf16[16,200,128]{2,1,0:T(8,128)(2,1)S(1)}, u32[]{:S(2)}, u32[]{:S(2)}) async-start(bf16[16,200,128]{2,1,0:T(8,128)(2,1)} %get-tuple-element.14), calls=%async_computation | async-start | bytes 1638400 | tf_op jit(solution)/shard_map/all_to_all | solution.py:390
  8.6 13.7 %all-to-all-done.got_ref = bf16[16,200,128]{2,1,0:T(8,128)(2,1)S(1)} async-done(((bf16[16,200,128]{2,1,0:T(8,128)(2,1)}), bf16[16,200,128]{2,1,0:T(8,128)(2,1)S(1)}, u32[]{:S(2)}, u32[]{:S(2)}) %all-to-all-start) | async-done | bytes 819232 | tf_op jit(solution)/shard_map/all_to_all | solution.py:390
  22.3 1.5 %total.1 = (bf16[136,512]{1,0:T(8,128)(2,1)S(1)}, f32[8,512]{1,0:T(8,128)S(1)}) custom-call(s32[1]{0:T(128)} %bitcast.3.sends_ref, bf16[16,200,128]{2,1,0:T(8,128)(2,1)S(1)} %all-to-all-done.got_ref, f32[8,768]{1,0:T(8,128)S(1)} %broadcast_in_dim.3.halo_ref, f32[20,768]{1,0:T(8,128)S(1)} %get-tuple-element.15.own_ref), custom_call_target="tpu_custom_call" | custom-call | tf_op jit(solution)/shard_map/total/pallas_call | solution.py:404
  23.8 3.0 %collective-permute-start = (bf16[136,512]{1,0:T(8,128)(2,1)S(1)}, bf16[136,512]{1,0:T(8,128)(2,1)S(1)}, u32[]{:S(2)}, u32[]{:S(2)}) collective-permute-start(bf16[136,512]{1,0:T(8,128)(2,1)S(1)} %get-tuple-element.16), channel_id=1, source_target_pairs={{0,16},{1,17},{2,18},{3,19},{4,20},{5,21},{6,22},{7,23},{8,24},{9,... | collective-permute-start | bytes 417800 | tf_op jit(solution)/shard_map/ppermute | solution.py:349
  26.8 2.6 %local.1 = (bf16[512,128]{1,0:T(8,128)(2,1)S(1)}, f32[512,512]{1,0:T(8,128)S(1)}, f32[512,512]{1,0:T(8,128)S(1)}, f32[2,128,64]{2,1,0:T(8,128)S(1)}, f32[8,512]{1,0:T(8,128)S(1)}) custom-call(bf16[16,200,128]{2,1,0:T(8,128)(2,1)S(1)} %all-to-all-done.got_ref, f32[8,768]{1,0:T(8,128)S(1)} %broadcast_in_dim.3.halo_ref, ...), custom_call_target="tpu_custom_call" | custom-call | flops 167772160 | bytes 3145728 | tf_op jit(solution)/shard_map/local/pallas_call | solution.py:420
  29.4 0.2 collective-permute-done.before_ref
  29.6 1.3 %carry.1 = bf16[512,512]{1,0:T(8,128)(2,1)} custom-call(bf16[16,200,128]{2,1,0:T(8,128)(2,1)S(1)} %all-to-all-done.got_ref, bf16[136,512]{1,0:T(8,128)(2,1)S(1)} %collective-permute-done.before_ref, f32[20,768]{1,0:T(8,128)S(1)} %get-tuple-element.15.own_ref, bf16[512,128]{1,0:T(8,128)(2,1)S(1)} %get-tuple-element.18.c_ref, ...), custom_call_target="tpu_custom_call" | custom-call | tf_op jit(solution)/shard_map/carry/pallas_call | solution.py:434
  30.9 0.0 copy-start
  30.9 5.9 %all-to-all-start.1 = ((bf16[16,32,512]{2,1,0:T(8,128)(2,1)}), bf16[16,32,512]{2,1,0:T(8,128)(2,1)S(1)}, u32[]{:S(2)}, u32[]{:S(2)}) async-start(bf16[16,32,512]{2,1,0:T(8,128)(2,1)} %bitcast.4), calls=%async_computation.1 | async-start | bytes 1048576 | tf_op jit(solution)/shard_map/all_to_all | solution.py:439
  36.8 0.0 copy-done
  36.8 0.0 copy-start.1
  36.8 0.1 gate.1.gate_ref
  37.0 10.4 %all-to-all-done.1.y_ref = bf16[16,32,512]{2,1,0:T(8,128)(2,1)S(1)} async-done(((bf16[16,32,512]{2,1,0:T(8,128)(2,1)}), bf16[16,32,512]{2,1,0:T(8,128)(2,1)S(1)}, u32[]{:S(2)}, u32[]{:S(2)}) %all-to-all-start.1) | async-done | bytes 524320 | tf_op jit(solution)/shard_map/all_to_all | solution.py:439
  47.3 0.0 copy-done.1
  47.3 1.0 %norm.1 = bf16[32,8192]{1,0:T(8,128)(2,1)} custom-call(bf16[16,32,512]{2,1,0:T(8,128)(2,1)S(1)} %all-to-all-done.1.y_ref, f32[32,8192]{1,0:T(8,128)S(1)} %gate.1.gate_ref, f32[1,8192]{1,0:T(1,128)S(1)} %bitcast.6), custom_call_target="tpu_custom_call" | custom-call | tf_op jit(solution)/shard_map/norm/pallas_call | solution.py:440
  (1 shorter events, 0.0 us)
Async XLA Ops:
  2.3 20.0 %all-to-all-start = ((bf16[16,200,128]{2,1,0:T(8,128)(2,1)}), bf16[16,200,128]{2,1,0:T(8,128)(2,1)S(1)}, u32[]{:S(2)}, u32[]{:S(2)}) async-start(bf16[16,200,128]{2,1,0:T(8,128)(2,1)} %get-tuple-element.14), calls=%async_computation | async-start | bytes 1638400 | tf_op jit(solution)/shard_map/all_to_all | solution.py:390
  23.8 5.8 %collective-permute-start = (bf16[136,512]{1,0:T(8,128)(2,1)S(1)}, bf16[136,512]{1,0:T(8,128)(2,1)S(1)}, u32[]{:S(2)}, u32[]{:S(2)}) collective-permute-start(bf16[136,512]{1,0:T(8,128)(2,1)S(1)} %get-tuple-element.16), channel_id=1, source_target_pairs={{0,16},{1,17},{2,18},{3,19},{4,20},{5,21},{6,22},{7,23},{8,24},{9,... | collective-permute-start | bytes 417800 | tf_op jit(solution)/shard_map/ppermute | solution.py:349
  30.9 5.9 %copy-start = (bf16[32,8192]{1,0:T(8,128)(2,1)S(1)}, bf16[32,8192]{1,0:T(8,128)(2,1)}, u32[]{:S(2)}) copy-start(bf16[32,8192]{1,0:T(8,128)(2,1)} %z_ref.1) | copy-start | bytes 1572868
  30.9 16.5 %all-to-all-start.1 = ((bf16[16,32,512]{2,1,0:T(8,128)(2,1)}), bf16[16,32,512]{2,1,0:T(8,128)(2,1)S(1)}, u32[]{:S(2)}, u32[]{:S(2)}) async-start(bf16[16,32,512]{2,1,0:T(8,128)(2,1)} %bitcast.4), calls=%async_computation.1 | async-start | bytes 1048576 | tf_op jit(solution)/shard_map/all_to_all | solution.py:439
  36.8 10.5 %copy-start.1 = (f32[8192]{0:T(1024)S(1)}, f32[8192]{0:T(1024)}, u32[]{:S(2)}) copy-start(f32[8192]{0:T(1024)} %param.21) | copy-start | bytes 98308

commit v5 on v4

--- a/solution.py
+++ b/solution.py
@@ -78,10 +78,10 @@
 
 
 def pack_body(
-    mine_ref, x_hbm, b_hbm, c_hbm, dt_hbm, tap_x, tap_b, tap_c, bias_hbm, log_hbm,
+    place_ref, x_hbm, b_hbm, c_hbm, dt_hbm, tap_x, tap_b, tap_c, bias_hbm, log_hbm,
     out_v, own_ref, x_v, b_v, c_v, dt_v, turn, x_tap, s_taps, heads_v, sem_in, sem_own,
 ):
-    mine = mine_ref[0]
+    mine = place_ref[0] // 2
     count = out_v.shape[0]
     rows = x_v.shape[0]
     share = count * STATE // b_v.shape[1]
@@ -142,11 +142,6 @@
         own_ref[at : at + OWN, :LANES] = jnp.broadcast_to(column, (OWN, LANES))
 
 
-def gate_body(z_ref, out_ref):
-    for lo in range(0, z_ref.shape[1], WIDE):
-        out_ref[:, lo : lo + WIDE] = silu(z_ref[:, lo : lo + WIDE].astype(F32))
-
-
 def sizes_of(got_ref):
     sources, total, _ = got_ref.shape
     rows = (total - OWN) // (TILES + 2)
@@ -187,8 +182,8 @@
     return [[v[j * OWN : (j + 1) * OWN] for j in range(blocks)] for v in (dt, cum)]
 
 
-def total_body(sends_ref, got_ref, halo_ref, own_ref, send_ref, fade_ref, win):
-    @pl.when(sends_ref[0] != 0)
+def total_body(place_ref, got_ref, halo_ref, own_ref, send_ref, fade_ref, win):
+    @pl.when(lax.rem(place_ref[0], 2) != 0)
     def _():
         sources, rows, blocks = sizes_of(got_ref)
         dts, cums = steps_of(got_ref, own_ref)
@@ -213,8 +208,11 @@
 
 
 def local_body(
-    got_ref, halo_ref, own_ref, order_ref, c_ref, part_ref, grown_ref, factor_ref, tail_ref, win, turn,
+    got_ref, halo_ref, own_ref, z_ref, order_ref,
+    c_ref, part_ref, grown_ref, factor_ref, tail_ref, gate_ref, win, turn,
 ):
+    for lo in range(0, z_ref.shape[1], WIDE):
+        gate_ref[:, lo : lo + WIDE] = silu(z_ref[:, lo : lo + WIDE].astype(F32))
     _, _, blocks = sizes_of(got_ref)
     dts, cums = steps_of(got_ref, own_ref)
     taps = tiles_of(own_ref)
@@ -368,7 +366,8 @@
     rows = x_in.shape[0]
     tokens = rows * dests
     blocks = tokens // BLOCK
-    mine = (lax.axis_index("inner") * head + lax.axis_index("head")).astype(jnp.int32).reshape(1)
+    mine = lax.axis_index("inner") * head + lax.axis_index("head")
+    place = (mine * 2 + (lax.axis_index("outer") < outer - 1)).astype(jnp.int32).reshape(1)
 
     def of(dtype, *shape):
         return jax.ShapeDtypeStruct(shape, dtype)
@@ -386,13 +385,8 @@
             pltpu.VMEM((lead, WIDE), F32), pltpu.VMEM((2, lead, STATE), F32), pltpu.VMEM((2, 1, LANES), F32),
             pltpu.SemaphoreType.DMA((7,)), pltpu.SemaphoreType.DMA((5,)),
         ],
-    )(mine, *(pltpu.with_memory_space_constraint(a, pltpu.HBM) for a in operands))
+    )(place, *(pltpu.with_memory_space_constraint(a, pltpu.HBM) for a in operands))
     got = lax.all_to_all(sent, ("inner", "head"), 0, 0, tiled=True)
-    [gate] = kernel(
-        gate_body, "gate", [IN_VMEM], [of(F32, *z_in.shape)],
-        cost=pl.CostEstimate(flops=5 * z_in.size, bytes_accessed=6 * z_in.size, transcendentals=z_in.size),
-    )(z_in)
-
     if outer > 2:
         ends = got[-1, : (TILES + 2) * rows].reshape(TILES + 2, rows, LANES)[:, -TOP:]
         halo = shift(ends, "outer", 1).transpose(1, 0, 2).reshape(TOP, -1).astype(F32)
@@ -400,12 +394,11 @@
         halo = jnp.zeros((TOP, (TILES + 2) * LANES), F32)
 
     extra = STATE + TOP
-    sends = (lax.axis_index("outer") < outer - 1).astype(jnp.int32).reshape(1)
     send, fade = kernel(
         total_body, "total", [IN_SMEM] + [IN_VMEM] * 3,
         [of(BF16, extra, WIDE), of(F32, 8, WIDE)],
         [pltpu.VMEM((TILES + 1, TOP + tokens, LANES), F32)],
-    )(sends, got, halo, own)
+    )(place, got, halo, own)
 
     before = shift(send, "outer", 1)
     if outer > 2:
@@ -417,11 +410,11 @@
         before = jnp.concatenate([entering.astype(BF16), before[STATE:]], 0)
 
     wide = OWN * TOP
-    c, part, grown, factor, tail = kernel(
-        local_body, "local", [IN_VMEM] * 4,
+    c, part, grown, factor, tail, gate = kernel(
+        local_body, "local", [IN_VMEM] * 5,
         [
             of(BF16, tokens, STATE), of(F32, tokens, WIDE), of(F32, tokens, WIDE),
-            of(F32, 2, BLOCK, wide), of(F32, TOP, WIDE),
+            of(F32, 2, BLOCK, wide), of(F32, TOP, WIDE), of(F32, *z_in.shape),
         ],
         [pltpu.VMEM((TILES + 2, TOP + tokens, LANES), F32), pltpu.VMEM((BLOCK, LANES), F32)],
         pl.CostEstimate(
@@ -429,7 +422,7 @@
             bytes_accessed=tokens * WIDE * 12,
             transcendentals=blocks * OWN * BLOCK * BLOCK,
         ),
-    )(got, halo, own, fade)
+    )(got, halo, own, z_in, fade)
 
     [y] = kernel(
         carry_body, "carry", [IN_VMEM] * 8, [of(BF16, tokens, WIDE)],

time: 48.7 us -> 46.1 us (0.947)
  blocking collectives: 0 us -> 35.4 us
  waiting for transfers between devices: 24.2 us -> 0.01 us
  starting transfers between devices: 15.2 us -> 3.16 us
  Pallas kernels: 8.81 us -> 7.22 us
    all_to_all x0 -> x2, blocking collectives: none -> 35.4 us  [the longest x1 19.8 us: shards(): got = lax.all_to_all(sent, ('inner', 'head'), 0, 0, tiled=True)]
    all_to_all x2 -> x0, waiting for transfers between devices: 24.1 us -> none  [the longest x1 13.7 us: shards(): got = lax.all_to_all(sent, ('inner', 'head'), 0, 0, tiled=True)]
    all_to_all x2 -> x0, starting transfers between devices: 12.2 us -> none  [the longest x1 6.3 us: shards(): got = lax.all_to_all(sent, ('inner', 'head'), 0, 0, tiled=True)]
    pallas_call x1, Pallas kernels: 2.27 us -> 1.45 us  [shards(): kernel(pack_body, 'pack', [IN_SMEM] + [hbm] * len(operands), [of(BF16, de...]
    pallas_call x1, Pallas kernels: 1.33 us -> 0.54 us  [shards(): kernel(carry_body, 'carry', [IN_VMEM] * 8, [of(BF16, tokens, WIDE)], [plt...]
    pallas_call x2 -> x1, Pallas kernels: 2.74 us -> 2.76 us  [shards(): kernel(local_body, 'local', [IN_VMEM] * 5, [of(BF16, tokens, STATE), of(F...]
  transfers between devices with their start and end apart: 3 -> 1, of which waited for: 3 -> 0; matrix products, arithmetic and copies ran while one was open for 0% -> 0% of each run, Pallas kernels for 6% -> 6%
where the time goes in v5:
time: 46.1 us; the launch traced here: 45.9 us
  blocking collectives  35.4 us (77%)
  Pallas kernels  7.22 us (16%)
  starting transfers between devices  3.16 us (7%)
    all_to_all x1, blocking collectives, shards(): got = lax.all_to_all(sent, ('inner', 'head'), 0, 0, tiled=True)  19.8 us
    all_to_all x1, blocking collectives, shards(): lax.all_to_all(y.reshape(dests, rows, WIDE), ('inner', 'head'), 0, 0, til...  15.6 us
    ppermute x1, starting transfers between devices, shift(): lax.ppermute(block, axis, [(i, i + distance) for i in range(size - distan...  3.16 us
    pallas_call x1, Pallas kernels, shards(): kernel(local_body, 'local', [IN_VMEM] * 5, [of(BF16, tokens, STATE), of(F...  2.76 us
    pallas_call x1, Pallas kernels, shards(): kernel(total_body, 'total', [IN_SMEM] + [IN_VMEM] * 3, [of(BF16, extra, W...  1.46 us
    pallas_call x1, Pallas kernels, shards(): kernel(pack_body, 'pack', [IN_SMEM] + [hbm] * len(operands), [of(BF16, de...  1.45 us
    pallas_call x1, Pallas kernels, shards(): kernel(norm_body, 'norm', [IN_VMEM] * 3, [of(BF16, rows, dests * WIDE)],...  1.02 us
  transfers between devices with their start and end apart: 1, of which 0 were waited for; matrix products, arithmetic and copies ran while one was open for 0% of the time, Pallas kernels for 6%

profile of v5, /device:TPU:0, one launch (start us, length us, event | category | flops | bytes accessed | tf_op | source)
XLA Modules:
  0.0 45.9 jit_solution(16119952899902398524)
XLA Ops:
  0.0 1.5 %pack.1 = (bf16[16,200,128]{2,1,0:T(8,128)(2,1)S(1)}, f32[20,768]{1,0:T(8,128)S(1)}) custom-call(s32[1]{0:T(128)} %bitcast.place_ref, bf16[32,8192]{1,0:T(8,128)(2,1)} %x_hbm.1, bf16[32,1024]{1,0:T(8,128)(2,1)} %b_hbm.1, bf16[32,1024]{1,0:T(8,128)(2,1)} %c_hbm.1, bf16[32,128]{1,0:T(8,128)(2,1)} %dt_hbm.1, f32[4,8192]{1,0:T(4,128)} %tap_x.1, ...), custom_call_target="tpu_custom_call" | custom-call | tf_op jit(solution)/shard_map/pack/pallas_call | solution.py:379
  1.5 19.8 %all_to_all.10.got_ref = bf16[16,200,128]{2,1,0:T(8,128)(2,1)S(1)} all-to-all(bf16[16,200,128]{2,1,0:T(8,128)(2,1)S(1)} %get-tuple-element.15), channel_id=1, replica_groups=mesh['outer'=2,'inner'=4,'head'=4] {'inner','head'}, dimensions={0} | all-to-all | bytes 1638400 | tf_op jit(solution)/shard_map/all_to_all | solution.py:389
  21.3 0.0 copy-start
  21.3 1.5 %total.1 = (bf16[136,512]{1,0:T(8,128)(2,1)S(1)}, f32[8,512]{1,0:T(8,128)S(1)}) custom-call(s32[1]{0:T(128)} %bitcast.place_ref, bf16[16,200,128]{2,1,0:T(8,128)(2,1)S(1)} %all_to_all.10.got_ref, f32[8,768]{1,0:T(8,128)S(1)} %broadcast_in_dim.3.halo_ref, f32[20,768]{1,0:T(8,128)S(1)} %get-tuple-element.16.own_ref), custom_call_target="tpu_custom_call" | custom-call | tf_op jit(solution)/shard_map/total/pallas_call | solution.py:397
  22.7 3.2 %collective-permute-start = (bf16[136,512]{1,0:T(8,128)(2,1)S(1)}, bf16[136,512]{1,0:T(8,128)(2,1)S(1)}, u32[]{:S(2)}, u32[]{:S(2)}) collective-permute-start(bf16[136,512]{1,0:T(8,128)(2,1)S(1)} %get-tuple-element.17), channel_id=1, source_target_pairs={{0,16},{1,17},{2,18},{3,19},{4,20},{5,21},{6,22},{7,23},{8,24},{9,... | collective-permute-start | bytes 417800 | tf_op jit(solution)/shard_map/ppermute | solution.py:347
  25.9 0.0 copy-done
  25.9 2.8 %local.1 = (bf16[512,128]{1,0:T(8,128)(2,1)S(1)}, f32[512,512]{1,0:T(8,128)S(1)}, f32[512,512]{1,0:T(8,128)S(1)}, f32[2,128,64]{2,1,0:T(8,128)S(1)}, f32[8,512]{1,0:T(8,128)S(1)}, /*index=5*/f32[32,8192]{1,0:T(8,128)S(1)}) custom-call(bf16[16,200,128]{2,1,0:T(8,128)(2,1)S(1)} %all_to_all.10.got_ref, f32[8,768]{1,0:T(8,128)S(1)} %broadcast_in_dim.3.halo_ref, ...), custom_call_target="tpu_custom_call" | custom-call | flops 167772160 | bytes 3145728 | tf_op jit(solution)/shard_map/local/pallas_call | solution.py:413
  28.7 0.0 collective-permute-done.before_ref
  28.7 0.5 %carry.1 = bf16[512,512]{1,0:T(8,128)(2,1)S(1)} custom-call(bf16[16,200,128]{2,1,0:T(8,128)(2,1)S(1)} %all_to_all.10.got_ref, bf16[136,512]{1,0:T(8,128)(2,1)S(1)} %collective-permute-done.before_ref, f32[20,768]{1,0:T(8,128)S(1)} %get-tuple-element.16.own_ref, bf16[512,128]{1,0:T(8,128)(2,1)S(1)} %get-tuple-element.19.c_ref, ...), custom_call_target="tpu_custom_call" | custom-call | tf_op jit(solution)/shard_map/carry/pallas_call | solution.py:427
  29.2 0.0 copy-start.1
  29.2 15.6 %all_to_all.11.y_ref = bf16[16,32,512]{2,1,0:T(8,128)(2,1)S(1)} all-to-all(bf16[16,32,512]{2,1,0:T(8,128)(2,1)S(1)} %bitcast.5), channel_id=1, replica_groups=mesh['outer'=2,'inner'=4,'head'=4] {'inner','head'}, dimensions={0} | all-to-all | bytes 1048576 | tf_op jit(solution)/shard_map/all_to_all | solution.py:432
  44.9 0.0 copy-done.1
  44.9 1.0 %norm.1 = bf16[32,8192]{1,0:T(8,128)(2,1)} custom-call(bf16[16,32,512]{2,1,0:T(8,128)(2,1)S(1)} %all_to_all.11.y_ref, f32[32,8192]{1,0:T(8,128)S(1)} %get-tuple-element.24.gate_ref, f32[1,8192]{1,0:T(1,128)S(1)} %bitcast.6), custom_call_target="tpu_custom_call" | custom-call | tf_op jit(solution)/shard_map/norm/pallas_call | solution.py:433
  (1 shorter events, 0.0 us)
Async XLA Ops:
  21.3 4.6 %copy-start = (bf16[32,8192]{1,0:T(8,128)(2,1)S(1)}, bf16[32,8192]{1,0:T(8,128)(2,1)}, u32[]{:S(2)}) copy-start(bf16[32,8192]{1,0:T(8,128)(2,1)} %z_ref.1) | copy-start | bytes 1572868
  22.7 5.9 %collective-permute-start = (bf16[136,512]{1,0:T(8,128)(2,1)S(1)}, bf16[136,512]{1,0:T(8,128)(2,1)S(1)}, u32[]{:S(2)}, u32[]{:S(2)}) collective-permute-start(bf16[136,512]{1,0:T(8,128)(2,1)S(1)} %get-tuple-element.17), channel_id=1, source_target_pairs={{0,16},{1,17},{2,18},{3,19},{4,20},{5,21},{6,22},{7,23},{8,24},{9,... | collective-permute-start | bytes 417800 | tf_op jit(solution)/shard_map/ppermute | solution.py:347
  29.2 15.6 %copy-start.1 = (f32[8192]{0:T(1024)S(1)}, f32[8192]{0:T(1024)}, u32[]{:S(2)}) copy-start(f32[8192]{0:T(1024)} %param.21) | copy-start | bytes 98308

commit v6 on v4

--- a/solution.py
+++ b/solution.py
@@ -1,3 +1,4 @@
+import functools
 import jax
 import jax.numpy as jnp
 from jax import lax
@@ -142,11 +143,6 @@
         own_ref[at : at + OWN, :LANES] = jnp.broadcast_to(column, (OWN, LANES))
 
 
-def gate_body(z_ref, out_ref):
-    for lo in range(0, z_ref.shape[1], WIDE):
-        out_ref[:, lo : lo + WIDE] = silu(z_ref[:, lo : lo + WIDE].astype(F32))
-
-
 def sizes_of(got_ref):
     sources, total, _ = got_ref.shape
     rows = (total - OWN) // (TILES + 2)
@@ -187,38 +183,44 @@
     return [[v[j * OWN : (j + 1) * OWN] for j in range(blocks)] for v in (dt, cum)]
 
 
-def total_body(sends_ref, got_ref, halo_ref, own_ref, send_ref, fade_ref, win):
-    @pl.when(sends_ref[0] != 0)
-    def _():
-        sources, rows, blocks = sizes_of(got_ref)
-        dts, cums = steps_of(got_ref, own_ref)
-        taps = tiles_of(own_ref)
-        fill(win, got_ref, halo_ref, TILES + 1)
-        state = jnp.zeros((STATE, WIDE), F32)
-        after = jnp.zeros((OWN, 1), F32)
-        for j in reversed(range(blocks)):
-            after = after + cums[j][:, BLOCK - 1 :]
-            tail = expand(jnp.exp(after - cums[j]) * dts[j])
-            x = jnp.concatenate([conv_tile(win, taps, j, q) for q in range(TILES)], 1)
-            b = conv_tile(win, taps, j, TILES)
-            state = state + dot_t(jnp.concatenate([b, b], 0), stacked(x.astype(F32) * tail, 2))
-        fade_ref[...] = expand(jnp.broadcast_to(jnp.exp(after), (OWN, LANES)))[:8]
-        send_ref[:STATE] = state.astype(BF16)
-        ends = [got_ref[sources - 1, q * rows : (q + 1) * rows, :].astype(F32)[rows - TOP :] for q in range(TILES + 2)]
-        ends += [jnp.zeros_like(ends[0])] * (TILES - 2)
-        half = TOP // 2
-        upper = pltpu.roll(jnp.concatenate(ends[:TILES], 1), half, 0)
-        keep = iota((TOP, WIDE), 0) < half
-        send_ref[STATE:] = jnp.where(keep, upper, jnp.concatenate(ends[TILES:], 1)).astype(BF16)
+def total_body(got_ref, halo_ref, own_ref, send_ref, other_ref, win, sem, *, last_but_one):
+    sources, rows, blocks = sizes_of(got_ref)
+    if last_but_one:
+        copy = pltpu.make_async_copy(got_ref, other_ref, sem)
+        copy.start()
+    dts, cums = steps_of(got_ref, own_ref)
+    taps = tiles_of(own_ref)
+    fill(win, got_ref, halo_ref, TILES + 1)
+    state = jnp.zeros((STATE, WIDE), F32)
+    after = jnp.zeros((OWN, 1), F32)
+    for j in reversed(range(blocks)):
+        after = after + cums[j][:, BLOCK - 1 :]
+        tail = expand(jnp.exp(after - cums[j]) * dts[j])
+        x = jnp.concatenate([conv_tile(win, taps, j, q) for q in range(TILES)], 1)
+        b = conv_tile(win, taps, j, TILES)
+        state = state + dot_t(jnp.concatenate([b, b], 0), stacked(x.astype(F32) * tail, 2))
+    send_ref[:STATE] = state.astype(BF16)
+    ends = [got_ref[sources - 1, q * rows : (q + 1) * rows, :].astype(F32)[rows - TOP :] for q in range(TILES + 2)]
+    ends += [jnp.zeros_like(ends[0])] * (TILES - 2)
+    half = TOP // 2
+    upper = pltpu.roll(jnp.concatenate(ends[:TILES], 1), half, 0)
+    keep = iota((TOP, WIDE), 0) < half
+    send_ref[STATE:] = jnp.where(keep, upper, jnp.concatenate(ends[TILES:], 1)).astype(BF16)
+    if last_but_one:
+        copy.wait()
+    else:
+        other_ref[...] = expand(jnp.broadcast_to(jnp.exp(after), (OWN, LANES)))[:8]
 
 
 def local_body(
-    got_ref, halo_ref, own_ref, order_ref, c_ref, part_ref, grown_ref, factor_ref, tail_ref, win, turn,
+    got_ref, halo_ref, own_ref, c_ref, part_ref, growth_ref, factor_ref, tail_ref, top_ref, win, turn,
 ):
     _, _, blocks = sizes_of(got_ref)
     dts, cums = steps_of(got_ref, own_ref)
     taps = tiles_of(own_ref)
     fill(win, got_ref, halo_ref, TILES + 2)
+    for q in range(TILES + 2):
+        top_ref[q] = win[q, TOP : 2 * TOP]
     turn[...] = jnp.zeros_like(turn)
     for j in range(blocks):
         turn[j * OWN : (j + 1) * OWN] = cums[j]
@@ -243,11 +245,9 @@
         cum, dt = cums[j], dts[j]
         last = cum[:, BLOCK - 1 :]
         grown = expand(jnp.exp(cum))
-        if j < 2:
-            grown_ref[at : at + BLOCK] = grown
-        else:
+        if j > 1:
             past = past + cums[j - 1][:, BLOCK - 1 :]
-            grown_ref[at : at + BLOCK] = expand(jnp.exp(cum + past))
+        growth_ref[j] = jnp.exp(cum + past)
         if j > 0:
             carried = dot(jnp.concatenate([c, c], 1), stacked(local, 2)) * grown
         for q in range(TILES):
@@ -281,8 +281,8 @@
     factor_ref[1] = jnp.broadcast_to(dt_s, (BLOCK, wide))
 
 
-def carry_body(got_ref, before_ref, own_ref, c_ref, part_ref, grown_ref, factor_ref, tail_ref, y_ref, win, c_first):
-    _, rows, blocks = sizes_of(got_ref)
+def carry_body(before_ref, own_ref, c_ref, part_ref, growth_ref, factor_ref, tail_ref, top_ref, y_ref, win, c_first):
+    blocks = c_ref.shape[0] // BLOCK
     taps = tiles_of(own_ref)
     first = TOP - taps[0].shape[0] + 1
 
@@ -292,7 +292,7 @@
     for q in range(TILES + 2):
         lo = q * LANES
         win[q, :TOP] = upper[:, lo : lo + LANES] if q < TILES else halo[:, lo - WIDE : lo - WIDE + LANES]
-        win[q, TOP:] = got_ref[0, q * rows : (q + 1) * rows, :].astype(F32)[:TOP]
+        win[q, TOP:] = top_ref[q]
         done = conv(lambda k: win[q, first + k : first + k + TOP], taps[q])
         tops.append(done.astype(BF16).astype(F32))
     x_top = jnp.concatenate(tops[:TILES], 1)
@@ -300,7 +300,8 @@
     b_twice = jnp.concatenate([b_top, b_top], 0).astype(BF16)
     head = dot_t(b_twice, stacked(x_top * tail_ref[...], 2))
     state = before_ref[:STATE]
-    later = stacked(grown_ref[BLOCK - 1 : BLOCK] * state.astype(F32) + head, 2)
+    grown = expand(growth_ref[0])
+    later = stacked(grown[BLOCK - 1 :] * state.astype(F32) + head, 2)
 
     c_first[...] = c_ref[:BLOCK].astype(F32)
     c_first[:TOP] = tops[TILES + 1]
@@ -313,15 +314,15 @@
     shape = (wide, WIDE)
     own = iota(shape, 0) // TOP == iota(shape, 1) // HEAD_DIM
     added = dot(mix, jnp.where(own, jnp.concatenate([x_top] * OWN, 0), 0.0).astype(BF16))
-    y_ref[:BLOCK] = (part_ref[:BLOCK] + added + dot(c, state) * grown_ref[:BLOCK]).astype(BF16)
+    y_ref[:BLOCK] = (part_ref[:BLOCK] + added + dot(c, state) * grown).astype(BF16)
     for j in range(1, blocks):
         at = j * BLOCK
         c = c_ref[at : at + BLOCK]
         carried = dot(jnp.concatenate([c, c], 1), later)
-        y_ref[at : at + BLOCK] = (part_ref[at : at + BLOCK] + carried * grown_ref[at : at + BLOCK]).astype(BF16)
-
-
-def norm_body(y_ref, gate_ref, gain_ref, out_hbm, out_v, sem):
+        y_ref[at : at + BLOCK] = (part_ref[at : at + BLOCK] + carried * expand(growth_ref[j])).astype(BF16)
+
+
+def norm_body(y_ref, z_ref, gain_ref, out_hbm, out_v, sem):
     count = y_ref.shape[0]
     per = count // GROUPS
     copies = []
@@ -329,7 +330,7 @@
         gated = []
         square = 0.0
         for k in range(g * per, (g + 1) * per):
-            v = y_ref[k].astype(F32) * gate_ref[:, k * WIDE : (k + 1) * WIDE]
+            v = y_ref[k].astype(F32) * silu(z_ref[:, k * WIDE : (k + 1) * WIDE].astype(F32))
             gated.append(v)
             square = square + jnp.sum(v * v, axis=1, keepdims=True)
         scale = lax.rsqrt(square / (per * WIDE) + eps_norm)
@@ -356,7 +357,7 @@
         out_specs=out_specs or [IN_VMEM] * len(outs),
         out_shape=outs,
         scratch_shapes=list(scratch),
-        compiler_params=pltpu.CompilerParams(vmem_limit_bytes=40 * 2**20),
+        compiler_params=pltpu.CompilerParams(vmem_limit_bytes=16 * 2**20),
         cost_estimate=cost,
         name=name,
     )
@@ -387,60 +388,77 @@
             pltpu.SemaphoreType.DMA((7,)), pltpu.SemaphoreType.DMA((5,)),
         ],
     )(mine, *(pltpu.with_memory_space_constraint(a, pltpu.HBM) for a in operands))
-    got = lax.all_to_all(sent, ("inner", "head"), 0, 0, tiled=True)
-    [gate] = kernel(
-        gate_body, "gate", [IN_VMEM], [of(F32, *z_in.shape)],
-        cost=pl.CostEstimate(flops=5 * z_in.size, bytes_accessed=6 * z_in.size, transcendentals=z_in.size),
-    )(z_in)
-
-    if outer > 2:
+
+    def exchanged(array):
+        return lax.all_to_all(array, ("inner", "head"), 0, 0, tiled=True)
+
+    extra = STATE + TOP
+    wide = OWN * TOP
+
+    def total_of(got, halo):
+        last_but_one = outer == 2
+        return kernel(
+            functools.partial(total_body, last_but_one=last_but_one), "total", [IN_VMEM] * 3,
+            [of(BF16, extra, WIDE), of(BF16, *got.shape) if last_but_one else of(F32, 8, WIDE)],
+            [pltpu.VMEM((TILES + 1, TOP + tokens, LANES), F32), pltpu.SemaphoreType.DMA],
+            out_specs=[IN_VMEM, hbm if last_but_one else IN_VMEM],
+        )(got, halo, own)
+
+    def local_of(got, halo):
+        return kernel(
+            local_body, "local", [IN_VMEM] * 3,
+            [
+                of(BF16, tokens, STATE), of(F32, tokens, WIDE), of(F32, blocks, OWN, BLOCK), of(F32, 2, BLOCK, wide),
+                of(F32, TOP, WIDE), of(F32, TILES + 2, TOP, LANES),
+            ],
+            [pltpu.VMEM((TILES + 2, TOP + tokens, LANES), F32), pltpu.VMEM((BLOCK, LANES), F32)],
+            pl.CostEstimate(
+                flops=2 * blocks * OWN * BLOCK * BLOCK * 160,
+                bytes_accessed=tokens * WIDE * 12,
+                transcendentals=blocks * OWN * BLOCK * BLOCK,
+            ),
+        )(got, halo, own)
+
+    if outer == 2:
+        halo = jnp.zeros((TOP, (TILES + 2) * LANES), F32)
+        leads = lax.axis_index("outer") == 0
+        send, kept = lax.cond(
+            leads,
+            lambda array: tuple(total_of(exchanged(array), halo)),
+            lambda array: (jnp.zeros((extra, WIDE), BF16), array),
+            sent,
+        )
+        before = shift(send, "outer", 1)
+        c, part, growth, factor, tail, top = lax.cond(
+            leads,
+            lambda array, kept: tuple(local_of(kept, halo)),
+            lambda array, kept: tuple(local_of(exchanged(array), halo)),
+            sent, kept,
+        )
+    else:
+        got = exchanged(sent)
         ends = got[-1, : (TILES + 2) * rows].reshape(TILES + 2, rows, LANES)[:, -TOP:]
         halo = shift(ends, "outer", 1).transpose(1, 0, 2).reshape(TOP, -1).astype(F32)
-    else:
-        halo = jnp.zeros((TOP, (TILES + 2) * LANES), F32)
-
-    extra = STATE + TOP
-    sends = (lax.axis_index("outer") < outer - 1).astype(jnp.int32).reshape(1)
-    send, fade = kernel(
-        total_body, "total", [IN_SMEM] + [IN_VMEM] * 3,
-        [of(BF16, extra, WIDE), of(F32, 8, WIDE)],
-        [pltpu.VMEM((TILES + 1, TOP + tokens, LANES), F32)],
-    )(sends, got, halo, own)
-
-    before = shift(send, "outer", 1)
-    if outer > 2:
+        send, fade = total_of(got, halo)
+        before = shift(send, "outer", 1)
         entering, held, reach = before[:STATE].astype(F32), shift(fade, "outer", 1), 1
         while reach < outer - 1:
             entering = entering + held[:1] * shift(entering, "outer", reach)
             held = held * shift(held, "outer", reach)
             reach *= 2
         before = jnp.concatenate([entering.astype(BF16), before[STATE:]], 0)
-
-    wide = OWN * TOP
-    c, part, grown, factor, tail = kernel(
-        local_body, "local", [IN_VMEM] * 4,
-        [
-            of(BF16, tokens, STATE), of(F32, tokens, WIDE), of(F32, tokens, WIDE),
-            of(F32, 2, BLOCK, wide), of(F32, TOP, WIDE),
-        ],
-        [pltpu.VMEM((TILES + 2, TOP + tokens, LANES), F32), pltpu.VMEM((BLOCK, LANES), F32)],
-        pl.CostEstimate(
-            flops=2 * blocks * OWN * BLOCK * BLOCK * 160,
-            bytes_accessed=tokens * WIDE * 12,
-            transcendentals=blocks * OWN * BLOCK * BLOCK,
-        ),
-    )(got, halo, own, fade)
+        c, part, growth, factor, tail, top = local_of(got, halo)
 
     [y] = kernel(
         carry_body, "carry", [IN_VMEM] * 8, [of(BF16, tokens, WIDE)],
         [pltpu.VMEM((TILES + 2, 2 * TOP, LANES), F32), pltpu.VMEM((BLOCK, STATE), F32)],
-    )(got, before, own, c, part, grown, factor, tail)
+    )(before, own, c, part, growth, factor, tail, top)
 
     home = lax.all_to_all(y.reshape(dests, rows, WIDE), ("inner", "head"), 0, 0, tiled=True)
     [out] = kernel(
         norm_body, "norm", [IN_VMEM] * 3, [of(BF16, rows, dests * WIDE)],
         [pltpu.VMEM((rows, dests * WIDE), BF16), pltpu.SemaphoreType.DMA((GROUPS,))], out_specs=[hbm],
-    )(home, gate, norm_gain.reshape(1, -1))
+    )(home, z_in, norm_gain.reshape(1, -1))
     return out
 
 

time: 48.7 us -> 45.2 us (0.928)
  blocking collectives: 0 us -> 35.9 us
  waiting for transfers between devices: 24.2 us -> 0.12 us
  starting transfers between devices: 15.2 us -> 1.3 us
  Pallas kernels: 8.81 us -> 7.47 us
    all_to_all x0 -> x2, blocking collectives: none -> 35.9 us  [the longest x1 19.8 us: exchanged(): return lax.all_to_all(array, ('inner', 'head'), 0, 0, tiled=True)]
    all_to_all x2 -> x0, waiting for transfers between devices: 24.1 us -> none  [the longest x1 13.7 us: shards(): got = lax.all_to_all(sent, ('inner', 'head'), 0, 0, tiled=True)]
    all_to_all x2 -> x0, starting transfers between devices: 12.2 us -> none  [the longest x1 6.3 us: shards(): got = lax.all_to_all(sent, ('inner', 'head'), 0, 0, tiled=True)]
    ppermute x1, starting transfers between devices: 3.02 us -> 1.3 us  [shift(): lax.ppermute(block, axis, [(i, i + distance) for i in range(size - distan...]
    pallas_call x1, Pallas kernels: 2.27 us -> 1.45 us  [shards(): kernel(pack_body, 'pack', [IN_SMEM] + [hbm] * len(operands), [of(BF16, de...]
    pallas_call x1, Pallas kernels: 1.33 us -> 0.7 us  [shards(): kernel(carry_body, 'carry', [IN_VMEM] * 8, [of(BF16, tokens, WIDE)], [plt...]
    pallas_call x3 -> x2, Pallas kernels: 4.19 us -> 4.13 us  [the longest x1 2.58 us: local_of(): kernel(local_body, 'local', [IN_VMEM] * 3, [of(BF16, tokens, STATE), of(F...]
  transfers between devices with their start and end apart: 3 -> 1, of which waited for: 3 -> 1; matrix products, arithmetic and copies ran while one was open for 0% -> 0% of each run, Pallas kernels for 6% -> 6%
where the time goes in v6:
time: 45.2 us; the launch traced here: 44.9 us
  blocking collectives  35.9 us (79%)
  Pallas kernels  7.47 us (17%)
  starting transfers between devices  1.3 us (3%)
    all_to_all x1, blocking collectives, exchanged(): return lax.all_to_all(array, ('inner', 'head'), 0, 0, tiled=True)  19.8 us
    all_to_all x1, blocking collectives, shards(): lax.all_to_all(y.reshape(dests, rows, WIDE), ('inner', 'head'), 0, 0, til...  16.1 us
    pallas_call x1, Pallas kernels, local_of(): kernel(local_body, 'local', [IN_VMEM] * 3, [of(BF16, tokens, STATE), of(F...  2.58 us
    pallas_call x1, Pallas kernels, total_of(): kernel(functools.partial(total_body, last_but_one=last_but_one), 'total',...  1.54 us
    pallas_call x1, Pallas kernels, shards(): kernel(pack_body, 'pack', [IN_SMEM] + [hbm] * len(operands), [of(BF16, de...  1.45 us
    ppermute x1, starting transfers between devices, shift(): lax.ppermute(block, axis, [(i, i + distance) for i in range(size - distan...  1.3 us
    pallas_call x1, Pallas kernels, shards(): kernel(norm_body, 'norm', [IN_VMEM] * 3, [of(BF16, rows, dests * WIDE)],...  1.19 us
  transfers between devices with their start and end apart: 1, of which 1 were waited for; matrix products, arithmetic and copies ran while one was open for 0% of the time, Pallas kernels for 6%

profile of v6, /device:TPU:0, one launch (start us, length us, event | category | flops | bytes accessed | tf_op | source)
XLA Modules:
  0.0 44.9 jit_solution(17342832810191972640)
XLA Ops:
  0.0 1.5 %pack.1 = (bf16[16,200,128]{2,1,0:T(8,128)(2,1)S(1)}, f32[20,768]{1,0:T(8,128)S(1)}) custom-call(s32[1]{0:T(128)} %bitcast.mine_ref, bf16[32,8192]{1,0:T(8,128)(2,1)} %x_hbm.1, bf16[32,1024]{1,0:T(8,128)(2,1)} %b_hbm.1, bf16[32,1024]{1,0:T(8,128)(2,1)} %c_hbm.1, bf16[32,128]{1,0:T(8,128)(2,1)} %dt_hbm.1, f32[4,8192]{1,0:T(4,128)} %tap_x.1, f32[4,1024]{1,0:T(4,128)} %tap_b.1, ...), custom_call_target="tpu_custom_call" | custom-call | tf_op jit(solution)/shard_map/pack/pallas_call | solution.py:381
  1.5 21.4 %conditional.2 = ((bf16[136,512]{1,0:T(8,128)(2,1)S(1)}, bf16[16,200,128]{2,1,0:T(8,128)(2,1)S(1)})) conditional(s32[]{:T(128)} %convert_element_type.4, bf16[16,200,128]{2,1,0:T(8,128)(2,1)S(1)} %get-tuple-element.34, (bf16[16,200,128]{2,1,0:T(8,128)(2,1)S(1)}, f32[20,768]{1,0:T(8,128)S(1)}) %pack.1), branch_computations={%region_0.0_spmd, %region_1.0_spmd} | conditional | bytes 1777690 | solution.py:425
  1.5 19.8 %all_to_all.13.got_ref = bf16[16,200,128]{2,1,0:T(8,128)(2,1)S(1)} all-to-all(bf16[16,200,128]{2,1,0:T(8,128)(2,1)S(1)} %get-tuple-element.18), channel_id=1, replica_groups=mesh['outer'=2,'inner'=4,'head'=4] {'inner','head'}, dimensions={0} | all-to-all | bytes 1638400 | tf_op jit(solution)/shard_map/cond/branch_1_fun/all_to_all | solution.py:393
  21.3 1.5 %total.1 = (bf16[136,512]{1,0:T(8,128)(2,1)S(1)}, bf16[16,200,128]{2,1,0:T(8,128)(2,1)S(1)}) custom-call(bf16[16,200,128]{2,1,0:T(8,128)(2,1)S(1)} %all_to_all.13.got_ref, f32[8,768]{1,0:T(8,128)S(1)} %broadcast_in_dim.6.halo_ref, f32[20,768]{1,0:T(8,128)S(1)} %get-tuple-element.19.own_ref), custom_call_target="tpu_custom_call" | custom-call | tf_op jit(solution)/shard_map/cond/branch_1_fun/total/pallas_call | solution.py:400
  22.8 1.3 %collective-permute-start = (bf16[136,512]{1,0:T(8,128)(2,1)S(1)}, bf16[136,512]{1,0:T(8,128)(2,1)S(1)}, u32[]{:S(2)}, u32[]{:S(2)}) collective-permute-start(bf16[136,512]{1,0:T(8,128)(2,1)S(1)} %get-tuple-element.35), channel_id=1, source_target_pairs={{0,16},{1,17},{2,18},{3,19},{4,20},{5,21},{6,22},{7,23},{8,24},{9,... | collective-permute-start | bytes 417800 | tf_op jit(solution)/shard_map/ppermute | solution.py:350
  24.1 2.6 %conditional.3 = ((bf16[512,128]{1,0:T(8,128)(2,1)S(1)}, f32[512,512]{1,0:T(8,128)S(1)}, f32[4,8,128]{2,1,0:T(8,128)S(1)}, f32[2,128,64]{2,1,0:T(8,128)S(1)}, f3...) conditional(s32[]{:T(128)} %convert_element_type.4, (bf16[16,200,128]{2,1,0:T(8,128)(2,1)S(1)}, ...), branch_computations={%region_2.0_spmd, %region_3.0_spmd} | conditional | flops 167772160 | bytes 4808716 | solution.py:432
  24.2 2.6 %local.3 = (bf16[512,128]{1,0:T(8,128)(2,1)S(1)}, f32[512,512]{1,0:T(8,128)S(1)}, f32[4,8,128]{2,1,0:T(8,128)S(1)}, f32[2,128,64]{2,1,0:T(8,128)S(1)}, f32[8,512]{1,0:T(8,128)S(1)}, /*index=5*/f32[6,8,128]{2,1,0:T(8,128)S(1)}) custom-call(bf16[16,200,128]{2,1,0:T(8,128)(2,1)S(1)} %get-tuple-element.22.got_ref, f32[8,768]{1,0:T(8,128)S(1)} %broadcast_in_dim.8.halo_ref, ...), custom_call_target="tpu_custom_call" | custom-call | flops 167772160 | bytes 3145728 | tf_op jit(solution)/shard_map/cond/branch_1_fun/local/pallas_call | solution.py:408
  26.8 0.1 collective-permute-done.before_ref
  26.9 0.7 %carry.1 = bf16[512,512]{1,0:T(8,128)(2,1)S(1)} custom-call(bf16[136,512]{1,0:T(8,128)(2,1)S(1)} %collective-permute-done.before_ref, f32[20,768]{1,0:T(8,128)S(1)} %get-tuple-element.36.own_ref, bf16[512,128]{1,0:T(8,128)(2,1)S(1)} %get-tuple-element.38.c_ref, f32[512,512]{1,0:T(8,128)S(1)} %get-tuple-element.39.part_ref, ...), custom_call_target="tpu_custom_call" | custom-call | tf_op jit(solution)/shard_map/carry/pallas_call | solution.py:452
  27.6 0.0 copy-start
  27.6 0.0 copy-start.1
  27.6 16.1 %all_to_all.15.y_ref = bf16[16,32,512]{2,1,0:T(8,128)(2,1)S(1)} all-to-all(bf16[16,32,512]{2,1,0:T(8,128)(2,1)S(1)} %bitcast.5), channel_id=1, replica_groups=mesh['outer'=2,'inner'=4,'head'=4] {'inner','head'}, dimensions={0} | all-to-all | bytes 1048576 | tf_op jit(solution)/shard_map/all_to_all | solution.py:457
  43.7 0.0 copy-done
  43.7 0.0 copy-done.1
  43.7 1.2 %norm.1 = bf16[32,8192]{1,0:T(8,128)(2,1)} custom-call(bf16[16,32,512]{2,1,0:T(8,128)(2,1)S(1)} %all_to_all.15.y_ref, bf16[32,8192]{1,0:T(8,128)(2,1)S(1)} %copy-done, f32[1,8192]{1,0:T(1,128)S(1)} %bitcast.6), custom_call_target="tpu_custom_call" | custom-call | tf_op jit(solution)/shard_map/norm/pallas_call | solution.py:458
  (2 shorter events, 0.0 us)
Async XLA Ops:
  22.8 4.0 %collective-permute-start = (bf16[136,512]{1,0:T(8,128)(2,1)S(1)}, bf16[136,512]{1,0:T(8,128)(2,1)S(1)}, u32[]{:S(2)}, u32[]{:S(2)}) collective-permute-start(bf16[136,512]{1,0:T(8,128)(2,1)S(1)} %get-tuple-element.35), channel_id=1, source_target_pairs={{0,16},{1,17},{2,18},{3,19},{4,20},{5,21},{6,22},{7,23},{8,24},{9,... | collective-permute-start | bytes 417800 | tf_op jit(solution)/shard_map/ppermute | solution.py:350
  27.6 16.1 %copy-start = (bf16[32,8192]{1,0:T(8,128)(2,1)S(1)}, bf16[32,8192]{1,0:T(8,128)(2,1)}, u32[]{:S(2)}) copy-start(bf16[32,8192]{1,0:T(8,128)(2,1)} %z_ref.1) | copy-start | bytes 1572868
  27.6 16.1 %copy-start.1 = (f32[8192]{0:T(1024)S(1)}, f32[8192]{0:T(1024)}, u32[]{:S(2)}) copy-start(f32[8192]{0:T(1024)} %param.25) | copy-start | bytes 98308

commit v7 on v6

--- a/solution.py
+++ b/solution.py
@@ -21,7 +21,7 @@
 F32 = jnp.float32
 BF16 = jnp.bfloat16
 IN_VMEM = pl.BlockSpec(memory_space=pltpu.VMEM)
-IN_SMEM = pl.BlockSpec(memory_space=pltpu.SMEM)
+AXES = ("outer", "inner", "head")
 
 
 def dot(a, b):
@@ -70,6 +70,14 @@
     return silu(total)
 
 
+def turned():
+    return lax.rem(lax.axis_index("outer"), 2) * (lax.axis_size("inner") * lax.axis_size("head") // 2)
+
+
+def holder(block, turn, count):
+    return block + turn if block < count // 2 else block - turn
+
+
 def tiles_of(own_ref):
     return [own_ref[:lead_of(own_ref), q * LANES : (q + 1) * LANES] for q in range(TILES + 2)]
 
@@ -79,11 +87,13 @@
 
 
 def pack_body(
-    mine_ref, x_hbm, b_hbm, c_hbm, dt_hbm, tap_x, tap_b, tap_c, bias_hbm, log_hbm,
-    out_v, own_ref, x_v, b_v, c_v, dt_v, turn, x_tap, s_taps, heads_v, sem_in, sem_own,
+    x_hbm, b_hbm, c_hbm, dt_hbm, tap_x, tap_b, tap_c, bias_hbm, log_hbm, gain_hbm,
+    out_v, own_ref, gain_ref, x_v, b_v, c_v, dt_v, turn, x_tap, s_taps, heads_v, sem_in, sem_own,
 ):
-    mine = mine_ref[0]
+    place = lax.axis_index("inner") * lax.axis_size("head") + lax.axis_index("head")
     count = out_v.shape[0]
+    half_turn = turned()
+    mine = lax.rem(place + half_turn, count)
     rows = x_v.shape[0]
     share = count * STATE // b_v.shape[1]
     cuts = 4
@@ -107,28 +117,30 @@
             (tap_c.at[:, pl.ds(at_s, STATE)], s_taps.at[1]),
             (bias_hbm, heads_v.at[0]),
             (log_hbm, heads_v.at[1]),
+            (gain_hbm, gain_ref),
         ))
     ]
     for copy in small + large + own:
         copy.start()
     small[0].wait()
     turn[...] = jnp.zeros_like(turn)
-    at = pl.multiple_of(lax.rem(mine, BLOCK // rows) * rows, rows)
+    at = pl.multiple_of(lax.rem(place, BLOCK // rows) * rows, rows)
     turn[pl.ds(at, rows), :] = dt_v[...].astype(F32)
     heads = turn[...].T
-    for k in range(count):
-        out_v[k, (TILES + 2) * rows :, :] = heads[k * OWN : (k + 1) * OWN].astype(BF16)
     small[1].wait()
     small[2].wait()
-    for k in range(count):
-        g = k // share
-        out_v[k, TILES * rows : (TILES + 1) * rows, :] = b_v[:, g * STATE : (g + 1) * STATE]
-        out_v[k, (TILES + 1) * rows : (TILES + 2) * rows, :] = c_v[:, g * STATE : (g + 1) * STATE]
+    for block in range(count):
+        k = holder(block, half_turn, count)
+        at = block // share * STATE
+        out_v[k, TILES * rows : (TILES + 1) * rows, :] = b_v[:, at : at + STATE]
+        out_v[k, (TILES + 1) * rows : (TILES + 2) * rows, :] = c_v[:, at : at + STATE]
+        out_v[k, (TILES + 2) * rows :, :] = heads[block * OWN : (block + 1) * OWN].astype(BF16)
     for i in range(cuts):
         large[i].wait()
-        for k in range(i * step, (i + 1) * step):
+        for block in range(i * step, (i + 1) * step):
+            k = holder(block, half_turn, count)
             for q in range(TILES):
-                lo = k * WIDE + q * LANES
+                lo = block * WIDE + q * LANES
                 out_v[k, q * rows : (q + 1) * rows, :] = x_v[:, lo : lo + LANES]
     for copy in own:
         copy.wait()
@@ -167,11 +179,12 @@
     _, rows, blocks = sizes_of(got_ref)
     per = BLOCK // rows
     lead = lead_of(own_ref)
+    at = got_ref.shape[1] - OWN
     raws = []
     for j in range(blocks):
-        raw = got_ref[j * per, (TILES + 2) * rows :, :].astype(F32)
+        raw = got_ref[j * per, at:, :].astype(F32)
         for s in range(1, per):
-            raw = raw + got_ref[j * per + s, (TILES + 2) * rows :, :].astype(F32)
+            raw = raw + got_ref[j * per + s, at:, :].astype(F32)
         raws.append(raw + own_ref[lead : lead + OWN, :LANES])
     raw = jnp.concatenate(raws, 0)
     dt = jnp.maximum(raw, 0.0) + jnp.log1p(jnp.exp(-jnp.abs(raw)))
@@ -213,8 +226,11 @@
 
 
 def local_body(
-    got_ref, halo_ref, own_ref, c_ref, part_ref, growth_ref, factor_ref, tail_ref, top_ref, win, turn,
+    got_ref, halo_ref, own_ref, z_hbm,
+    c_ref, part_ref, growth_ref, factor_ref, tail_ref, top_ref, z_ref, order_ref, win, turn, sem,
 ):
+    fetch = pltpu.make_async_copy(z_hbm, z_ref, sem)
+    fetch.start()
     _, _, blocks = sizes_of(got_ref)
     dts, cums = steps_of(got_ref, own_ref)
     taps = tiles_of(own_ref)
@@ -279,6 +295,8 @@
     seen = iota((BLOCK, wide), 0) >= iota((BLOCK, wide), 1) % TOP
     factor_ref[0] = jnp.where(seen, decay, 0.0)
     factor_ref[1] = jnp.broadcast_to(dt_s, (BLOCK, wide))
+    order_ref[...] = jnp.zeros_like(order_ref)
+    fetch.wait()
 
 
 def carry_body(before_ref, own_ref, c_ref, part_ref, growth_ref, factor_ref, tail_ref, top_ref, y_ref, win, c_first):
@@ -322,15 +340,23 @@
         y_ref[at : at + BLOCK] = (part_ref[at : at + BLOCK] + carried * expand(growth_ref[j])).astype(BF16)
 
 
-def norm_body(y_ref, z_ref, gain_ref, out_hbm, out_v, sem):
-    count = y_ref.shape[0]
+def unset_body(*refs):
+    refs[-1][...] = jnp.zeros_like(refs[-1])
+
+
+def norm_body(early_ref, late_ref, z_ref, gain_ref, out_hbm, out_v, sem):
+    count = late_ref.shape[0]
     per = count // GROUPS
+    leads = (lax.axis_index("outer") == 0) & (lax.axis_size("outer") == 2)
+    half_turn = turned()
     copies = []
     for g in range(GROUPS):
         gated = []
         square = 0.0
         for k in range(g * per, (g + 1) * per):
-            v = y_ref[k].astype(F32) * silu(z_ref[:, k * WIDE : (k + 1) * WIDE].astype(F32))
+            at = holder(k, half_turn, count)
+            y = jnp.where(leads, early_ref[at].astype(F32), late_ref[at].astype(F32))
+            v = y * silu(z_ref[:, k * WIDE : (k + 1) * WIDE].astype(F32))
             gated.append(v)
             square = square + jnp.sum(v * v, axis=1, keepdims=True)
         scale = lax.rsqrt(square / (per * WIDE) + eps_norm)
@@ -345,9 +371,15 @@
         copy.wait()
 
 
-def shift(block, axis, distance):
-    size = lax.axis_size(axis)
-    return lax.ppermute(block, axis, [(i, i + distance) for i in range(size - distance)])
+def shift(array, distance):
+    outer, inner, head = (lax.axis_size(a) for a in AXES)
+    count = inner * head
+
+    def at(stretch, block):
+        return stretch * count + holder(block, stretch % 2 * (count // 2), count)
+
+    route = [(at(o, k), at(o + distance, k)) for o in range(outer - distance) for k in range(count)]
+    return lax.ppermute(array, AXES, route)
 
 
 def kernel(body, name, ins, outs, scratch=(), cost=None, out_specs=None):
@@ -364,12 +396,11 @@
 
 
 def shards(x_in, b_in, c_in, dt_in, z_in, conv_x, input_state_taps, conv_c, dt_bias, a_log, norm_gain):
-    outer, inner, head = (lax.axis_size(a) for a in ("outer", "inner", "head"))
+    outer, inner, head = (lax.axis_size(a) for a in AXES)
     dests = inner * head
     rows = x_in.shape[0]
     tokens = rows * dests
     blocks = tokens // BLOCK
-    mine = (lax.axis_index("inner") * head + lax.axis_index("head")).astype(jnp.int32).reshape(1)
 
     def of(dtype, *shape):
         return jax.ShapeDtypeStruct(shape, dtype)
@@ -377,17 +408,19 @@
     total = (TILES + 2) * rows + OWN
     lead = conv_x.shape[0]
     hbm = pl.BlockSpec(memory_space=pltpu.HBM)
-    operands = (x_in, b_in, c_in, dt_in, conv_x, input_state_taps, conv_c, dt_bias.reshape(1, -1), a_log.reshape(1, -1))
-    sent, own = kernel(
-        pack_body, "pack", [IN_SMEM] + [hbm] * len(operands),
-        [of(BF16, dests, total, LANES), of(F32, lead + 2 * OWN, WIDE + 2 * STATE)],
+    rows_of = [v.reshape(1, -1) for v in (dt_bias, a_log, norm_gain)]
+    operands = (x_in, b_in, c_in, dt_in, conv_x, input_state_taps, conv_c, *rows_of)
+    z_pinned = pltpu.with_memory_space_constraint(z_in, pltpu.HBM)
+    sent, own, gain = kernel(
+        pack_body, "pack", [hbm] * len(operands),
+        [of(BF16, dests, total, LANES), of(F32, lead + 2 * OWN, WIDE + 2 * STATE), of(F32, 1, norm_gain.size)],
         [
             pltpu.VMEM(x_in.shape, BF16), pltpu.VMEM(b_in.shape, BF16), pltpu.VMEM(c_in.shape, BF16),
             pltpu.VMEM(dt_in.shape, BF16), pltpu.VMEM((BLOCK, LANES), F32),
             pltpu.VMEM((lead, WIDE), F32), pltpu.VMEM((2, lead, STATE), F32), pltpu.VMEM((2, 1, LANES), F32),
-            pltpu.SemaphoreType.DMA((7,)), pltpu.SemaphoreType.DMA((5,)),
+            pltpu.SemaphoreType.DMA((7,)), pltpu.SemaphoreType.DMA((6,)),
         ],
-    )(mine, *(pltpu.with_memory_space_constraint(a, pltpu.HBM) for a in operands))
+    )(*(pltpu.with_memory_space_constraint(a, pltpu.HBM) for a in operands))
 
     def exchanged(array):
         return lax.all_to_all(array, ("inner", "head"), 0, 0, tiled=True)
@@ -399,25 +432,39 @@
         last_but_one = outer == 2
         return kernel(
             functools.partial(total_body, last_but_one=last_but_one), "total", [IN_VMEM] * 3,
-            [of(BF16, extra, WIDE), of(BF16, *got.shape) if last_but_one else of(F32, 8, WIDE)],
+            [pltpu.VMEM((extra, WIDE), BF16), of(BF16, *got.shape) if last_but_one else of(F32, 8, WIDE)],
             [pltpu.VMEM((TILES + 1, TOP + tokens, LANES), F32), pltpu.SemaphoreType.DMA],
             out_specs=[IN_VMEM, hbm if last_but_one else IN_VMEM],
         )(got, halo, own)
 
     def local_of(got, halo):
         return kernel(
-            local_body, "local", [IN_VMEM] * 3,
+            local_body, "local", [IN_VMEM] * 3 + [hbm],
             [
                 of(BF16, tokens, STATE), of(F32, tokens, WIDE), of(F32, blocks, OWN, BLOCK), of(F32, 2, BLOCK, wide),
-                of(F32, TOP, WIDE), of(F32, TILES + 2, TOP, LANES),
+                of(F32, TOP, WIDE), of(F32, TILES + 2, TOP, LANES), of(BF16, *z_in.shape),
+                of(F32, 8, LANES),
             ],
-            [pltpu.VMEM((TILES + 2, TOP + tokens, LANES), F32), pltpu.VMEM((BLOCK, LANES), F32)],
+            [
+                pltpu.VMEM((TILES + 2, TOP + tokens, LANES), F32), pltpu.VMEM((BLOCK, LANES), F32),
+                pltpu.SemaphoreType.DMA,
+            ],
             pl.CostEstimate(
                 flops=2 * blocks * OWN * BLOCK * BLOCK * 160,
                 bytes_accessed=tokens * WIDE * 12,
                 transcendentals=blocks * OWN * BLOCK * BLOCK,
             ),
-        )(got, halo, own)
+        )(got, halo, own, z_pinned)
+
+    def unset(like, *after):
+        return tuple(kernel(unset_body, "unset", [IN_VMEM] * len(after), [of(a.dtype, *a.shape) for a in like])(*after))
+
+    def leaving(before, *done):
+        [y] = kernel(
+            carry_body, "carry", [IN_VMEM] * 8, [of(BF16, tokens, WIDE)],
+            [pltpu.VMEM((TILES + 2, 2 * TOP, LANES), F32), pltpu.VMEM((BLOCK, STATE), F32)],
+        )(before, own, *done)
+        return exchanged(y.reshape(dests, rows, WIDE))
 
     if outer == 2:
         halo = jnp.zeros((TOP, (TILES + 2) * LANES), F32)
@@ -425,48 +472,54 @@
         send, kept = lax.cond(
             leads,
             lambda array: tuple(total_of(exchanged(array), halo)),
-            lambda array: (jnp.zeros((extra, WIDE), BF16), array),
+            lambda array: unset([of(BF16, extra, WIDE), sent]),
             sent,
         )
-        before = shift(send, "outer", 1)
-        c, part, growth, factor, tail, top = lax.cond(
+        before = shift(send, 1)
+
+        def first(array, kept):
+            *done, z, order = local_of(kept, halo)
+            *rest, nothing = unset([*done, send], order)
+            return leaving(nothing, *done), tuple(rest), z
+
+        def second(array, kept):
+            *done, z, order = local_of(exchanged(array), halo)
+            return unset([of(BF16, dests, rows, WIDE)], order)[0], tuple(done), z
+
+        early, done, z = lax.cond(leads, first, second, sent, kept)
+        late = lax.cond(
             leads,
-            lambda array, kept: tuple(local_of(kept, halo)),
-            lambda array, kept: tuple(local_of(exchanged(array), halo)),
-            sent, kept,
+            lambda before, done: unset([of(BF16, dests, rows, WIDE)])[0],
+            lambda before, done: leaving(before, *done),
+            before, done,
         )
     else:
         got = exchanged(sent)
         ends = got[-1, : (TILES + 2) * rows].reshape(TILES + 2, rows, LANES)[:, -TOP:]
-        halo = shift(ends, "outer", 1).transpose(1, 0, 2).reshape(TOP, -1).astype(F32)
+        halo = shift(ends, 1).transpose(1, 0, 2).reshape(TOP, -1).astype(F32)
         send, fade = total_of(got, halo)
-        before = shift(send, "outer", 1)
-        entering, held, reach = before[:STATE].astype(F32), shift(fade, "outer", 1), 1
+        before = shift(send, 1)
+        entering, held, reach = before[:STATE].astype(F32), shift(fade, 1), 1
         while reach < outer - 1:
-            entering = entering + held[:1] * shift(entering, "outer", reach)
-            held = held * shift(held, "outer", reach)
+            entering = entering + held[:1] * shift(entering, reach)
+            held = held * shift(held, reach)
             reach *= 2
         before = jnp.concatenate([entering.astype(BF16), before[STATE:]], 0)
-        c, part, growth, factor, tail, top = local_of(got, halo)
-
-    [y] = kernel(
-        carry_body, "carry", [IN_VMEM] * 8, [of(BF16, tokens, WIDE)],
-        [pltpu.VMEM((TILES + 2, 2 * TOP, LANES), F32), pltpu.VMEM((BLOCK, STATE), F32)],
-    )(before, own, c, part, growth, factor, tail, top)
-
-    home = lax.all_to_all(y.reshape(dests, rows, WIDE), ("inner", "head"), 0, 0, tiled=True)
+        *done, z, _ = local_of(got, halo)
+        early = late = leaving(before, *done)
+
     [out] = kernel(
-        norm_body, "norm", [IN_VMEM] * 3, [of(BF16, rows, dests * WIDE)],
+        norm_body, "norm", [IN_VMEM] * 4, [of(BF16, rows, dests * WIDE)],
         [pltpu.VMEM((rows, dests * WIDE), BF16), pltpu.SemaphoreType.DMA((GROUPS,))], out_specs=[hbm],
-    )(home, z_in, norm_gain.reshape(1, -1))
+    )(early, late, z, gain)
     return out
 
 
 def solution(mesh):
     ctx, head = mesh.devices.shape
     inner = max(1, GROUPS * 16 // (OWN * head))
-    cut = Mesh(mesh.devices.reshape(ctx // inner, inner, head), ("outer", "inner", "head"))
-    rows = P(("outer", "inner", "head"), None)
+    cut = Mesh(mesh.devices.reshape(ctx // inner, inner, head), AXES)
+    rows = P(AXES, None)
     return jax.shard_map(
         shards,
         mesh=cut,

time: 45.2 us -> 44 us (0.973)
  the two profiles are of different devices: /device:TPU:0 before, /device:TPU:16 now
where the time goes in v7:
time: 44 us; the launch traced here: 43.8 us
  blocking collectives  31.5 us (72%)
  Pallas kernels  6.11 us (14%)
  waiting for transfers between devices  4.74 us (11%)
  starting transfers between devices  1.29 us (3%)
    all_to_all x2, blocking collectives, exchanged(): return lax.all_to_all(array, ('inner', 'head'), 0, 0, tiled=True)  31.5 us
    ppermute x1, waiting for transfers between devices, shift(): return lax.ppermute(array, AXES, route)  4.74 us
    pallas_call x1, Pallas kernels, local_of(): kernel(local_body, 'local', [IN_VMEM] * 3 + [hbm], [of(BF16, tokens, STAT...  2.58 us
    pallas_call x1, Pallas kernels, shards(): kernel(pack_body, 'pack', [hbm] * len(operands), [of(BF16, dests, total,...  1.46 us
    ppermute x1, starting transfers between devices, shift(): return lax.ppermute(array, AXES, route)  1.29 us
    pallas_call x1, Pallas kernels, shards(): kernel(norm_body, 'norm', [IN_VMEM] * 4, [of(BF16, rows, dests * WIDE)],...  1.25 us
  transfers between devices with their start and end apart: 1, of which 1 were waited for; matrix products, arithmetic and copies ran while one was open for 0% of the time, Pallas kernels for 6%

profile of v7, /device:TPU:16, one launch (start us, length us, event | category | flops | bytes accessed | tf_op | source)
XLA Modules:
  0.0 43.8 jit_solution(17179585178072449376)
XLA Ops:
  0.0 1.5 %pack.1 = (bf16[16,200,128]{2,1,0:T(8,128)(2,1)S(1)}, f32[20,768]{1,0:T(8,128)S(1)}, f32[1,8192]{1,0:T(1,128)S(1)}) custom-call(bf16[32,8192]{1,0:T(8,128)(2,1)} %x_hbm.1, bf16[32,1024]{1,0:T(8,128)(2,1)} %b_hbm.1, bf16[32,1024]{1,0:T(8,128)(2,1)} %c_hbm.1, bf16[32,128]{1,0:T(8,128)(2,1)} %dt_hbm.1, f32[4,8192]{1,0:T(4,128)} %tap_x.1, f32[4,1024]{1,0:T(4,128)} %tap_b.1, ...), custom_call_target="tpu_custom_call" | custom-call | tf_op jit(solution)/shard_map/pack/pallas_call | solution.py:414
  1.5 0.1 conditional.3
  1.5 0.1 unset.4
  1.6 1.3 %collective-permute-start = (bf16[136,512]{1,0:T(8,128)(2,1)S(1)}, bf16[136,512]{1,0:T(8,128)(2,1)S(1)}, u32[]{:S(2)}, u32[]{:S(2)}) collective-permute-start(bf16[136,512]{1,0:T(8,128)(2,1)S(1)} %get-tuple-element.96), channel_id=1, source_target_pairs={{0,24},{1,25},{2,26},{3,27},{4,28},{5,29},{6,30},{7,31},{8,16},{9,... | collective-permute-start | bytes 417800 | tf_op jit(solution)/shard_map/ppermute | solution.py:382
  2.9 21.0 %conditional.4 = (bf16[16,32,512]{2,1,0:T(8,128)(2,1)S(1)}, bf16[512,128]{1,0:T(8,128)(2,1)S(1)}, f32[512,512]{1,0:T(8,128)S(1)}, f32[4,8,128]{2,1,0:T(8,128)S(1...) conditional(s32[]{:T(128)} %convert_element_type.2, ...), branch_computations={%region_2.0_spmd, %region_3.0_spmd} | conditional | flops 167772160 | bytes 4808772 | solution.py:489
  2.9 18.3 %all_to_all.17.got_ref = bf16[16,200,128]{2,1,0:T(8,128)(2,1)S(1)} all-to-all(bf16[16,200,128]{2,1,0:T(8,128)(2,1)S(1)} %get-tuple-element.42), channel_id=1, replica_groups=mesh['outer'=2,'inner'=4,'head'=4] {'inner','head'}, dimensions={0} | all-to-all | bytes 1638400 | tf_op jit(solution)/shard_map/cond/branch_0_fun/all_to_all | solution.py:426
  21.3 2.6 %local.2 = (bf16[512,128]{1,0:T(8,128)(2,1)S(1)}, f32[512,512]{1,0:T(8,128)S(1)}, f32[4,8,128]{2,1,0:T(8,128)S(1)}, f32[2,128,64]{2,1,0:T(8,128)S(1)}, f32[8,512...) custom-call(bf16[16,200,128]{2,1,0:T(8,128)(2,1)S(1)} %all_to_all.17.got_ref, ...), custom_call_target="tpu_custom_call" | custom-call | flops 167772160 | bytes 3145728 | tf_op jit(solution)/shard_map/cond/branch_0_fun/local/pallas_call | solution.py:441
  23.9 4.7 %collective-permute-done = bf16[136,512]{1,0:T(8,128)(2,1)S(1)} collective-permute-done((bf16[136,512]{1,0:T(8,128)(2,1)S(1)}, bf16[136,512]{1,0:T(8,128)(2,1)S(1)}, u32[]{:S(2)}, u32[]{:S(2)}) %collective-permute-start) | collective-permute-done | bytes 139296 | tf_op jit(solution)/shard_map/ppermute | solution.py:382
  28.6 13.9 %conditional.5 = (bf16[16,32,512]{2,1,0:T(8,128)(2,1)S(1)}) conditional(s32[]{:T(128)} %convert_element_type.2, (bf16[136,512]{1,0:T(8,128)(2,1)S(1)}, f32[20,768]{1,0:T(8,128)S(1)}, bf16[512,128]{1,0:T(8,128)(2,1)S(1)}, f32[512,512]{1,0:T(8,128)S(1)}, f32[4,8,128]{2,1,0:T(8,128)S(1)}, /*index=5*/f32[2,128,64]{2,1,0:T(8,128)S(1)}, ...), branch_computations={%region_4.0_spmd, %region_5.0_spmd} | conditional | bytes 1048584 | solution.py:490
  28.6 0.7 %carry.3 = bf16[512,512]{1,0:T(8,128)(2,1)S(1)} custom-call(bf16[136,512]{1,0:T(8,128)(2,1)S(1)} %get-tuple-element.71.before_ref, f32[20,768]{1,0:T(8,128)S(1)} %get-tuple-element.72.own_ref, bf16[512,128]{1,0:T(8,128)(2,1)S(1)} %get-tuple-element.73.c_ref, f32[512,512]{1,0:T(8,128)S(1)} %get-tuple-element.74.part_ref, ...), custom_call_target="tpu_custom_call" | custom-call | tf_op jit(solution)/shard_map/cond/branch_0_fun/carry/pallas_call | solution.py:463
  29.3 13.2 %all_to_all.19 = bf16[16,32,512]{2,1,0:T(8,128)(2,1)S(1)} all-to-all(bf16[16,32,512]{2,1,0:T(8,128)(2,1)S(1)} %bitcast.6), channel_id=1, replica_groups=mesh['outer'=2,'inner'=4,'head'=4] {'inner','head'}, dimensions={0} | all-to-all | bytes 1048576 | tf_op jit(solution)/shard_map/cond/branch_0_fun/all_to_all | solution.py:426
  42.5 1.2 %norm.1 = bf16[32,8192]{1,0:T(8,128)(2,1)} custom-call(bf16[16,32,512]{2,1,0:T(8,128)(2,1)S(1)} %get-tuple-element.95.early_ref, bf16[16,32,512]{2,1,0:T(8,128)(2,1)S(1)} %get-tuple-element.126.late_ref, bf16[32,8192]{1,0:T(8,128)(2,1)S(1)} %get-tuple-element.103.z_ref, f32[1,8192]{1,0:T(1,128)S(1)} %get-tuple-element.104.gain_ref), custom_call_target="tpu_custom_call" | custom-call | tf_op jit(solution)/shard_map/norm/pallas_call | solution.py:511
  (2 shorter events, 0.0 us)
Async XLA Ops:
  1.6 27.0 %collective-permute-start = (bf16[136,512]{1,0:T(8,128)(2,1)S(1)}, bf16[136,512]{1,0:T(8,128)(2,1)S(1)}, u32[]{:S(2)}, u32[]{:S(2)}) collective-permute-start(bf16[136,512]{1,0:T(8,128)(2,1)S(1)} %get-tuple-element.96), channel_id=1, source_target_pairs={{0,24},{1,25},{2,26},{3,27},{4,28},{5,29},{6,30},{7,31},{8,16},{9,... | collective-permute-start | bytes 417800 | tf_op jit(solution)/shard_map/ppermute | solution.py:382

commit v8 on v7

--- a/solution.py
+++ b/solution.py
@@ -227,7 +227,7 @@
 
 def local_body(
     got_ref, halo_ref, own_ref, z_hbm,
-    c_ref, part_ref, growth_ref, factor_ref, tail_ref, top_ref, z_ref, order_ref, win, turn, sem,
+    c_ref, part_ref, growth_ref, factor_ref, tail_ref, top_ref, gate_ref, order_ref, win, turn, z_ref, sem,
 ):
     fetch = pltpu.make_async_copy(z_hbm, z_ref, sem)
     fetch.start()
@@ -263,7 +263,7 @@
         grown = expand(jnp.exp(cum))
         if j > 1:
             past = past + cums[j - 1][:, BLOCK - 1 :]
-        growth_ref[j] = jnp.exp(cum + past)
+        growth_ref[at : at + BLOCK] = expand(jnp.exp(cum + past)) if j > 1 else grown
         if j > 0:
             carried = dot(jnp.concatenate([c, c], 1), stacked(local, 2)) * grown
         for q in range(TILES):
@@ -297,6 +297,8 @@
     factor_ref[1] = jnp.broadcast_to(dt_s, (BLOCK, wide))
     order_ref[...] = jnp.zeros_like(order_ref)
     fetch.wait()
+    for lo in range(0, z_ref.shape[1], WIDE):
+        gate_ref[:, lo : lo + WIDE] = silu(z_ref[:, lo : lo + WIDE].astype(F32))
 
 
 def carry_body(before_ref, own_ref, c_ref, part_ref, growth_ref, factor_ref, tail_ref, top_ref, y_ref, win, c_first):
@@ -318,7 +320,7 @@
     b_twice = jnp.concatenate([b_top, b_top], 0).astype(BF16)
     head = dot_t(b_twice, stacked(x_top * tail_ref[...], 2))
     state = before_ref[:STATE]
-    grown = expand(growth_ref[0])
+    grown = growth_ref[:BLOCK]
     later = stacked(grown[BLOCK - 1 :] * state.astype(F32) + head, 2)
 
     c_first[...] = c_ref[:BLOCK].astype(F32)
@@ -337,14 +339,14 @@
         at = j * BLOCK
         c = c_ref[at : at + BLOCK]
         carried = dot(jnp.concatenate([c, c], 1), later)
-        y_ref[at : at + BLOCK] = (part_ref[at : at + BLOCK] + carried * expand(growth_ref[j])).astype(BF16)
+        y_ref[at : at + BLOCK] = (part_ref[at : at + BLOCK] + carried * growth_ref[at : at + BLOCK]).astype(BF16)
 
 
 def unset_body(*refs):
     refs[-1][...] = jnp.zeros_like(refs[-1])
 
 
-def norm_body(early_ref, late_ref, z_ref, gain_ref, out_hbm, out_v, sem):
+def norm_body(early_ref, late_ref, gate_ref, gain_ref, out_hbm, out_v, sem):
     count = late_ref.shape[0]
     per = count // GROUPS
     leads = (lax.axis_index("outer") == 0) & (lax.axis_size("outer") == 2)
@@ -356,7 +358,7 @@
         for k in range(g * per, (g + 1) * per):
             at = holder(k, half_turn, count)
             y = jnp.where(leads, early_ref[at].astype(F32), late_ref[at].astype(F32))
-            v = y * silu(z_ref[:, k * WIDE : (k + 1) * WIDE].astype(F32))
+            v = y * gate_ref[:, k * WIDE : (k + 1) * WIDE]
             gated.append(v)
             square = square + jnp.sum(v * v, axis=1, keepdims=True)
         scale = lax.rsqrt(square / (per * WIDE) + eps_norm)
@@ -441,13 +443,13 @@
         return kernel(
             local_body, "local", [IN_VMEM] * 3 + [hbm],
             [
-                of(BF16, tokens, STATE), of(F32, tokens, WIDE), of(F32, blocks, OWN, BLOCK), of(F32, 2, BLOCK, wide),
-                of(F32, TOP, WIDE), of(F32, TILES + 2, TOP, LANES), of(BF16, *z_in.shape),
+                of(BF16, tokens, STATE), of(F32, tokens, WIDE), pltpu.VMEM((tokens, WIDE), F32), of(F32, 2, BLOCK, wide),
+                of(F32, TOP, WIDE), of(F32, TILES + 2, TOP, LANES), pltpu.VMEM(z_in.shape, F32),
                 of(F32, 8, LANES),
             ],
             [
                 pltpu.VMEM((TILES + 2, TOP + tokens, LANES), F32), pltpu.VMEM((BLOCK, LANES), F32),
-                pltpu.SemaphoreType.DMA,
+                pltpu.VMEM(z_in.shape, BF16), pltpu.SemaphoreType.DMA,
             ],
             pl.CostEstimate(
                 flops=2 * blocks * OWN * BLOCK * BLOCK * 160,
@@ -478,15 +480,15 @@
         before = shift(send, 1)
 
         def first(array, kept):
-            *done, z, order = local_of(kept, halo)
+            *done, gate, order = local_of(kept, halo)
             *rest, nothing = unset([*done, send], order)
-            return leaving(nothing, *done), tuple(rest), z
+            return leaving(nothing, *done), tuple(rest), gate
 
         def second(array, kept):
-            *done, z, order = local_of(exchanged(array), halo)
-            return unset([of(BF16, dests, rows, WIDE)], order)[0], tuple(done), z
-
-        early, done, z = lax.cond(leads, first, second, sent, kept)
+            *done, gate, order = local_of(exchanged(array), halo)
+            return unset([of(BF16, dests, rows, WIDE)], order)[0], tuple(done), gate
+
+        early, done, gate = lax.cond(leads, first, second, sent, kept)
         late = lax.cond(
             leads,
             lambda before, done: unset([of(BF16, dests, rows, WIDE)])[0],
@@ -505,13 +507,13 @@
             held = held * shift(held, reach)
             reach *= 2
         before = jnp.concatenate([entering.astype(BF16), before[STATE:]], 0)
-        *done, z, _ = local_of(got, halo)
+        *done, gate, _ = local_of(got, halo)
         early = late = leaving(before, *done)
 
     [out] = kernel(
         norm_body, "norm", [IN_VMEM] * 4, [of(BF16, rows, dests * WIDE)],
         [pltpu.VMEM((rows, dests * WIDE), BF16), pltpu.SemaphoreType.DMA((GROUPS,))], out_specs=[hbm],
-    )(early, late, z, gain)
+    )(early, late, gate, gain)
     return out
 
 

time: 44 us -> 43.8 us (level)
  no operation moved by 1% of the time
where the time goes in v8:
time: 43.8 us; the launch traced here: 43.5 us
  blocking collectives  31.5 us (72%)
  Pallas kernels  6.03 us (14%)
  waiting for transfers between devices  4.55 us (10%)
  starting transfers between devices  1.29 us (3%)
    all_to_all x2, blocking collectives, exchanged(): return lax.all_to_all(array, ('inner', 'head'), 0, 0, tiled=True)  31.5 us
    ppermute x1, waiting for transfers between devices, shift(): return lax.ppermute(array, AXES, route)  4.55 us
    pallas_call x1, Pallas kernels, local_of(): kernel(local_body, 'local', [IN_VMEM] * 3 + [hbm], [of(BF16, tokens, STAT...  2.77 us
    pallas_call x1, Pallas kernels, shards(): kernel(pack_body, 'pack', [hbm] * len(operands), [of(BF16, dests, total,...  1.46 us
    ppermute x1, starting transfers between devices, shift(): return lax.ppermute(array, AXES, route)  1.29 us
    pallas_call x1, Pallas kernels, shards(): kernel(norm_body, 'norm', [IN_VMEM] * 4, [of(BF16, rows, dests * WIDE)],...  1.08 us
  transfers between devices with their start and end apart: 1, of which 1 were waited for; matrix products, arithmetic and copies ran while one was open for 0% of the time, Pallas kernels for 6%

profile of v8, /device:TPU:16, one launch (start us, length us, event | category | flops | bytes accessed | tf_op | source)
XLA Modules:
  0.0 43.5 jit_solution(1668614241028723826)
XLA Ops:
  0.0 1.5 %pack.1 = (bf16[16,200,128]{2,1,0:T(8,128)(2,1)S(1)}, f32[20,768]{1,0:T(8,128)S(1)}, f32[1,8192]{1,0:T(1,128)S(1)}) custom-call(bf16[32,8192]{1,0:T(8,128)(2,1)} %x_hbm.1, bf16[32,1024]{1,0:T(8,128)(2,1)} %b_hbm.1, bf16[32,1024]{1,0:T(8,128)(2,1)} %c_hbm.1, bf16[32,128]{1,0:T(8,128)(2,1)} %dt_hbm.1, f32[4,8192]{1,0:T(4,128)} %tap_x.1, f32[4,1024]{1,0:T(4,128)} %tap_b.1, ...), custom_call_target="tpu_custom_call" | custom-call | tf_op jit(solution)/shard_map/pack/pallas_call | solution.py:416
  1.5 0.1 conditional.3
  1.5 0.1 unset.4
  1.6 1.3 %collective-permute-start = (bf16[136,512]{1,0:T(8,128)(2,1)S(1)}, bf16[136,512]{1,0:T(8,128)(2,1)S(1)}, u32[]{:S(2)}, u32[]{:S(2)}) collective-permute-start(bf16[136,512]{1,0:T(8,128)(2,1)S(1)} %get-tuple-element.96), channel_id=1, source_target_pairs={{0,24},{1,25},{2,26},{3,27},{4,28},{5,29},{6,30},{7,31},{8,16},{9,... | collective-permute-start | bytes 417800 | tf_op jit(solution)/shard_map/ppermute | solution.py:384
  2.9 21.2 %conditional.4 = (bf16[16,32,512]{2,1,0:T(8,128)(2,1)S(1)}, bf16[512,128]{1,0:T(8,128)(2,1)S(1)}, f32[512,512]{1,0:T(8,128)S(1)}, f32[512,512]{1,0:T(8,128)S(1)}...) conditional(s32[]{:T(128)} %convert_element_type.2, ...), branch_computations={%region_2.0_spmd, %region_3.0_spmd} | conditional | flops 167772160 | bytes 4808772 | solution.py:491
  2.9 18.3 %all_to_all.17.got_ref = bf16[16,200,128]{2,1,0:T(8,128)(2,1)S(1)} all-to-all(bf16[16,200,128]{2,1,0:T(8,128)(2,1)S(1)} %get-tuple-element.42), channel_id=1, replica_groups=mesh['outer'=2,'inner'=4,'head'=4] {'inner','head'}, dimensions={0} | all-to-all | bytes 1638400 | tf_op jit(solution)/shard_map/cond/branch_0_fun/all_to_all | solution.py:428
  21.3 2.8 %local.2 = (bf16[512,128]{1,0:T(8,128)(2,1)S(1)}, f32[512,512]{1,0:T(8,128)S(1)}, f32[512,512]{1,0:T(8,128)S(1)}, f32[2,128,64]{2,1,0:T(8,128)S(1)}, f32[8,512]{...) custom-call(bf16[16,200,128]{2,1,0:T(8,128)(2,1)S(1)} %all_to_all.17.got_ref, ...), custom_call_target="tpu_custom_call" | custom-call | flops 167772160 | bytes 3145728 | tf_op jit(solution)/shard_map/cond/branch_0_fun/local/pallas_call | solution.py:443
  24.1 4.6 %collective-permute-done = bf16[136,512]{1,0:T(8,128)(2,1)S(1)} collective-permute-done((bf16[136,512]{1,0:T(8,128)(2,1)S(1)}, bf16[136,512]{1,0:T(8,128)(2,1)S(1)}, u32[]{:S(2)}, u32[]{:S(2)}) %collective-permute-start) | collective-permute-done | bytes 139296 | tf_op jit(solution)/shard_map/ppermute | solution.py:384
  28.6 13.8 %conditional.5 = (bf16[16,32,512]{2,1,0:T(8,128)(2,1)S(1)}) conditional(s32[]{:T(128)} %convert_element_type.2, (bf16[136,512]{1,0:T(8,128)(2,1)S(1)}, f32[20,768]{1,0:T(8,128)S(1)}, bf16[512,128]{1,0:T(8,128)(2,1)S(1)}, f32[512,512]{1,0:T(8,128)S(1)}, f32[512,512]{1,0:T(8,128)S(1)}, /*index=5*/f32[2,128,64]{2,1,0:T(8,128)S(1)}, ...), branch_computations={%region_4.0_spmd, %region_5.0_spmd} | conditional | bytes 1048584 | solution.py:492
  28.7 0.6 %carry.3 = bf16[512,512]{1,0:T(8,128)(2,1)S(1)} custom-call(bf16[136,512]{1,0:T(8,128)(2,1)S(1)} %get-tuple-element.71.before_ref, f32[20,768]{1,0:T(8,128)S(1)} %get-tuple-element.72.own_ref, bf16[512,128]{1,0:T(8,128)(2,1)S(1)} %get-tuple-element.73.c_ref, f32[512,512]{1,0:T(8,128)S(1)} %get-tuple-element.74.part_ref, ...), custom_call_target="tpu_custom_call" | custom-call | tf_op jit(solution)/shard_map/cond/branch_0_fun/carry/pallas_call | solution.py:465
  29.2 13.2 %all_to_all.19 = bf16[16,32,512]{2,1,0:T(8,128)(2,1)S(1)} all-to-all(bf16[16,32,512]{2,1,0:T(8,128)(2,1)S(1)} %bitcast.6), channel_id=1, replica_groups=mesh['outer'=2,'inner'=4,'head'=4] {'inner','head'}, dimensions={0} | all-to-all | bytes 1048576 | tf_op jit(solution)/shard_map/cond/branch_0_fun/all_to_all | solution.py:428
  42.4 1.1 %norm.1 = bf16[32,8192]{1,0:T(8,128)(2,1)} custom-call(bf16[16,32,512]{2,1,0:T(8,128)(2,1)S(1)} %get-tuple-element.95.early_ref, bf16[16,32,512]{2,1,0:T(8,128)(2,1)S(1)} %get-tuple-element.126.late_ref, f32[32,8192]{1,0:T(8,128)S(1)} %get-tuple-element.103.gate_ref, f32[1,8192]{1,0:T(1,128)S(1)} %get-tuple-element.104.gain_ref), custom_call_target="tpu_custom_call" | custom-call | tf_op jit(solution)/shard_map/norm/pallas_call | solution.py:513
  (2 shorter events, 0.0 us)
Async XLA Ops:
  1.6 27.0 %collective-permute-start = (bf16[136,512]{1,0:T(8,128)(2,1)S(1)}, bf16[136,512]{1,0:T(8,128)(2,1)S(1)}, u32[]{:S(2)}, u32[]{:S(2)}) collective-permute-start(bf16[136,512]{1,0:T(8,128)(2,1)S(1)} %get-tuple-element.96), channel_id=1, source_target_pairs={{0,24},{1,25},{2,26},{3,27},{4,28},{5,29},{6,30},{7,31},{8,16},{9,... | collective-permute-start | bytes 417800 | tf_op jit(solution)/shard_map/ppermute | solution.py:384

commit v9 on v8

--- a/solution.py
+++ b/solution.py
@@ -204,14 +204,16 @@
     dts, cums = steps_of(got_ref, own_ref)
     taps = tiles_of(own_ref)
     fill(win, got_ref, halo_ref, TILES + 1)
-    state = jnp.zeros((STATE, WIDE), F32)
+    lefts, rights = [], []
     after = jnp.zeros((OWN, 1), F32)
     for j in reversed(range(blocks)):
         after = after + cums[j][:, BLOCK - 1 :]
         tail = expand(jnp.exp(after - cums[j]) * dts[j])
         x = jnp.concatenate([conv_tile(win, taps, j, q) for q in range(TILES)], 1)
         b = conv_tile(win, taps, j, TILES)
-        state = state + dot_t(jnp.concatenate([b, b], 0), stacked(x.astype(F32) * tail, 2))
+        lefts += [b, b]
+        rights.append(stacked(x.astype(F32) * tail, 2))
+    state = dot_t(jnp.concatenate(lefts, 0), jnp.concatenate(rights, 0))
     send_ref[:STATE] = state.astype(BF16)
     ends = [got_ref[sources - 1, q * rows : (q + 1) * rows, :].astype(F32)[rows - TOP :] for q in range(TILES + 2)]
     ends += [jnp.zeros_like(ends[0])] * (TILES - 2)

time: 43.8 us -> 43.7 us (level)
  no operation moved by 1% of the time
where the time goes in v9:
time: 43.7 us; the launch traced here: 43.4 us
  blocking collectives  31.5 us (72%)
  Pallas kernels  6.03 us (14%)
  waiting for transfers between devices  4.48 us (10%)
  starting transfers between devices  1.29 us (3%)
    all_to_all x2, blocking collectives, exchanged(): return lax.all_to_all(array, ('inner', 'head'), 0, 0, tiled=True)  31.5 us
    ppermute x1, waiting for transfers between devices, shift(): return lax.ppermute(array, AXES, route)  4.48 us
    pallas_call x1, Pallas kernels, local_of(): kernel(local_body, 'local', [IN_VMEM] * 3 + [hbm], [of(BF16, tokens, STAT...  2.77 us
    pallas_call x1, Pallas kernels, shards(): kernel(pack_body, 'pack', [hbm] * len(operands), [of(BF16, dests, total,...  1.46 us
    ppermute x1, starting transfers between devices, shift(): return lax.ppermute(array, AXES, route)  1.29 us
    pallas_call x1, Pallas kernels, shards(): kernel(norm_body, 'norm', [IN_VMEM] * 4, [of(BF16, rows, dests * WIDE)],...  1.08 us
  transfers between devices with their start and end apart: 1, of which 1 were waited for; matrix products, arithmetic and copies ran while one was open for 0% of the time, Pallas kernels for 6%

profile of v9, /device:TPU:16, one launch (start us, length us, event | category | flops | bytes accessed | tf_op | source)
XLA Modules:
  0.0 43.4 jit_solution(9191437115363288034)
XLA Ops:
  0.0 1.5 %pack.1 = (bf16[16,200,128]{2,1,0:T(8,128)(2,1)S(1)}, f32[20,768]{1,0:T(8,128)S(1)}, f32[1,8192]{1,0:T(1,128)S(1)}) custom-call(bf16[32,8192]{1,0:T(8,128)(2,1)} %x_hbm.1, bf16[32,1024]{1,0:T(8,128)(2,1)} %b_hbm.1, bf16[32,1024]{1,0:T(8,128)(2,1)} %c_hbm.1, bf16[32,128]{1,0:T(8,128)(2,1)} %dt_hbm.1, f32[4,8192]{1,0:T(4,128)} %tap_x.1, f32[4,1024]{1,0:T(4,128)} %tap_b.1, ...), custom_call_target="tpu_custom_call" | custom-call | tf_op jit(solution)/shard_map/pack/pallas_call | solution.py:418
  1.5 0.1 conditional.3
  1.5 0.1 unset.4
  1.6 1.3 %collective-permute-start = (bf16[136,512]{1,0:T(8,128)(2,1)S(1)}, bf16[136,512]{1,0:T(8,128)(2,1)S(1)}, u32[]{:S(2)}, u32[]{:S(2)}) collective-permute-start(bf16[136,512]{1,0:T(8,128)(2,1)S(1)} %get-tuple-element.96), channel_id=1, source_target_pairs={{0,24},{1,25},{2,26},{3,27},{4,28},{5,29},{6,30},{7,31},{8,16},{9,... | collective-permute-start | bytes 417800 | tf_op jit(solution)/shard_map/ppermute | solution.py:386
  2.9 21.2 %conditional.4 = (bf16[16,32,512]{2,1,0:T(8,128)(2,1)S(1)}, bf16[512,128]{1,0:T(8,128)(2,1)S(1)}, f32[512,512]{1,0:T(8,128)S(1)}, f32[512,512]{1,0:T(8,128)S(1)}...) conditional(s32[]{:T(128)} %convert_element_type.2, ...), branch_computations={%region_2.0_spmd, %region_3.0_spmd} | conditional | flops 167772160 | bytes 4808772 | solution.py:493
  2.9 18.3 %all_to_all.17.got_ref = bf16[16,200,128]{2,1,0:T(8,128)(2,1)S(1)} all-to-all(bf16[16,200,128]{2,1,0:T(8,128)(2,1)S(1)} %get-tuple-element.42), channel_id=1, replica_groups=mesh['outer'=2,'inner'=4,'head'=4] {'inner','head'}, dimensions={0} | all-to-all | bytes 1638400 | tf_op jit(solution)/shard_map/cond/branch_0_fun/all_to_all | solution.py:430
  21.3 2.8 %local.2 = (bf16[512,128]{1,0:T(8,128)(2,1)S(1)}, f32[512,512]{1,0:T(8,128)S(1)}, f32[512,512]{1,0:T(8,128)S(1)}, f32[2,128,64]{2,1,0:T(8,128)S(1)}, f32[8,512]{...) custom-call(bf16[16,200,128]{2,1,0:T(8,128)(2,1)S(1)} %all_to_all.17.got_ref, ...), custom_call_target="tpu_custom_call" | custom-call | flops 167772160 | bytes 3145728 | tf_op jit(solution)/shard_map/cond/branch_0_fun/local/pallas_call | solution.py:445
  24.1 4.5 %collective-permute-done = bf16[136,512]{1,0:T(8,128)(2,1)S(1)} collective-permute-done((bf16[136,512]{1,0:T(8,128)(2,1)S(1)}, bf16[136,512]{1,0:T(8,128)(2,1)S(1)}, u32[]{:S(2)}, u32[]{:S(2)}) %collective-permute-start) | collective-permute-done | bytes 139296 | tf_op jit(solution)/shard_map/ppermute | solution.py:386
  28.6 13.8 %conditional.5 = (bf16[16,32,512]{2,1,0:T(8,128)(2,1)S(1)}) conditional(s32[]{:T(128)} %convert_element_type.2, (bf16[136,512]{1,0:T(8,128)(2,1)S(1)}, f32[20,768]{1,0:T(8,128)S(1)}, bf16[512,128]{1,0:T(8,128)(2,1)S(1)}, f32[512,512]{1,0:T(8,128)S(1)}, f32[512,512]{1,0:T(8,128)S(1)}, /*index=5*/f32[2,128,64]{2,1,0:T(8,128)S(1)}, ...), branch_computations={%region_4.0_spmd, %region_5.0_spmd} | conditional | bytes 1048584 | solution.py:494
  28.6 0.6 %carry.3 = bf16[512,512]{1,0:T(8,128)(2,1)S(1)} custom-call(bf16[136,512]{1,0:T(8,128)(2,1)S(1)} %get-tuple-element.71.before_ref, f32[20,768]{1,0:T(8,128)S(1)} %get-tuple-element.72.own_ref, bf16[512,128]{1,0:T(8,128)(2,1)S(1)} %get-tuple-element.73.c_ref, f32[512,512]{1,0:T(8,128)S(1)} %get-tuple-element.74.part_ref, ...), custom_call_target="tpu_custom_call" | custom-call | tf_op jit(solution)/shard_map/cond/branch_0_fun/carry/pallas_call | solution.py:467
  29.2 13.2 %all_to_all.19 = bf16[16,32,512]{2,1,0:T(8,128)(2,1)S(1)} all-to-all(bf16[16,32,512]{2,1,0:T(8,128)(2,1)S(1)} %bitcast.6), channel_id=1, replica_groups=mesh['outer'=2,'inner'=4,'head'=4] {'inner','head'}, dimensions={0} | all-to-all | bytes 1048576 | tf_op jit(solution)/shard_map/cond/branch_0_fun/all_to_all | solution.py:430
  42.3 1.1 %norm.1 = bf16[32,8192]{1,0:T(8,128)(2,1)} custom-call(bf16[16,32,512]{2,1,0:T(8,128)(2,1)S(1)} %get-tuple-element.95.early_ref, bf16[16,32,512]{2,1,0:T(8,128)(2,1)S(1)} %get-tuple-element.126.late_ref, f32[32,8192]{1,0:T(8,128)S(1)} %get-tuple-element.103.gate_ref, f32[1,8192]{1,0:T(1,128)S(1)} %get-tuple-element.104.gain_ref), custom_call_target="tpu_custom_call" | custom-call | tf_op jit(solution)/shard_map/norm/pallas_call | solution.py:515
  (2 shorter events, 0.0 us)
Async XLA Ops:
  1.6 27.0 %collective-permute-start = (bf16[136,512]{1,0:T(8,128)(2,1)S(1)}, bf16[136,512]{1,0:T(8,128)(2,1)S(1)}, u32[]{:S(2)}, u32[]{:S(2)}) collective-permute-start(bf16[136,512]{1,0:T(8,128)(2,1)S(1)} %get-tuple-element.96), channel_id=1, source_target_pairs={{0,24},{1,25},{2,26},{3,27},{4,28},{5,29},{6,30},{7,31},{8,16},{9,... | collective-permute-start | bytes 417800 | tf_op jit(solution)/shard_map/ppermute | solution.py:386
